TPU v7x, 32 devices: a whole 2x2x4 slice. The times are simulated.
32 devices in a mesh: groups: 2 (over x), pair: 16 (over z, y, core).
Axes of the slice: x: 2, y: 2, z: 4, core: 2. Of those that a mesh axis runs over, the one named last changes fastest.
Arguments:
- chol: bfloat16 [2048, 262144], P('groups', 'pair'), parts along dimension 0, may hold values from -0.3125 to 0.3125
- walkers: bfloat16 [64, 512, 128], P(('groups', 'pair')), parts along dimension 0, may hold values from -6 to 6
- trial: bfloat16 [1024, 128], P('groups'), parts along dimension 0, may hold values from -0.5 to 0.5
- one_body: bfloat16 [1024, 512], P('groups'), parts along dimension 0, may hold values from -0.625 to 0.625
- fields: float32 [64, 1024], P(('groups', 'pair')), parts along dimension 0, may hold values from -6 to 6
- src_shift: int32 [64], P(('groups', 'pair')), parts along dimension 0, may hold values from -1 to 1
- src_slot: int32 [64], P(('groups', 'pair')), parts along dimension 0, may hold values from 0 to 1
Outputs:
- next_walkers: bfloat16 [64, 512, 128], P(('groups', 'pair')), parts along dimension 0
There are 2 independent parts, one for each index of `groups`. A program takes and returns all parts, laid end to end along the dimension named above; each array names one. Nothing has to cross between parts.
All inputs are finite; a program needn't handle non-finite values.
Results may differ from a plain program's by a relative error of at most 0.012.
Values may be sent and summed in bfloat16 or wider, within the bound.
No kernel may reach another device: no remote copies, remote signals or barrier semaphores. Data moves between devices by JAX's collectives and lax.ppermute only.
A program may use at most 64 MiB of HBM per device.

v0:
```python
import jax
import jax.numpy as jnp
from jax import lax
from jax.sharding import PartitionSpec as P

TERMS = 6


sqrt_tau = 0.1
bias_cap = 1.0


def padded_2(block, sides, width):
    for axis, dim in sides:
        count = lax.axis_size(axis)
        forward = [(i, i + 1) for i in range(count - 1)]
        forward.append((count - 1, 0))
        backward = [(target, source) for source, target in forward]
        low = lax.ppermute(
            lax.slice_in_dim(block, block.shape[dim] - width, None, axis=dim), axis, forward
        )
        high = lax.ppermute(lax.slice_in_dim(block, 0, width, axis=dim), axis, backward)
        block = jnp.concatenate([low, block, high], axis=dim)
    return block


def shards(chol, walkers, trial, one_body, fields, src_shift, src_slot):
    w_local = walkers.shape[0]
    orbitals = walkers.shape[1]
    moved = lax.all_to_all(walkers, "pair", split_axis=1, concat_axis=0, tiled=True)
    formed = jnp.einsum("wia,ka->wik", moved, trial, preferred_element_type=jnp.float32)
    green_rows = formed.astype(jnp.bfloat16).reshape(moved.shape[0], moved.shape[1] * orbitals)
    partial_bias = lax.dot_general(
        green_rows, chol, (((1,), (1,)), ((), ())), preferred_element_type=jnp.float32
    )
    summed = lax.psum(partial_bias, "pair")
    every_field = lax.all_gather(fields, "pair", axis=0, tiled=True)
    shift = (every_field - jnp.clip(sqrt_tau * summed, -bias_cap, bias_cap)).astype(jnp.bfloat16)
    local_potential = (sqrt_tau * jnp.dot(shift, chol, preferred_element_type=jnp.float32)).astype(
        jnp.bfloat16
    )
    own_potential = lax.all_to_all(local_potential, "pair", split_axis=0, concat_axis=1, tiled=True)
    amat = own_potential.astype(jnp.float32).reshape(w_local, orbitals, orbitals) + one_body.astype(
        jnp.float32
    )
    amat = amat.astype(jnp.bfloat16)
    term = walkers
    total = walkers.astype(jnp.float32)
    for order in range(1, TERMS):
        product = jnp.einsum("wik,wka->wia", amat, term, preferred_element_type=jnp.float32) / order
        total = total + product
        term = product.astype(jnp.bfloat16)
    propagated = total.astype(jnp.bfloat16)
    padded = padded_2(propagated, (("pair", 0),), w_local)
    position = (src_shift + 1) * w_local + src_slot
    return jnp.take(padded, position, axis=0)


def solution(mesh):
    placed = (
        P("groups", "pair"),
        P(("groups", "pair"), None, None),
        P("groups", None),
        P("groups", None),
        P(("groups", "pair"), None),
        P(("groups", "pair")),
        P(("groups", "pair")),
    )
    return jax.shard_map(
        shards,
        mesh=mesh,
        in_specs=placed,
        out_specs=P(("groups", "pair"), None, None),
        check_vma=False,
    )
```

profile of v0, /device:TPU:1, one launch (start us, length us, event | category | flops | bytes accessed | tf_op | source)
XLA Modules:
  0.0 202.4 jit_solution(3262210192182722894)
XLA Ops:
  6.5 0.0 copy-start
  6.5 0.0 all-reduce.2.cloned.1.call-start
  6.5 1.3 copy.10
  7.8 16.6 %all_to_all.31 = bf16[2,512,128]{2,0,1:T(2,128)(2,1)S(1)} all-to-all(bf16[2,512,128]{2,0,1:T(2,128)(2,1)S(1)} %copy.10), channel_id=1, replica_groups=mesh['groups'=2,'pair'=16] {'pair'}, dimensions={1} | all-to-all | bytes 524288 | tf_op jit(solution)/shard_map/all_to_all | solution.py:30
  24.5 0.0 copy-done
  24.5 0.4 convolution_convert_fusion
  24.9 0.6 copy.13
  25.5 0.0 copy-start.3
  25.6 15.8 %fusion.14 = f32[32,1024]{1,0:T(8,128)} fusion(bf16[32,16384]{1,0:T(8,128)(2,1)S(1)} %bitcast.22, bf16[1024,16384]{1,0:T(8,128)(2,1)} %param.7), kind=kOutput, calls=%fused_computation.29 | convolution fusion | flops 1073741824 | bytes 34734080 | tf_op jit(solution)/shard_map/dot_general | solution.py:33
  41.3 0.0 all-reduce.2.cloned.1.call-update
  41.3 0.0 copy-done.3
  41.3 19.4 %all-gather = f32[16,2,1024]{2,1,0:T(2,128)S(1)} all-gather(f32[1,2,1024]{2,1,0:T(2,128)S(1)} %bitcast.26), channel_id=1, replica_groups=mesh['groups'=2,'pair'=16] {'pair'}, dimensions={0}, use_global_device_ids=true | all-gather | bytes 139264 | tf_op jit(solution)/shard_map/all_gather | solution.py:37
  60.8 0.1 reshape.28
  60.9 67.3 %all-reduce.2.cloned.1.call-done = f32[32,1024]{1,0:T(8,128)} async-done(((f32[32,1024]{1,0:T(8,128)}), f32[32,1024]{1,0:T(8,128)}) %all-reduce.2.cloned.1.call-update) | async-done | bytes 131088 | tf_op jit(solution)/shard_map/psum | solution.py:36
  128.2 16.5 %fusion = bf16[32,16384]{1,0:T(8,128)(2,1)S(1)} fusion(bf16[1024,16384]{1,0:T(8,128)(2,1)} %param.7, f32[32,1024]{1,0:T(8,128)S(1)} %reshape.28, f32[32,1024]{1,0:T(8,128)} %all-reduce.2.cloned.1.call-done), kind=kOutput, calls=%fused_computation.2 | convolution fusion | flops 1074921472 | bytes 34865152 | tf_op jit(solution)/shard_map/dot_general | solution.py:39
  144.7 0.0 copy-start.2
  144.7 1.5 all_to_all.27
  146.1 6.6 %all-to-all-start.1 = ((bf16[16,2,16384]{2,1,0:T(2,128)(2,1)}), bf16[16,2,16384]{2,1,0:T(2,128)(2,1)S(1)}, u32[]{:S(2)}, u32[]{:S(2)}) async-start(bf16[16,2,16384]{2,1,0:T(2,128)(2,1)} %all_to_all.27), calls=%async_computation.1 | async-start | bytes 2097152 | tf_op jit(solution)/shard_map/all_to_all | solution.py:42
  152.7 0.0 copy-done.2
  152.7 0.1 convert_element_type.50
  152.9 23.0 %all-to-all-done.1 = bf16[16,2,16384]{2,1,0:T(2,128)(2,1)S(1)} async-done(((bf16[16,2,16384]{2,1,0:T(2,128)(2,1)}), bf16[16,2,16384]{2,1,0:T(2,128)(2,1)S(1)}, u32[]{:S(2)}, u32[]{:S(2)}) %all-to-all-start.1) | async-done | bytes 1048608 | tf_op jit(solution)/shard_map/all_to_all | solution.py:42
  175.9 0.9 convert_bitcast_fusion
  176.8 2.5 %copy.12 = f32[2,16,16384]{2,1,0:T(8,128)} copy(f32[2,16,16384]{2,0,1:T(2,128)S(1)} %convert_bitcast_fusion) | data formatting | bytes 4194304 | tf_op jit(solution)/shard_map/convert_element_type | solution.py:43
  179.3 1.7 reshape.17
  181.1 0.0 copy-start.1
  181.1 0.4 add_convert_fusion
  181.5 0.5 copy-done.1
  182.0 0.4 fusion.15
  182.5 0.4 convolution_multiply_fusion.4
  182.9 0.4 convolution_multiply_fusion.3
  183.4 0.4 convolution_multiply_fusion.2
  183.8 0.0 copy-start.4
  183.8 0.0 copy-start.5
  183.8 0.5 fusion.2
  184.3 1.2 collective-permute-start
  185.5 0.0 collective-permute-start.1
  185.5 0.0 copy-done.4
  185.5 0.0 copy-done.5
  185.5 3.3 %collective-permute-done = bf16[2,512,128]{2,1,0:T(8,128)(2,1)S(1)} collective-permute-done((bf16[2,512,128]{2,1,0:T(8,128)(2,1)S(1)}, bf16[2,512,128]{2,1,0:T(8,128)(2,1)S(1)}, u32[]{:S(2)}, u32[]{:S(2)}) %collective-permute-start) | collective-permute-done | bytes 262176 | tf_op jit(solution)/shard_map/ppermute | solution.py:19
  188.8 5.3 %collective-permute-done.1 = bf16[2,512,128]{2,1,0:T(8,128)(2,1)S(1)} collective-permute-done((bf16[2,512,128]{2,1,0:T(8,128)(2,1)S(1)}, bf16[2,512,128]{2,1,0:T(8,128)(2,1)S(1)}, u32[]{:S(2)}, u32[]{:S(2)}) %collective-permute-start.1) | collective-permute-done | bytes 262176 | tf_op jit(solution)/shard_map/ppermute | solution.py:22
  194.1 0.1 pad_maximum_fusion
  194.2 0.6 gather_fusion
  194.8 0.8 broadcast_select_fusion
  (3 shorter events, 0.1 us)
Async XLA Ops:
  6.5 18.0 %copy-start = (bf16[512,128]{1,0:T(8,128)(2,1)S(1)}, bf16[512,128]{1,0:T(8,128)(2,1)}, u32[]{:S(2)}) copy-start(bf16[512,128]{1,0:T(8,128)(2,1)} %param.9) | copy-start | bytes 393220
  6.5 121.6 %all-reduce.2.cloned.1.call-start = ((), (), s32[]{:S(2)}) async-start(), calls=%async_computation.2 | async-start | bytes 262144 | tf_op jit(solution)/shard_map/psum | solution.py:36
  25.5 15.8 %copy-start.3 = (f32[2,1024]{1,0:T(2,128)S(1)}, f32[2,1024]{1,0:T(2,128)}, u32[]{:S(2)}) copy-start(f32[2,1024]{1,0:T(2,128)} %param.11) | copy-start | bytes 24580
  144.7 8.1 %copy-start.2 = (bf16[512,512]{1,0:T(8,128)(2,1)S(1)}, bf16[512,512]{1,0:T(8,128)(2,1)}, u32[]{:S(2)}) copy-start(bf16[512,512]{1,0:T(8,128)(2,1)} %param.10) | copy-start | bytes 1572868
  146.1 29.8 %all-to-all-start.1 = ((bf16[16,2,16384]{2,1,0:T(2,128)(2,1)}), bf16[16,2,16384]{2,1,0:T(2,128)(2,1)S(1)}, u32[]{:S(2)}, u32[]{:S(2)}) async-start(bf16[16,2,16384]{2,1,0:T(2,128)(2,1)} %all_to_all.27), calls=%async_computation.1 | async-start | bytes 2097152 | tf_op jit(solution)/shard_map/all_to_all | solution.py:42
  181.1 1.0 copy-start.1
  183.8 1.7 copy-start.4
  183.8 1.6 copy-start.5
  184.3 4.5 %collective-permute-start = (bf16[2,512,128]{2,1,0:T(8,128)(2,1)S(1)}, bf16[2,512,128]{2,1,0:T(8,128)(2,1)S(1)}, u32[]{:S(2)}, u32[]{:S(2)}) collective-permute-start(bf16[2,512,128]{2,1,0:T(8,128)(2,1)S(1)} %fusion.2), channel_id=1, source_target_pairs={{0,1},{1,2},{2,3},{3,4},{4,5},{5,6},{6,7},{7,8},{8,9},{9,10},{10,1... | collective-permute-start | bytes 786440 | tf_op jit(solution)/shard_map/ppermute | solution.py:19
  185.5 8.6 %collective-permute-start.1 = (bf16[2,512,128]{2,1,0:T(8,128)(2,1)S(1)}, bf16[2,512,128]{2,1,0:T(8,128)(2,1)S(1)}, u32[]{:S(2)}, u32[]{:S(2)}) collective-permute-start(bf16[2,512,128]{2,1,0:T(8,128)(2,1)S(1)} %fusion.2), channel_id=1, source_target_pairs={{1,0},{2,1},{3,2},{4,3},{5,4},{6,5},{7,6},{8,7},{9,8},{10,9},{11,1... | collective-permute-start | bytes 786440 | tf_op jit(solution)/shard_map/ppermute | solution.py:22
Sparse Core Ops, SparseCore 0:
  41.4 86.6 all-reduce.1
where the time goes:
time: 203 us; the launch traced here: 202 us
  waiting for transfers between devices  98.9 us (49%)
  blocking collectives  36.1 us (18%)
  matrix products  34.9 us (17%)
  between operations  13.6 us (7%)
  local copies, waits for them, and re-layouts  8.9 us (4%)
  starting transfers between devices  7.75 us (4%)
  other arithmetic  2.3 us (1%)
    psum x1, waiting for transfers between devices, shards(): summed = lax.psum(partial_bias, 'pair')  67.3 us
    all_to_all x1, waiting for transfers between devices, shards(): lax.all_to_all(local_potential, 'pair', split_axis=0, concat_axis=1, tile...  23 us
    all_gather x1, blocking collectives, shards(): every_field = lax.all_gather(fields, 'pair', axis=0, tiled=True)  19.4 us
    all_to_all x1, blocking collectives, shards(): lax.all_to_all(walkers, 'pair', split_axis=1, concat_axis=0, tiled=True)  16.6 us
    dot_general x1, matrix products, shards(): jnp.dot(shift, chol, preferred_element_type=jnp.float32)  16.5 us
    dot_general x1, matrix products, shards(): lax.dot_general(green_rows, chol, (((1,), (1,)), ((), ())), preferred_ele...  15.8 us
    all_to_all x1, starting transfers between devices, shards(): lax.all_to_all(local_potential, 'pair', split_axis=0, concat_axis=1, tile...  6.57 us
    ppermute x1, waiting for transfers between devices, padded_2(): lax.ppermute(lax.slice_in_dim(block, 0, width, axis=dim), axis, backward)  5.29 us
  transfers between devices with their start and end apart: 4, of which 4 were waited for; matrix products, arithmetic and copies ran while one was open for 0% of the time, Pallas kernels for 0%

commit v1 on v0

v1 whole, which is shorter than its diff:
```python
import jax
import jax.numpy as jnp
from jax import lax
from jax.experimental import pallas as pl
from jax.experimental.pallas import tpu as pltpu
from jax.sharding import PartitionSpec as P

TERMS = 6
LANES = 128
MIB = 1 << 20

sqrt_tau = 0.1
bias_cap = 1.0

VMEM = pl.BlockSpec(memory_space=pltpu.VMEM)
SMEM = pl.BlockSpec(memory_space=pltpu.SMEM)
ANY = pl.BlockSpec(memory_space=pl.ANY)


def params(mib):
    return pltpu.CompilerParams(vmem_limit_bytes=mib * MIB)


def in_vmem(array):
    return pltpu.with_memory_space_constraint(array, pltpu.VMEM)


def exchange(blocks):
    return lax.all_to_all(blocks, "pair", split_axis=0, concat_axis=0, tiled=True)


def neighbours(block):
    count = lax.axis_size("pair")
    forward = [(i, (i + 1) % count) for i in range(count)]
    backward = [(target, source) for source, target in forward]
    return lax.ppermute(block, "pair", forward), lax.ppermute(block, "pair", backward)


def fold_trial(chol, trial):
    vectors, pairs = chol.shape
    orbitals, occupied = trial.shape
    rows = pairs // orbitals
    per = 4

    def body(chol_ref, trial_ref, folded_ref):
        for row in range(per):
            folded_ref[:, row * occupied : (row + 1) * occupied] = jnp.dot(
                chol_ref[:, row * orbitals : (row + 1) * orbitals],
                trial_ref[...],
                preferred_element_type=jnp.float32,
            ).astype(jnp.bfloat16)

    return pl.pallas_call(
        body,
        out_shape=pltpu.HBM((vectors, rows * occupied), jnp.bfloat16),
        grid=(rows // per,),
        in_specs=[
            pl.BlockSpec((vectors, per * orbitals), lambda i: (0, i)),
            pl.BlockSpec((orbitals, occupied), lambda i: (0, 0)),
        ],
        out_specs=pl.BlockSpec((vectors, per * occupied), lambda i: (0, i)),
        compiler_params=params(24),
        cost_estimate=pl.CostEstimate(
            flops=2 * vectors * pairs * occupied, bytes_accessed=2 * vectors * pairs, transcendentals=0
        ),
        name="fold_trial",
    )(chol, trial)


def bias_partial(moved, folded):
    walkers, depth = moved.shape
    vectors = folded.shape[0]
    strips = vectors // LANES
    steps = 4
    each = strips // steps

    def body(moved_ref, folded_ref, out_ref, acc_ref):
        step = pl.program_id(0)
        part = lax.dot_general(
            moved_ref[...], folded_ref[...], (((1,), (1,)), ((), ())), preferred_element_type=jnp.float32
        )
        for strip in range(each):
            acc_ref[pl.ds(step * each + strip, walkers, stride=strips), :] = part[
                :, strip * LANES : (strip + 1) * LANES
            ]

        @pl.when(step == steps - 1)
        def _():
            out_ref[...] = acc_ref[...].astype(jnp.bfloat16)

    return pl.pallas_call(
        body,
        out_shape=jax.ShapeDtypeStruct((walkers * strips, LANES), jnp.bfloat16),
        grid=(steps,),
        in_specs=[
            pl.BlockSpec((walkers, depth), lambda i: (0, 0)),
            pl.BlockSpec((vectors // steps, depth), lambda i: (i, 0)),
        ],
        out_specs=pl.BlockSpec((walkers * strips, LANES), lambda i: (0, 0)),
        scratch_shapes=[pltpu.VMEM((walkers * strips, LANES), jnp.float32)],
        compiler_params=params(10),
        name="bias_partial",
    )(moved, pltpu.with_memory_space_constraint(folded, pltpu.HBM))


def shift_blocks(partials, fields, table):
    count, strips, _ = partials.shape

    def body(partials_ref, fields_ref, table_ref, out_ref):
        total = jnp.sum(partials_ref[...].astype(jnp.float32), axis=0)
        shift = fields_ref[...] - jnp.clip(sqrt_tau * total, -bias_cap, bias_cap)
        block = jnp.concatenate([shift, table_ref[...]], axis=0).astype(jnp.bfloat16)
        out_ref[...] = jnp.broadcast_to(block[None], out_ref.shape)

    return pl.pallas_call(
        body,
        out_shape=jax.ShapeDtypeStruct((count, strips + table.shape[0], LANES), jnp.bfloat16),
        in_specs=[VMEM, VMEM, VMEM],
        out_specs=VMEM,
        compiler_params=params(4),
        name="shift_blocks",
    )(partials, fields, table)


def potential(blocks, chol, w_local, orbitals):
    count, height, _ = blocks.shape
    vectors, pairs = chol.shape
    rows = pairs // orbitals
    each = vectors // LANES
    walkers = count * w_local
    group = 8

    def body(blocks_ref, chol_ref, out_ref, wide_ref, shift_ref, acc_ref):
        wide_ref[...] = blocks_ref[...].astype(jnp.float32).reshape(count * height, LANES)
        for slot in range(w_local):
            for strip in range(each):
                shift_ref[pl.ds(slot * count, count), pl.ds(strip * LANES, LANES)] = wide_ref[
                    pl.ds(slot * each + strip, count, stride=height), :
                ].astype(jnp.bfloat16)
        table = wide_ref[pl.ds(w_local * each, count, stride=height), :]
        device = lax.broadcasted_iota(jnp.int32, (count, walkers), 0).astype(jnp.float32)
        place = lax.broadcasted_iota(jnp.int32, (count, walkers), 1).astype(jnp.float32)
        picks = []
        for slot in range(w_local):
            parent = device + table[:, slot : slot + 1]
            parent = jnp.where(parent < 0, parent + count, parent)
            parent = jnp.where(parent >= count, parent - count, parent)
            parent = parent + count * table[:, w_local + slot : w_local + slot + 1]
            picks.append(jnp.where(place == parent, 1.0, 0.0))
        pick = jnp.concatenate(picks, axis=0).astype(jnp.bfloat16)
        shift = jnp.dot(pick, shift_ref[...], preferred_element_type=jnp.float32).astype(jnp.bfloat16)

        @pl.loop(0, rows // group)
        def _(step):
            for inner in range(group):
                row = step * group + inner
                cols = pl.ds(pl.multiple_of(row * orbitals, orbitals), orbitals)
                part = sqrt_tau * jnp.dot(shift, chol_ref[:, cols], preferred_element_type=jnp.float32)
                for slot in range(w_local):
                    for lane in range(orbitals // LANES):
                        acc_ref[lane, pl.ds(slot * group + inner, count, stride=w_local * group), :] = part[
                            slot * count : (slot + 1) * count, lane * LANES : (lane + 1) * LANES
                        ]
            for lane in range(orbitals // LANES):
                done = acc_ref[lane].reshape(count, w_local, group, LANES).astype(jnp.bfloat16)
                for slot in range(w_local):
                    start = pl.multiple_of(slot * rows + step * group, group)
                    out_ref[:, pl.ds(start, group), pl.ds(lane * LANES, LANES)] = done[:, slot]

    return pl.pallas_call(
        body,
        out_shape=jax.ShapeDtypeStruct((count, w_local * rows, orbitals), jnp.bfloat16),
        in_specs=[VMEM, VMEM],
        out_specs=VMEM,
        scratch_shapes=[
            pltpu.VMEM((count * height, LANES), jnp.float32),
            pltpu.VMEM((walkers, vectors), jnp.bfloat16),
            pltpu.VMEM((orbitals // LANES, walkers * group, LANES), jnp.float32),
        ],
        compiler_params=params(10),
        name="potential",
    )(blocks, chol)


def propagate(blocks, one_body, low, own, high, src_shift, src_slot):
    w_local, orbitals, occupied = own.shape
    count, height, _ = blocks.shape
    rows = height // w_local

    def body(blocks_ref, one_ref, low_ref, own_ref, high_ref, shift_ref, slot_ref, out_ref, start_ref):
        one = one_ref[...].astype(jnp.float32)
        for walker in range(w_local):
            for offset, source in ((-1, low_ref), (0, own_ref), (1, high_ref)):

                @pl.when(shift_ref[walker] == offset)
                def _():
                    start_ref[...] = source[slot_ref[walker]]

            mine = blocks_ref[:, walker * rows : (walker + 1) * rows, :]
            amat = mine.astype(jnp.float32).reshape(orbitals, orbitals) + one
            amat = amat.astype(jnp.bfloat16)
            term = start_ref[...]
            total = term.astype(jnp.float32)
            for order in range(1, TERMS):
                product = jnp.dot(amat, term, preferred_element_type=jnp.float32) / order
                total = total + product
                term = product.astype(jnp.bfloat16)
            out_ref[walker] = total.astype(jnp.bfloat16)

    return pl.pallas_call(
        body,
        out_shape=jax.ShapeDtypeStruct(own.shape, jnp.bfloat16),
        in_specs=[VMEM, VMEM, VMEM, VMEM, VMEM, SMEM, SMEM],
        out_specs=VMEM,
        scratch_shapes=[pltpu.VMEM((orbitals, occupied), jnp.bfloat16)],
        compiler_params=params(16),
        name="propagate",
    )(blocks, one_body, low, own, high, src_shift, src_slot)


def plain(chol, walkers, trial, one_body, fields, src_shift, src_slot):
    count = lax.axis_size("pair")
    w_local, orbitals, _ = walkers.shape
    moved = lax.all_to_all(walkers, "pair", split_axis=1, concat_axis=0, tiled=True)
    formed = jnp.einsum("wia,ka->wik", moved, trial, preferred_element_type=jnp.float32)
    green_rows = formed.astype(jnp.bfloat16).reshape(moved.shape[0], moved.shape[1] * orbitals)
    partial_bias = lax.dot_general(
        green_rows, chol, (((1,), (1,)), ((), ())), preferred_element_type=jnp.float32
    )
    partials = exchange(partial_bias).reshape(count, w_local, -1)
    total = jnp.sum(partials, axis=0)
    shift = (fields - jnp.clip(sqrt_tau * total, -bias_cap, bias_cap)).astype(jnp.bfloat16)
    shifts = exchange(jnp.broadcast_to(shift[None], (count,) + shift.shape))
    shifts = shifts.reshape(count * w_local, -1)
    local_potential = (sqrt_tau * jnp.dot(shifts, chol, preferred_element_type=jnp.float32)).astype(
        jnp.bfloat16
    )
    own_potential = lax.all_to_all(local_potential, "pair", split_axis=0, concat_axis=1, tiled=True)
    amat = own_potential.astype(jnp.float32).reshape(w_local, orbitals, orbitals) + one_body.astype(
        jnp.float32
    )
    amat = amat.astype(jnp.bfloat16)
    term = walkers
    total = walkers.astype(jnp.float32)
    for order in range(1, TERMS):
        product = jnp.einsum("wik,wka->wia", amat, term, preferred_element_type=jnp.float32) / order
        total = total + product
        term = product.astype(jnp.bfloat16)
    propagated = total.astype(jnp.bfloat16)
    low, high = neighbours(propagated)
    position = (src_shift + 1) * w_local + src_slot
    return jnp.take(jnp.concatenate([low, propagated, high], axis=0), position, axis=0)


def held(chol, walkers, trial, one_body, fields, src_shift, src_slot):
    count = lax.axis_size("pair")
    w_local, orbitals, occupied = walkers.shape
    vectors, pairs = chol.shape
    rows = pairs // orbitals
    strips = w_local * vectors // LANES

    low, high = neighbours(walkers)
    sent = walkers.reshape(w_local, count, rows, occupied).transpose(1, 0, 2, 3)
    moved = exchange(sent.reshape(count, w_local * rows, occupied))
    folded = fold_trial(chol, trial)
    moved = moved.reshape(count * w_local, rows * occupied)
    entries = jnp.concatenate([src_shift, src_slot]).astype(jnp.float32)
    table = jnp.zeros((8, LANES), jnp.float32).at[0, : 2 * w_local].set(entries)
    fields = fields.reshape(strips, LANES)
    moved, table, fields = lax.optimization_barrier((moved, table, fields))
    partial = bias_partial(moved, folded).reshape(count, strips, LANES)
    partials = exchange(partial)
    blocks = exchange(shift_blocks(partials, fields, table))
    received = exchange(potential(blocks, chol, w_local, orbitals))
    return propagate(received, one_body, low, walkers, high, src_shift, src_slot)


def shards(chol, walkers, *rest):
    rows = chol.shape[1] // walkers.shape[1]
    fits = 2 * chol.size <= 32 * MIB and rows % 16 == 0 and chol.shape[0] % LANES == 0
    return (held if fits else plain)(chol, walkers, *rest)


def solution(mesh):
    placed = (
        P("groups", "pair"),
        P(("groups", "pair"), None, None),
        P("groups", None),
        P("groups", None),
        P(("groups", "pair"), None),
        P(("groups", "pair")),
        P(("groups", "pair")),
    )
    return jax.shard_map(
        shards,
        mesh=mesh,
        in_specs=placed,
        out_specs=P(("groups", "pair"), None, None),
        check_vma=False,
    )
```

time: 203 us -> 113 us (0.56)
  waiting for transfers between devices: 98.9 us -> 24.3 us
  Pallas kernels: 0 us -> 37.1 us
  matrix products: 34.9 us -> 0 us
  blocking collectives: 36.1 us -> 21.7 us
  between operations: 13.6 us -> 0.05 us
  starting transfers between devices: 7.75 us -> 13.6 us
  local copies, waits for them, and re-layouts: 8.9 us -> 14 us
    psum x1 -> x0, waiting for transfers between devices: 67.3 us -> none  [shards(): summed = lax.psum(partial_bias, 'pair')]
    pallas_call x0 -> x5, Pallas kernels: none -> 37.1 us  [the longest x1 18.4 us: fold_trial(): pl.pallas_call(body, out_shape=pltpu.HBM((vectors, rows * occupied), jnp....]
    dot_general x8 -> x0, matrix products: 34.9 us -> none  [the longest x1 16.5 us: shards(): jnp.dot(shift, chol, preferred_element_type=jnp.float32)]
    all_gather x1 -> x0, blocking collectives: 19.4 us -> none  [shards(): every_field = lax.all_gather(fields, 'pair', axis=0, tiled=True)]
    all_to_all x1 -> x2, waiting for transfers between devices: 23 us -> 13.1 us  [exchange(): lax.all_to_all(blocks, 'pair', split_axis=0, concat_axis=0, tiled=True)]
    unnamed x15 -> x12, local copies, waits for them, and re-layouts: 2.49 us -> 11.5 us
    all_to_all x1 -> x2, starting transfers between devices: 6.57 us -> 11.9 us  [exchange(): lax.all_to_all(blocks, 'pair', split_axis=0, concat_axis=0, tiled=True)]
    all_to_all x1 -> x2, blocking collectives: 16.6 us -> 21.7 us  [exchange(): lax.all_to_all(blocks, 'pair', split_axis=0, concat_axis=0, tiled=True)]
  transfers between devices with their start and end apart: 4 -> 4, of which waited for: 4 -> 3; matrix products, arithmetic and copies ran while one was open for 0% -> 1% of each run, Pallas kernels for 0% -> 17%
where the time goes in v1:
time: 113 us; the launch traced here: 112 us
  Pallas kernels  37.1 us (33%)
  waiting for transfers between devices  24.3 us (22%)
  blocking collectives  21.7 us (19%)
  local copies, waits for them, and re-layouts  14 us (12%)
  starting transfers between devices  13.6 us (12%)
    all_to_all x2, blocking collectives, exchange(): lax.all_to_all(blocks, 'pair', split_axis=0, concat_axis=0, tiled=True)  21.7 us
    pallas_call x1, Pallas kernels, fold_trial(): pl.pallas_call(body, out_shape=pltpu.HBM((vectors, rows * occupied), jnp....  18.4 us
    all_to_all x2, waiting for transfers between devices, exchange(): lax.all_to_all(blocks, 'pair', split_axis=0, concat_axis=0, tiled=True)  13.1 us
    all_to_all x2, starting transfers between devices, exchange(): lax.all_to_all(blocks, 'pair', split_axis=0, concat_axis=0, tiled=True)  11.9 us
    unnamed x12, local copies, waits for them, and re-layouts  11.5 us
    pallas_call x1, Pallas kernels, potential(): pl.pallas_call(body, out_shape=jax.ShapeDtypeStruct((count, w_local * row...  8.35 us
    ppermute x1, waiting for transfers between devices, neighbours(): lax.ppermute(block, 'pair', forward)  7.6 us
    pallas_call x1, Pallas kernels, bias_partial(): pl.pallas_call(body, out_shape=jax.ShapeDtypeStruct((walkers * strips, LA...  5.62 us
  transfers between devices with their start and end apart: 4, of which 3 were waited for; matrix products, arithmetic and copies ran while one was open for 1% of the time, Pallas kernels for 17%

profile of v1, /device:TPU:1, one launch (start us, length us, event | category | flops | bytes accessed | tf_op | source)
XLA Modules:
  0.0 111.5 jit_solution(17783527726628829457)
XLA Ops:
  0.0 1.7 %copy.8 = bf16[16,2,32,128]{3,2,1,0:T(8,128)(2,1)} copy(bf16[16,2,32,128]{3,2,0,1:T(8,128)(2,1)} %bitcast.7) | data formatting | bytes 524288 | tf_op jit(solution)/shard_map/transpose | solution.py:263
  1.7 7.3 %all-to-all-start = ((bf16[16,64,128]{2,1,0:T(8,128)(2,1)}), bf16[16,64,128]{2,1,0:T(8,128)(2,1)S(1)}, u32[]{:S(2)}, u32[]{:S(2)}) async-start(bf16[16,64,128]{2,1,0:T(8,128)(2,1)} %bitcast.2), calls=%async_computation | async-start | bytes 524288 | tf_op jit(solution)/shard_map/all_to_all | solution.py:29
  9.0 0.7 reshape.66.fields_ref
  9.7 0.7 add_convert_fusion
  10.5 0.0 copy-start.3
  10.5 0.9 copy-done.3
  11.4 18.4 %fold_trial.1.folded_ref = bf16[1024,4096]{1,0:T(8,128)(2,1)} custom-call(bf16[1024,16384]{1,0:T(8,128)(2,1)} %chol_ref.3, bf16[512,128]{1,0:T(8,128)(2,1)S(1)} %copy-done.3), custom_call_target="tpu_custom_call" | custom-call | flops 4294967296 | bytes 33554432 | tf_op jit(solution)/shard_map/fold_trial/pallas_call | solution.py:53
  29.8 0.0 copy-start.1
  29.8 0.0 copy-start.2
  29.8 0.0 copy-start.4
  29.8 0.0 copy-start.5
  29.8 0.0 all-to-all-done
  29.8 0.1 reshape.65.moved_ref
  30.0 5.6 %bias_partial.1 = bf16[256,128]{1,0:T(8,128)(2,1)S(1)} custom-call(bf16[32,4096]{1,0:T(8,128)(2,1)S(1)} %reshape.65.moved_ref, bf16[1024,4096]{1,0:T(8,128)(2,1)} %fold_trial.1.folded_ref), custom_call_target="tpu_custom_call" | custom-call | tf_op jit(solution)/shard_map/bias_partial/pallas_call | solution.py:91
  35.6 11.9 %all_to_all.20.partials_ref = bf16[16,16,128]{2,1,0:T(8,128)(2,1)S(1)} all-to-all(bf16[16,16,128]{2,1,0:T(8,128)(2,1)S(1)} %bitcast.8), channel_id=1, replica_groups=mesh['groups'=2,'pair'=16] {'pair'}, dimensions={0} | all-to-all | bytes 131072 | tf_op jit(solution)/shard_map/all_to_all | solution.py:29
  47.5 9.8 %all_to_all.21.blocks_ref = bf16[16,24,128]{2,1,0:T(8,128)(2,1)S(1)} all-to-all(bf16[16,24,128]{2,1,0:T(8,128)(2,1)S(1)} %shift_blocks.1), channel_id=1, replica_groups=mesh['groups'=2,'pair'=16] {'pair'}, dimensions={0} | all-to-all | bytes 196608 | tf_op jit(solution)/shard_map/all_to_all | solution.py:29
  57.3 0.0 copy-start
  57.3 10.5 %copy-done = bf16[1024,16384]{1,0:T(8,128)(2,1)S(1)} copy-done((bf16[1024,16384]{1,0:T(8,128)(2,1)S(1)}, bf16[1024,16384]{1,0:T(8,128)(2,1)}, u32[]{:S(2)}) %copy-start) | copy-done | bytes 33554456
  67.8 8.3 %potential.1 = bf16[16,64,512]{2,1,0:T(8,128)(2,1)} custom-call(bf16[16,24,128]{2,1,0:T(8,128)(2,1)S(1)} %all_to_all.21.blocks_ref, bf16[1024,16384]{1,0:T(8,128)(2,1)S(1)} %copy-done), custom_call_target="tpu_custom_call" | custom-call | tf_op jit(solution)/shard_map/potential/pallas_call | solution.py:170
  76.2 4.5 %all-to-all-start.3 = ((bf16[16,64,512]{2,1,0:T(8,128)(2,1)}), bf16[16,64,512]{2,1,0:T(8,128)(2,1)S(1)}, u32[]{:S(2)}, u32[]{:S(2)}) async-start(bf16[16,64,512]{2,1,0:T(8,128)(2,1)} %potential.1), calls=%async_computation.3 | async-start | bytes 2097152 | tf_op jit(solution)/shard_map/all_to_all | solution.py:29
  80.7 0.0 copy-done.1
  80.7 1.7 %collective-permute-start = (bf16[2,512,128]{2,1,0:T(8,128)(2,1)S(1)}, bf16[2,512,128]{2,1,0:T(8,128)(2,1)S(1)}, u32[]{:S(2)}, u32[]{:S(2)}) collective-permute-start(bf16[2,512,128]{2,1,0:T(8,128)(2,1)S(1)} %copy-done.1), channel_id=1, source_target_pairs={{0,1},{1,2},{2,3},{3,4},{4,5},{5,6},{6,7},{7,8},{8,9},{9,10},{10,1... | collective-permute-start | bytes 786440 | tf_op jit(solution)/shard_map/ppermute | solution.py:36
  82.4 0.0 collective-permute-start.1
  82.4 7.6 %collective-permute-done.low_ref = bf16[2,512,128]{2,1,0:T(8,128)(2,1)S(1)} collective-permute-done((bf16[2,512,128]{2,1,0:T(8,128)(2,1)S(1)}, bf16[2,512,128]{2,1,0:T(8,128)(2,1)S(1)}, u32[]{:S(2)}, u32[]{:S(2)}) %collective-permute-start) | collective-permute-done | bytes 262176 | tf_op jit(solution)/shard_map/ppermute | solution.py:36
  90.0 3.7 %collective-permute-done.1.high_ref = bf16[2,512,128]{2,1,0:T(8,128)(2,1)S(1)} collective-permute-done((bf16[2,512,128]{2,1,0:T(8,128)(2,1)S(1)}, bf16[2,512,128]{2,1,0:T(8,128)(2,1)S(1)}, u32[]{:S(2)}, u32[]{:S(2)}) %collective-permute-start.1) | collective-permute-done | bytes 262176 | tf_op jit(solution)/shard_map/ppermute | solution.py:36
  93.7 13.1 %all-to-all-done.3.blocks_ref = bf16[16,64,512]{2,1,0:T(8,128)(2,1)S(1)} async-done(((bf16[16,64,512]{2,1,0:T(8,128)(2,1)}), bf16[16,64,512]{2,1,0:T(8,128)(2,1)S(1)}, u32[]{:S(2)}, u32[]{:S(2)}) %all-to-all-start.3) | async-done | bytes 1048608 | tf_op jit(solution)/shard_map/all_to_all | solution.py:29
  106.8 0.0 copy-done.2
  106.8 0.0 copy-done.4
  106.8 0.0 copy-done.5
  106.8 4.7 %propagate.1 = bf16[2,512,128]{2,1,0:T(8,128)(2,1)} custom-call(bf16[16,64,512]{2,1,0:T(8,128)(2,1)S(1)} %all-to-all-done.3.blocks_ref, bf16[512,512]{1,0:T(8,128)(2,1)S(1)} %copy-done.2, bf16[2,512,128]{2,1,0:T(8,128)(2,1)S(1)} %collective-permute-done.low_ref, bf16[2,512,128]{2,1,0:T(8,128)(2,1)S(1)} %copy-done.1, ...), custom_call_target="tpu_custom_call" | custom-call | tf_op jit(solution)/shard_map/propagate/pallas_call | solution.py:210
  (2 shorter events, 0.0 us)
Async XLA Ops:
  1.7 28.1 %all-to-all-start = ((bf16[16,64,128]{2,1,0:T(8,128)(2,1)}), bf16[16,64,128]{2,1,0:T(8,128)(2,1)S(1)}, u32[]{:S(2)}, u32[]{:S(2)}) async-start(bf16[16,64,128]{2,1,0:T(8,128)(2,1)} %bitcast.2), calls=%async_computation | async-start | bytes 524288 | tf_op jit(solution)/shard_map/all_to_all | solution.py:29
  10.5 0.9 copy-start.3
  29.8 50.9 %copy-start.1 = (bf16[2,512,128]{2,1,0:T(8,128)(2,1)S(1)}, bf16[2,512,128]{2,1,0:T(8,128)(2,1)}, u32[]{:S(2)}) copy-start(bf16[2,512,128]{2,1,0:T(8,128)(2,1)} %own_ref.1) | copy-start | bytes 786436
  29.8 77.0 %copy-start.2 = (bf16[512,512]{1,0:T(8,128)(2,1)S(1)}, bf16[512,512]{1,0:T(8,128)(2,1)}, u32[]{:S(2)}) copy-start(bf16[512,512]{1,0:T(8,128)(2,1)} %one_ref.1) | copy-start | bytes 1572868
  29.8 77.0 %copy-start.4 = (s32[2]{0:T(128)S(1)}, s32[2]{0:T(128)}, u32[]{:S(2)}) copy-start(s32[2]{0:T(128)} %slot_ref.1) | copy-start | bytes 28
  29.8 77.0 %copy-start.5 = (s32[2]{0:T(128)S(1)}, s32[2]{0:T(128)}, u32[]{:S(2)}) copy-start(s32[2]{0:T(128)} %shift_ref.1) | copy-start | bytes 28
  57.3 10.5 %copy-start = (bf16[1024,16384]{1,0:T(8,128)(2,1)S(1)}, bf16[1024,16384]{1,0:T(8,128)(2,1)}, u32[]{:S(2)}) copy-start(bf16[1024,16384]{1,0:T(8,128)(2,1)} %chol_ref.3) | copy-start | bytes 100663296
  76.2 30.6 %all-to-all-start.3 = ((bf16[16,64,512]{2,1,0:T(8,128)(2,1)}), bf16[16,64,512]{2,1,0:T(8,128)(2,1)S(1)}, u32[]{:S(2)}, u32[]{:S(2)}) async-start(bf16[16,64,512]{2,1,0:T(8,128)(2,1)} %potential.1), calls=%async_computation.3 | async-start | bytes 2097152 | tf_op jit(solution)/shard_map/all_to_all | solution.py:29
  80.7 9.3 %collective-permute-start = (bf16[2,512,128]{2,1,0:T(8,128)(2,1)S(1)}, bf16[2,512,128]{2,1,0:T(8,128)(2,1)S(1)}, u32[]{:S(2)}, u32[]{:S(2)}) collective-permute-start(bf16[2,512,128]{2,1,0:T(8,128)(2,1)S(1)} %copy-done.1), channel_id=1, source_target_pairs={{0,1},{1,2},{2,3},{3,4},{4,5},{5,6},{6,7},{7,8},{8,9},{9,10},{10,1... | collective-permute-start | bytes 786440 | tf_op jit(solution)/shard_map/ppermute | solution.py:36
  82.4 11.3 %collective-permute-start.1 = (bf16[2,512,128]{2,1,0:T(8,128)(2,1)S(1)}, bf16[2,512,128]{2,1,0:T(8,128)(2,1)S(1)}, u32[]{:S(2)}, u32[]{:S(2)}) collective-permute-start(bf16[2,512,128]{2,1,0:T(8,128)(2,1)S(1)} %copy-done.1), channel_id=1, source_target_pairs={{1,0},{2,1},{3,2},{4,3},{5,4},{6,5},{7,6},{8,7},{9,8},{10,9},{11,1... | collective-permute-start | bytes 786440 | tf_op jit(solution)/shard_map/ppermute | solution.py:36

commit v2 on v0

v2 whole, which is shorter than its diff:
```python
import jax
import jax.numpy as jnp
from jax import lax
from jax.experimental import pallas as pl
from jax.experimental.pallas import tpu as pltpu
from jax.sharding import PartitionSpec as P


TERMS = 6
LANES = 128
MIB = 1 << 20
GROUP = 8
COVER = pl.CostEstimate(flops=100_000_000_000, bytes_accessed=400_000_000, transcendentals=0)

sqrt_tau = 0.1
bias_cap = 1.0

VMEM = pl.BlockSpec(memory_space=pltpu.VMEM)
SMEM = pl.BlockSpec(memory_space=pltpu.SMEM)
ANY = pl.BlockSpec(memory_space=pl.ANY)


def params(mib):
    return pltpu.CompilerParams(vmem_limit_bytes=mib * MIB)


def exchange(blocks):
    return lax.all_to_all(blocks, "pair", split_axis=0, concat_axis=0, tiled=True)


def neighbours(block):
    count = lax.axis_size("pair")
    forward = [(i, (i + 1) % count) for i in range(count)]
    backward = [(target, source) for source, target in forward]
    return lax.ppermute(block, "pair", forward), lax.ppermute(block, "pair", backward)


def pack(walkers, count):
    w_local, orbitals, occupied = walkers.shape
    rows = orbitals // count

    def body(in_ref, out_ref):
        for walker in range(w_local):
            out_ref[:, walker * rows : (walker + 1) * rows, :] = in_ref[walker].reshape(count, rows, occupied)

    return pl.pallas_call(
        body,
        out_shape=jax.ShapeDtypeStruct((count, w_local * rows, occupied), jnp.bfloat16),
        in_specs=[VMEM],
        out_specs=VMEM,
        compiler_params=params(4),
        cost_estimate=COVER,
        name="pack",
    )(walkers)


def bias_partial(moved, trial, chol, w_local):
    count, height, occupied = moved.shape
    orbitals = trial.shape[0]
    vectors, pairs = chol.shape
    rows = pairs // orbitals
    walkers = count * w_local
    strips = vectors // LANES
    steps = 4
    width = pairs // steps

    def body(moved_ref, trial_ref, chol_ref, out_ref, wide_ref, lhs_ref, green_ref, acc_ref, flat_ref):
        wide_ref[...] = moved_ref[...].astype(jnp.float32).reshape(count * height, occupied)
        for row in range(rows):
            lhs_ref[row * walkers : (row + 1) * walkers, :] = wide_ref[
                pl.ds(row, walkers, stride=rows), :
            ].astype(jnp.bfloat16)
        formed = lax.dot_general(
            lhs_ref[...], trial_ref[...], (((1,), (1,)), ((), ())), preferred_element_type=jnp.float32
        )
        for row in range(rows):
            green_ref[:, row * orbitals : (row + 1) * orbitals] = formed[
                row * walkers : (row + 1) * walkers, :
            ].astype(jnp.bfloat16)
        acc_ref[...] = jnp.zeros_like(acc_ref)

        @pl.loop(0, steps)
        def _(step):
            cols = pl.ds(pl.multiple_of(step * width, width), width)
            acc_ref[...] += lax.dot_general(
                chol_ref[:, cols], green_ref[:, cols], (((1,), (1,)), ((), ())), preferred_element_type=jnp.float32
            )

        for strip in range(strips):
            flat_ref[pl.ds(strip, walkers, stride=strips), :] = acc_ref[strip * LANES : (strip + 1) * LANES, :].T
        out_ref[...] = flat_ref[...].astype(jnp.bfloat16).reshape(out_ref.shape)

    return pl.pallas_call(
        body,
        out_shape=jax.ShapeDtypeStruct((count, w_local * strips, LANES), jnp.bfloat16),
        in_specs=[VMEM, VMEM, VMEM],
        out_specs=VMEM,
        scratch_shapes=[
            pltpu.VMEM((count * height, occupied), jnp.float32),
            pltpu.VMEM((count * height, occupied), jnp.bfloat16),
            pltpu.VMEM((walkers, pairs), jnp.bfloat16),
            pltpu.VMEM((vectors, walkers), jnp.float32),
            pltpu.VMEM((walkers * strips, LANES), jnp.float32),
        ],
        compiler_params=params(16),
        name="bias_partial",
    )(moved, trial, chol)


def shift_blocks(partials, fields, src_shift, src_slot):
    count, strips, _ = partials.shape
    w_local, vectors = fields.shape
    each = vectors // LANES

    def body(partials_ref, fields_ref, from_ref, slot_ref, out_ref, flat_ref):
        for walker in range(w_local):
            for strip in range(each):
                flat_ref[walker * each + strip, :] = fields_ref[walker, strip * LANES : (strip + 1) * LANES]
        total = jnp.sum(partials_ref[...].astype(jnp.float32), axis=0)
        shift = flat_ref[...] - jnp.clip(sqrt_tau * total, -bias_cap, bias_cap)
        lane = lax.broadcasted_iota(jnp.int32, (8, LANES), 1)
        table = jnp.zeros((8, LANES), jnp.int32)
        for walker in range(w_local):
            table = jnp.where(lane == walker, from_ref[walker], table)
            table = jnp.where(lane == w_local + walker, slot_ref[walker], table)
        block = jnp.concatenate([shift, table.astype(jnp.float32)], axis=0).astype(jnp.bfloat16)
        out_ref[...] = jnp.broadcast_to(block[None], out_ref.shape)

    return pl.pallas_call(
        body,
        out_shape=jax.ShapeDtypeStruct((count, strips + 8, LANES), jnp.bfloat16),
        in_specs=[VMEM, VMEM, SMEM, SMEM],
        out_specs=VMEM,
        scratch_shapes=[pltpu.VMEM((strips, LANES), jnp.float32)],
        compiler_params=params(4),
        cost_estimate=COVER,
        name="shift_blocks",
    )(partials, fields, src_shift, src_slot)


def parents_shift(blocks_ref, wide_ref, shift_ref, w_local, each):
    count, height, _ = blocks_ref.shape
    walkers = count * w_local
    wide_ref[...] = blocks_ref[...].astype(jnp.float32).reshape(count * height, LANES)
    for slot in range(w_local):
        for strip in range(each):
            shift_ref[slot * count : (slot + 1) * count, strip * LANES : (strip + 1) * LANES] = wide_ref[
                pl.ds(slot * each + strip, count, stride=height), :
            ].astype(jnp.bfloat16)
    table = wide_ref[pl.ds(w_local * each, count, stride=height), :]
    device = lax.broadcasted_iota(jnp.int32, (count, walkers), 0).astype(jnp.float32)
    place = lax.broadcasted_iota(jnp.int32, (count, walkers), 1).astype(jnp.float32)
    picks = []
    for slot in range(w_local):
        parent = device + table[:, slot : slot + 1]
        parent = jnp.where(parent < 0, parent + count, parent)
        parent = jnp.where(parent >= count, parent - count, parent)
        parent = parent + count * table[:, w_local + slot : w_local + slot + 1]
        picks.append(jnp.where(place == parent, 1.0, 0.0))
    pick = jnp.concatenate(picks, axis=0).astype(jnp.bfloat16)
    return jnp.dot(pick, shift_ref[...], preferred_element_type=jnp.float32).astype(jnp.bfloat16)


def spread(part, acc_ref, inner, count, w_local, group):
    for slot in range(w_local):
        for lane in range(part.shape[1] // LANES):
            acc_ref[lane, pl.ds(slot * group + inner, count, stride=w_local * group), :] = part[
                slot * count : (slot + 1) * count, lane * LANES : (lane + 1) * LANES
            ]


def settle(acc_ref, out_ref, start, count, w_local, group, rows):
    for lane in range(acc_ref.shape[0]):
        done = acc_ref[lane].reshape(count, w_local, group, LANES).astype(jnp.bfloat16)
        for slot in range(w_local):
            out_ref[:, pl.ds(pl.multiple_of(slot * rows + start, group), group), pl.ds(lane * LANES, LANES)] = done[
                :, slot
            ]


def potential_held(blocks, chol, w_local, orbitals, rows):
    count, height, _ = blocks.shape
    vectors = chol.shape[0]
    walkers = count * w_local
    each = vectors // LANES

    def body(blocks_ref, chol_ref, out_ref, picked_ref, wide_ref, shift_ref, acc_ref):
        shift = parents_shift(blocks_ref, wide_ref, shift_ref, w_local, each)
        picked_ref[...] = shift

        @pl.loop(0, rows // GROUP)
        def _(step):
            for pair in range(0, GROUP, 4):
                start = (step * GROUP + pair) * orbitals
                cols = pl.ds(pl.multiple_of(start, 4 * orbitals), 4 * orbitals)
                part = sqrt_tau * jnp.dot(shift, chol_ref[:, cols], preferred_element_type=jnp.float32)
                for inner in range(4):
                    spread(
                        part[:, inner * orbitals : (inner + 1) * orbitals], acc_ref, pair + inner, count, w_local, GROUP
                    )
            settle(acc_ref, out_ref, step * GROUP, count, w_local, GROUP, rows)

    return pl.pallas_call(
        body,
        out_shape=(
            jax.ShapeDtypeStruct((count, w_local * rows, orbitals), jnp.bfloat16),
            jax.ShapeDtypeStruct((walkers, vectors), jnp.bfloat16),
        ),
        in_specs=[VMEM, VMEM],
        out_specs=(VMEM, VMEM),
        scratch_shapes=[
            pltpu.VMEM((count * height, LANES), jnp.float32),
            pltpu.VMEM((walkers, vectors), jnp.bfloat16),
            pltpu.VMEM((orbitals // LANES, walkers * GROUP, LANES), jnp.float32),
        ],
        compiler_params=params(12),
        name="potential_held",
    )(blocks, chol)


def potential_streamed(shift, chol, w_local, orbitals, first, rows):
    walkers, vectors = shift.shape
    count = walkers // w_local
    per = 4

    def body(shift_ref, chol_ref, out_ref, acc_ref):
        step = pl.program_id(0)
        half = lax.rem(step, GROUP // per)
        part = sqrt_tau * jnp.dot(shift_ref[...], chol_ref[...], preferred_element_type=jnp.float32)
        for inner in range(per):
            spread(
                part[:, inner * orbitals : (inner + 1) * orbitals], acc_ref, half * per + inner, count, w_local, GROUP
            )

        @pl.when(half == GROUP // per - 1)
        def _():
            settle(acc_ref, out_ref, (step * per) // GROUP * GROUP, count, w_local, GROUP, rows)

    return pl.pallas_call(
        body,
        out_shape=jax.ShapeDtypeStruct((count, w_local * rows, orbitals), jnp.bfloat16),
        grid=(rows // per,),
        in_specs=[
            pl.BlockSpec((walkers, vectors), lambda i: (0, 0)),
            pl.BlockSpec((vectors, per * orbitals), lambda i: (0, first // per + i)),
        ],
        out_specs=pl.BlockSpec((count, w_local * rows, orbitals), lambda i: (0, 0, 0)),
        scratch_shapes=[pltpu.VMEM((orbitals // LANES, walkers * GROUP, LANES), jnp.float32)],
        compiler_params=params(20),
        cost_estimate=pl.CostEstimate(
            flops=2 * walkers * vectors * rows * orbitals, bytes_accessed=2 * vectors * rows * orbitals, transcendentals=0
        ),
        name="potential_streamed",
    )(shift, pltpu.with_memory_space_constraint(chol, pltpu.HBM))


def propagate(early, late, one_body, low, own, high, src_shift, src_slot):
    w_local, orbitals, occupied = own.shape
    count = early.shape[0]
    rows = orbitals // count
    cut = early.shape[1] // w_local

    def body(early_ref, late_ref, one_ref, low_ref, own_ref, high_ref, from_ref, slot_ref, out_ref, start_ref, mat_ref):
        one = one_ref[...].astype(jnp.float32).reshape(count, rows, orbitals)
        for walker in range(w_local):
            for offset, source in ((-1, low_ref), (0, own_ref), (1, high_ref)):

                @pl.when(from_ref[walker] == offset)
                def _():
                    start_ref[...] = source[slot_ref[walker]]

            for ref, low_row, high_row in ((early_ref, 0, cut), (late_ref, cut, rows)):
                tall = high_row - low_row
                mine = ref[:, walker * tall : (walker + 1) * tall, :].astype(jnp.float32)
                mat_ref[:, low_row:high_row, :] = (mine + one[:, low_row:high_row, :]).astype(jnp.bfloat16)
            amat = mat_ref[...].reshape(orbitals, orbitals)
            term = start_ref[...]
            total = term.astype(jnp.float32)
            for order in range(1, TERMS):
                product = jnp.dot(amat, term, preferred_element_type=jnp.float32) / order
                total = total + product
                term = product.astype(jnp.bfloat16)
            out_ref[walker] = total.astype(jnp.bfloat16)

    return pl.pallas_call(
        body,
        out_shape=jax.ShapeDtypeStruct(own.shape, jnp.bfloat16),
        in_specs=[VMEM, VMEM, VMEM, VMEM, VMEM, VMEM, SMEM, SMEM],
        out_specs=VMEM,
        scratch_shapes=[
            pltpu.VMEM((orbitals, occupied), jnp.bfloat16),
            pltpu.VMEM((count, rows, orbitals), jnp.bfloat16),
        ],
        compiler_params=params(16),
        name="propagate",
    )(early, late, one_body, low, own, high, src_shift, src_slot)


def plain(chol, walkers, trial, one_body, fields, src_shift, src_slot):
    count = lax.axis_size("pair")
    w_local, orbitals, _ = walkers.shape
    moved = lax.all_to_all(walkers, "pair", split_axis=1, concat_axis=0, tiled=True)
    formed = jnp.einsum("wia,ka->wik", moved, trial, preferred_element_type=jnp.float32)
    green_rows = formed.astype(jnp.bfloat16).reshape(moved.shape[0], moved.shape[1] * orbitals)
    partial_bias = lax.dot_general(
        green_rows, chol, (((1,), (1,)), ((), ())), preferred_element_type=jnp.float32
    )
    partials = exchange(partial_bias).reshape(count, w_local, -1)
    total = jnp.sum(partials, axis=0)
    shift = (fields - jnp.clip(sqrt_tau * total, -bias_cap, bias_cap)).astype(jnp.bfloat16)
    shifts = exchange(jnp.broadcast_to(shift[None], (count,) + shift.shape))
    shifts = shifts.reshape(count * w_local, -1)
    local_potential = (sqrt_tau * jnp.dot(shifts, chol, preferred_element_type=jnp.float32)).astype(
        jnp.bfloat16
    )
    own_potential = lax.all_to_all(local_potential, "pair", split_axis=0, concat_axis=1, tiled=True)
    amat = own_potential.astype(jnp.float32).reshape(w_local, orbitals, orbitals) + one_body.astype(
        jnp.float32
    )
    amat = amat.astype(jnp.bfloat16)
    term = walkers
    total = walkers.astype(jnp.float32)
    for order in range(1, TERMS):
        product = jnp.einsum("wik,wka->wia", amat, term, preferred_element_type=jnp.float32) / order
        total = total + product
        term = product.astype(jnp.bfloat16)
    propagated = total.astype(jnp.bfloat16)
    low, high = neighbours(propagated)
    position = (src_shift + 1) * w_local + src_slot
    return jnp.take(jnp.concatenate([low, propagated, high], axis=0), position, axis=0)


def held(chol, walkers, trial, one_body, fields, src_shift, src_slot):
    count = lax.axis_size("pair")
    w_local, orbitals, _ = walkers.shape
    rows = chol.shape[1] // orbitals
    cut = rows // 2

    low, high = neighbours(walkers)
    moved = exchange(pack(walkers, count))
    partials = exchange(bias_partial(moved, trial, chol, w_local))
    blocks = exchange(shift_blocks(partials, fields, src_shift, src_slot))
    early, shift = potential_held(blocks, chol, w_local, orbitals, cut)
    early = exchange(early)
    late = potential_streamed(shift, chol, w_local, orbitals, cut, rows - cut)
    late = exchange(late)
    return propagate(early, late, one_body, low, walkers, high, src_shift, src_slot)


def shards(chol, walkers, *rest):
    rows = chol.shape[1] // walkers.shape[1]
    fits = 2 * chol.size <= 32 * MIB and rows % 16 == 0 and chol.shape[0] % LANES == 0
    return (held if fits else plain)(chol, walkers, *rest)


def solution(mesh):
    placed = (
        P("groups", "pair"),
        P(("groups", "pair"), None, None),
        P("groups", None),
        P("groups", None),
        P(("groups", "pair"), None),
        P(("groups", "pair")),
        P(("groups", "pair")),
    )
    return jax.shard_map(
        shards,
        mesh=mesh,
        in_specs=placed,
        out_specs=P(("groups", "pair"), None, None),
        check_vma=False,
    )
```

time: 203 us -> 105 us (0.52)
  waiting for transfers between devices: 98.9 us -> 15.1 us
  matrix products: 34.9 us -> 0 us
  Pallas kernels: 0 us -> 27.9 us
  blocking collectives: 36.1 us -> 54.1 us
  between operations: 13.6 us -> 0.07 us
  local copies, waits for them, and re-layouts: 8.9 us -> 1.14 us
  other arithmetic: 2.3 us -> 0 us
    psum x1 -> x0, waiting for transfers between devices: 67.3 us -> none  [shards(): summed = lax.psum(partial_bias, 'pair')]
    all_to_all x1 -> x4, blocking collectives: 16.6 us -> 54.1 us  [exchange(): lax.all_to_all(blocks, 'pair', split_axis=0, concat_axis=0, tiled=True)]
    dot_general x8 -> x0, matrix products: 34.9 us -> none  [the longest x1 16.5 us: shards(): jnp.dot(shift, chol, preferred_element_type=jnp.float32)]
    pallas_call x0 -> x6, Pallas kernels: none -> 27.9 us  [the longest x1 10.1 us: bias_partial(): pl.pallas_call(body, out_shape=jax.ShapeDtypeStruct((count, w_local * str...]
    all_gather x1 -> x0, blocking collectives: 19.4 us -> none  [shards(): every_field = lax.all_gather(fields, 'pair', axis=0, tiled=True)]
    all_to_all x1, waiting for transfers between devices: 23 us -> 7.32 us  [exchange(): lax.all_to_all(blocks, 'pair', split_axis=0, concat_axis=0, tiled=True)]
    convert_element_type x2 -> x0, local copies, waits for them, and re-layouts: 4.29 us -> none  [shards(): own_potential.astype(jnp.float32).reshape(w_local, orbitals, orbitals)]
    all_to_all x1, starting transfers between devices: 6.57 us -> 4.39 us  [exchange(): lax.all_to_all(blocks, 'pair', split_axis=0, concat_axis=0, tiled=True)]
  transfers between devices with their start and end apart: 4 -> 3, of which waited for: 4 -> 3; matrix products, arithmetic and copies ran while one was open for 0% -> 0% of each run, Pallas kernels for 0% -> 0%
where the time goes in v2:
time: 105 us; the launch traced here: 104 us
  blocking collectives  54.1 us (52%)
  Pallas kernels  27.9 us (27%)
  waiting for transfers between devices  15.1 us (14%)
  starting transfers between devices  6.08 us (6%)
  local copies, waits for them, and re-layouts  1.14 us (1%)
    all_to_all x4, blocking collectives, exchange(): lax.all_to_all(blocks, 'pair', split_axis=0, concat_axis=0, tiled=True)  54.1 us
    pallas_call x1, Pallas kernels, bias_partial(): pl.pallas_call(body, out_shape=jax.ShapeDtypeStruct((count, w_local * str...  10.1 us
    pallas_call x1, Pallas kernels, potential_streamed(): pl.pallas_call(body, out_shape=jax.ShapeDtypeStruct((count, w_local * row...  7.88 us
    all_to_all x1, waiting for transfers between devices, exchange(): lax.all_to_all(blocks, 'pair', split_axis=0, concat_axis=0, tiled=True)  7.32 us
    ppermute x1, waiting for transfers between devices, neighbours(): lax.ppermute(block, 'pair', forward)  6.14 us
    pallas_call x1, Pallas kernels, propagate(): pl.pallas_call(body, out_shape=jax.ShapeDtypeStruct(own.shape, jnp.bfloat...  4.72 us
    pallas_call x1, Pallas kernels, potential_held(): pl.pallas_call(body, out_shape=(jax.ShapeDtypeStruct((count, w_local * ro...  4.61 us
    all_to_all x1, starting transfers between devices, exchange(): lax.all_to_all(blocks, 'pair', split_axis=0, concat_axis=0, tiled=True)  4.39 us
  transfers between devices with their start and end apart: 3, of which 3 were waited for; matrix products, arithmetic and copies ran while one was open for 0% of the time, Pallas kernels for 0%

profile of v2, /device:TPU:1, one launch (start us, length us, event | category | flops | bytes accessed | tf_op | source)
XLA Modules:
  0.0 104.4 jit_solution(4319185519308933638)
XLA Ops:
  0.0 0.0 copy-start
  0.0 0.0 copy-start.3
  0.0 1.1 %copy-done.3 = bf16[2,512,128]{2,1,0:T(8,128)(2,1)S(1)} copy-done((bf16[2,512,128]{2,1,0:T(8,128)(2,1)S(1)}, bf16[2,512,128]{2,1,0:T(8,128)(2,1)}, u32[]{:S(2)}) %copy-start.3) | copy-done | bytes 262168
  1.1 0.0 copy-start.5
  1.1 0.0 copy-start.6
  1.1 0.0 copy-start.7
  1.2 0.0 copy-start.8
  1.2 16.9 %all_to_all.25.moved_ref = bf16[16,64,128]{2,1,0:T(8,128)(2,1)S(1)} all-to-all(bf16[16,64,128]{2,1,0:T(8,128)(2,1)S(1)} %pack.1), channel_id=1, replica_groups=mesh['groups'=2,'pair'=16] {'pair'}, dimensions={0} | all-to-all | bytes 524288 | tf_op jit(solution)/shard_map/all_to_all | solution.py:28
  18.1 0.0 copy-done
  18.1 0.0 copy-done.5
  18.1 10.1 %bias_partial.1 = bf16[16,16,128]{2,1,0:T(8,128)(2,1)S(1)} custom-call(bf16[16,64,128]{2,1,0:T(8,128)(2,1)S(1)} %all_to_all.25.moved_ref, bf16[512,128]{1,0:T(8,128)(2,1)S(1)} %copy-done.5, bf16[1024,16384]{1,0:T(8,128)(2,1)S(1)} %copy-done), custom_call_target="tpu_custom_call" | custom-call | tf_op jit(solution)/shard_map/bias_partial/pallas_call | solution.py:93
  28.2 9.2 %all_to_all.26.partials_ref = bf16[16,16,128]{2,1,0:T(8,128)(2,1)S(1)} all-to-all(bf16[16,16,128]{2,1,0:T(8,128)(2,1)S(1)} %bias_partial.1), channel_id=1, replica_groups=mesh['groups'=2,'pair'=16] {'pair'}, dimensions={0} | all-to-all | bytes 131072 | tf_op jit(solution)/shard_map/all_to_all | solution.py:28
  37.4 0.0 copy-done.6
  37.4 0.0 copy-done.7
  37.4 0.0 copy-done.8
  37.4 0.0 copy-start.1
  37.4 0.6 shift_blocks.1
  38.0 10.4 %all_to_all.27.blocks_ref = bf16[16,24,128]{2,1,0:T(8,128)(2,1)S(1)} all-to-all(bf16[16,24,128]{2,1,0:T(8,128)(2,1)S(1)} %shift_blocks.1), channel_id=1, replica_groups=mesh['groups'=2,'pair'=16] {'pair'}, dimensions={0} | all-to-all | bytes 196608 | tf_op jit(solution)/shard_map/all_to_all | solution.py:28
  48.3 0.0 copy-done.1
  48.3 0.0 copy-start.4
  48.4 0.0 copy-start.2
  48.4 4.6 %potential_held.1 = (bf16[16,32,512]{2,1,0:T(8,128)(2,1)}, bf16[32,1024]{1,0:T(8,128)(2,1)S(1)}) custom-call(bf16[16,24,128]{2,1,0:T(8,128)(2,1)S(1)} %all_to_all.27.blocks_ref, bf16[1024,16384]{1,0:T(8,128)(2,1)S(1)} %copy-done.1), custom_call_target="tpu_custom_call" | custom-call | tf_op jit(solution)/shard_map/potential_held/pallas_call | solution.py:203
  53.0 7.9 %potential_streamed.1 = bf16[16,32,512]{2,1,0:T(8,128)(2,1)S(1)} custom-call(bf16[32,1024]{1,0:T(8,128)(2,1)S(1)} %get-tuple-element.8.shift_ref, bf16[1024,16384]{1,0:T(8,128)(2,1)} %chol_ref.5), custom_call_target="tpu_custom_call" | custom-call | flops 536870912 | bytes 16777216 | tf_op jit(solution)/shard_map/potential_streamed/pallas_call | solution.py:239
  60.8 17.6 %all_to_all.28.late_ref = bf16[16,32,512]{2,1,0:T(8,128)(2,1)S(1)} all-to-all(bf16[16,32,512]{2,1,0:T(8,128)(2,1)S(1)} %potential_streamed.1), channel_id=1, replica_groups=mesh['groups'=2,'pair'=16] {'pair'}, dimensions={0} | all-to-all | bytes 1048576 | tf_op jit(solution)/shard_map/all_to_all | solution.py:28
  78.4 4.4 %all-to-all-start.3 = ((bf16[16,32,512]{2,1,0:T(8,128)(2,1)}), bf16[16,32,512]{2,1,0:T(8,128)(2,1)S(1)}, u32[]{:S(2)}, u32[]{:S(2)}) async-start(bf16[16,32,512]{2,1,0:T(8,128)(2,1)} %get-tuple-element.7), calls=%async_computation.3 | async-start | bytes 1048576 | tf_op jit(solution)/shard_map/all_to_all | solution.py:28
  82.8 0.0 copy-done.4
  82.8 1.7 %collective-permute-start = (bf16[2,512,128]{2,1,0:T(8,128)(2,1)S(1)}, bf16[2,512,128]{2,1,0:T(8,128)(2,1)S(1)}, u32[]{:S(2)}, u32[]{:S(2)}) collective-permute-start(bf16[2,512,128]{2,1,0:T(8,128)(2,1)S(1)} %copy-done.4), channel_id=1, source_target_pairs={{0,1},{1,2},{2,3},{3,4},{4,5},{5,6},{6,7},{7,8},{8,9},{9,10},{10,1... | collective-permute-start | bytes 786440 | tf_op jit(solution)/shard_map/ppermute | solution.py:35
  84.5 0.0 collective-permute-start.1
  84.5 6.1 %collective-permute-done.low_ref = bf16[2,512,128]{2,1,0:T(8,128)(2,1)S(1)} collective-permute-done((bf16[2,512,128]{2,1,0:T(8,128)(2,1)S(1)}, bf16[2,512,128]{2,1,0:T(8,128)(2,1)S(1)}, u32[]{:S(2)}, u32[]{:S(2)}) %collective-permute-start) | collective-permute-done | bytes 262176 | tf_op jit(solution)/shard_map/ppermute | solution.py:35
  90.7 1.7 %collective-permute-done.1.high_ref = bf16[2,512,128]{2,1,0:T(8,128)(2,1)S(1)} collective-permute-done((bf16[2,512,128]{2,1,0:T(8,128)(2,1)S(1)}, bf16[2,512,128]{2,1,0:T(8,128)(2,1)S(1)}, u32[]{:S(2)}, u32[]{:S(2)}) %collective-permute-start.1) | collective-permute-done | bytes 262176 | tf_op jit(solution)/shard_map/ppermute | solution.py:35
  92.3 7.3 %all-to-all-done.3.early_ref = bf16[16,32,512]{2,1,0:T(8,128)(2,1)S(1)} async-done(((bf16[16,32,512]{2,1,0:T(8,128)(2,1)}), bf16[16,32,512]{2,1,0:T(8,128)(2,1)S(1)}, u32[]{:S(2)}, u32[]{:S(2)}) %all-to-all-start.3) | async-done | bytes 524320 | tf_op jit(solution)/shard_map/all_to_all | solution.py:28
  99.6 0.0 copy-done.2
  99.6 4.7 %propagate.1 = bf16[2,512,128]{2,1,0:T(8,128)(2,1)} custom-call(bf16[16,32,512]{2,1,0:T(8,128)(2,1)S(1)} %all-to-all-done.3.early_ref, bf16[16,32,512]{2,1,0:T(8,128)(2,1)S(1)} %all_to_all.28.late_ref, bf16[512,512]{1,0:T(8,128)(2,1)S(1)} %copy-done.2, bf16[2,512,128]{2,1,0:T(8,128)(2,1)S(1)} %collective-permute-done.low_ref, ...), custom_call_target="tpu_custom_call" | custom-call | tf_op jit(solution)/shard_map/propagate/pallas_call | solution.py:285
  (1 shorter events, 0.0 us)
Async XLA Ops:
  0.0 18.1 %copy-start = (bf16[1024,16384]{1,0:T(8,128)(2,1)S(1)}, bf16[1024,16384]{1,0:T(8,128)(2,1)}, u32[]{:S(2)}) copy-start(bf16[1024,16384]{1,0:T(8,128)(2,1)} %chol_ref.5) | copy-start | bytes 100663296
  0.0 1.1 %copy-start.3 = (bf16[2,512,128]{2,1,0:T(8,128)(2,1)S(1)}, bf16[2,512,128]{2,1,0:T(8,128)(2,1)}, u32[]{:S(2)}) copy-start(bf16[2,512,128]{2,1,0:T(8,128)(2,1)} %own_ref.1) | copy-start | bytes 786436
  1.1 17.0 %copy-start.5 = (bf16[512,128]{1,0:T(8,128)(2,1)S(1)}, bf16[512,128]{1,0:T(8,128)(2,1)}, u32[]{:S(2)}) copy-start(bf16[512,128]{1,0:T(8,128)(2,1)} %trial_ref.1) | copy-start | bytes 393220
  1.1 36.3 %copy-start.6 = (s32[2]{0:T(128)S(1)}, s32[2]{0:T(128)}, u32[]{:S(2)}) copy-start(s32[2]{0:T(128)} %from_ref.3) | copy-start | bytes 28
  1.1 36.3 %copy-start.7 = (s32[2]{0:T(128)S(1)}, s32[2]{0:T(128)}, u32[]{:S(2)}) copy-start(s32[2]{0:T(128)} %slot_ref.3) | copy-start | bytes 28
  1.2 36.2 %copy-start.8 = (f32[2,1024]{1,0:T(2,128)S(1)}, f32[2,1024]{1,0:T(2,128)}, u32[]{:S(2)}) copy-start(f32[2,1024]{1,0:T(2,128)} %fields_ref.1) | copy-start | bytes 24580
  37.4 11.0 %copy-start.1 = (bf16[1024,16384]{1,0:T(8,128)(2,1)S(1)}, bf16[1024,16384]{1,0:T(8,128)(2,1)}, u32[]{:S(2)}) copy-start(bf16[1024,16384]{1,0:T(8,128)(2,1)} %chol_ref.5) | copy-start | bytes 100663296
  48.3 34.5 %copy-start.4 = (bf16[2,512,128]{2,1,0:T(8,128)(2,1)S(1)}, bf16[2,512,128]{2,1,0:T(8,128)(2,1)}, u32[]{:S(2)}) copy-start(bf16[2,512,128]{2,1,0:T(8,128)(2,1)} %own_ref.1) | copy-start | bytes 786436
  48.4 51.3 %copy-start.2 = (bf16[512,512]{1,0:T(8,128)(2,1)S(1)}, bf16[512,512]{1,0:T(8,128)(2,1)}, u32[]{:S(2)}) copy-start(bf16[512,512]{1,0:T(8,128)(2,1)} %one_ref.1) | copy-start | bytes 1572868
  78.4 21.2 %all-to-all-start.3 = ((bf16[16,32,512]{2,1,0:T(8,128)(2,1)}), bf16[16,32,512]{2,1,0:T(8,128)(2,1)S(1)}, u32[]{:S(2)}, u32[]{:S(2)}) async-start(bf16[16,32,512]{2,1,0:T(8,128)(2,1)} %get-tuple-element.7), calls=%async_computation.3 | async-start | bytes 1048576 | tf_op jit(solution)/shard_map/all_to_all | solution.py:28
  82.8 7.8 %collective-permute-start = (bf16[2,512,128]{2,1,0:T(8,128)(2,1)S(1)}, bf16[2,512,128]{2,1,0:T(8,128)(2,1)S(1)}, u32[]{:S(2)}, u32[]{:S(2)}) collective-permute-start(bf16[2,512,128]{2,1,0:T(8,128)(2,1)S(1)} %copy-done.4), channel_id=1, source_target_pairs={{0,1},{1,2},{2,3},{3,4},{4,5},{5,6},{6,7},{7,8},{8,9},{9,10},{10,1... | collective-permute-start | bytes 786440 | tf_op jit(solution)/shard_map/ppermute | solution.py:35
  84.5 7.8 %collective-permute-start.1 = (bf16[2,512,128]{2,1,0:T(8,128)(2,1)S(1)}, bf16[2,512,128]{2,1,0:T(8,128)(2,1)S(1)}, u32[]{:S(2)}, u32[]{:S(2)}) collective-permute-start(bf16[2,512,128]{2,1,0:T(8,128)(2,1)S(1)} %copy-done.4), channel_id=1, source_target_pairs={{1,0},{2,1},{3,2},{4,3},{5,4},{6,5},{7,6},{8,7},{9,8},{10,9},{11,1... | collective-permute-start | bytes 786440 | tf_op jit(solution)/shard_map/ppermute | solution.py:35

commit v3 on v2

--- a/solution.py
+++ b/solution.py
@@ -178,15 +178,15 @@
             ]
 
 
-def potential_held(blocks, chol, w_local, orbitals, rows):
+def potential(blocks, chol, w_local, orbitals):
     count, height, _ = blocks.shape
-    vectors = chol.shape[0]
+    vectors, pairs = chol.shape
+    rows = pairs // orbitals
     walkers = count * w_local
     each = vectors // LANES
 
-    def body(blocks_ref, chol_ref, out_ref, picked_ref, wide_ref, shift_ref, acc_ref):
+    def body(blocks_ref, chol_ref, out_ref, wide_ref, shift_ref, acc_ref):
         shift = parents_shift(blocks_ref, wide_ref, shift_ref, w_local, each)
-        picked_ref[...] = shift
 
         @pl.loop(0, rows // GROUP)
         def _(step):
@@ -202,98 +202,60 @@
 
     return pl.pallas_call(
         body,
-        out_shape=(
-            jax.ShapeDtypeStruct((count, w_local * rows, orbitals), jnp.bfloat16),
-            jax.ShapeDtypeStruct((walkers, vectors), jnp.bfloat16),
-        ),
+        out_shape=jax.ShapeDtypeStruct((count, w_local * rows, orbitals), jnp.bfloat16),
         in_specs=[VMEM, VMEM],
-        out_specs=(VMEM, VMEM),
+        out_specs=VMEM,
         scratch_shapes=[
             pltpu.VMEM((count * height, LANES), jnp.float32),
             pltpu.VMEM((walkers, vectors), jnp.bfloat16),
             pltpu.VMEM((orbitals // LANES, walkers * GROUP, LANES), jnp.float32),
         ],
         compiler_params=params(12),
-        name="potential_held",
+        name="potential",
     )(blocks, chol)
 
 
-def potential_streamed(shift, chol, w_local, orbitals, first, rows):
-    walkers, vectors = shift.shape
-    count = walkers // w_local
-    per = 4
-
-    def body(shift_ref, chol_ref, out_ref, acc_ref):
-        step = pl.program_id(0)
-        half = lax.rem(step, GROUP // per)
-        part = sqrt_tau * jnp.dot(shift_ref[...], chol_ref[...], preferred_element_type=jnp.float32)
-        for inner in range(per):
-            spread(
-                part[:, inner * orbitals : (inner + 1) * orbitals], acc_ref, half * per + inner, count, w_local, GROUP
-            )
-
-        @pl.when(half == GROUP // per - 1)
-        def _():
-            settle(acc_ref, out_ref, (step * per) // GROUP * GROUP, count, w_local, GROUP, rows)
-
-    return pl.pallas_call(
-        body,
-        out_shape=jax.ShapeDtypeStruct((count, w_local * rows, orbitals), jnp.bfloat16),
-        grid=(rows // per,),
-        in_specs=[
-            pl.BlockSpec((walkers, vectors), lambda i: (0, 0)),
-            pl.BlockSpec((vectors, per * orbitals), lambda i: (0, first // per + i)),
-        ],
-        out_specs=pl.BlockSpec((count, w_local * rows, orbitals), lambda i: (0, 0, 0)),
-        scratch_shapes=[pltpu.VMEM((orbitals // LANES, walkers * GROUP, LANES), jnp.float32)],
-        compiler_params=params(20),
-        cost_estimate=pl.CostEstimate(
-            flops=2 * walkers * vectors * rows * orbitals, bytes_accessed=2 * vectors * rows * orbitals, transcendentals=0
-        ),
-        name="potential_streamed",
-    )(shift, pltpu.with_memory_space_constraint(chol, pltpu.HBM))
-
-
-def propagate(early, late, one_body, low, own, high, src_shift, src_slot):
-    w_local, orbitals, occupied = own.shape
-    count = early.shape[0]
+def propagate(blocks, one_body, low, own, high, src_shift, src_slot):
+    w_local, orbitals, _ = own.shape
+    count = blocks.shape[0]
     rows = orbitals // count
-    cut = early.shape[1] // w_local
-
-    def body(early_ref, late_ref, one_ref, low_ref, own_ref, high_ref, from_ref, slot_ref, out_ref, start_ref, mat_ref):
-        one = one_ref[...].astype(jnp.float32).reshape(count, rows, orbitals)
+
+    def body(blocks_ref, one_ref, low_ref, own_ref, high_ref, from_ref, slot_ref, out_ref, term_ref, mat_ref):
         for walker in range(w_local):
             for offset, source in ((-1, low_ref), (0, own_ref), (1, high_ref)):
 
                 @pl.when(from_ref[walker] == offset)
                 def _():
-                    start_ref[...] = source[slot_ref[walker]]
-
-            for ref, low_row, high_row in ((early_ref, 0, cut), (late_ref, cut, rows)):
-                tall = high_row - low_row
-                mine = ref[:, walker * tall : (walker + 1) * tall, :].astype(jnp.float32)
-                mat_ref[:, low_row:high_row, :] = (mine + one[:, low_row:high_row, :]).astype(jnp.bfloat16)
-            amat = mat_ref[...].reshape(orbitals, orbitals)
-            term = start_ref[...]
-            total = term.astype(jnp.float32)
-            for order in range(1, TERMS):
-                product = jnp.dot(amat, term, preferred_element_type=jnp.float32) / order
-                total = total + product
-                term = product.astype(jnp.bfloat16)
-            out_ref[walker] = total.astype(jnp.bfloat16)
+                    term_ref[walker] = source[slot_ref[walker]]
+
+        one = one_ref[...].astype(jnp.float32).reshape(count, rows, orbitals)
+        for walker in range(w_local):
+            mine = blocks_ref[:, walker * rows : (walker + 1) * rows, :].astype(jnp.float32)
+            mat_ref[walker] = (mine + one).reshape(orbitals, orbitals).astype(jnp.bfloat16)
+        terms = [term_ref[walker] for walker in range(w_local)]
+        totals = [term.astype(jnp.float32) for term in terms]
+        for order in range(1, TERMS):
+            products = [
+                jnp.dot(mat_ref[walker], terms[walker], preferred_element_type=jnp.float32) / order
+                for walker in range(w_local)
+            ]
+            totals = [total + product for total, product in zip(totals, products)]
+            terms = [product.astype(jnp.bfloat16) for product in products]
+        for walker in range(w_local):
+            out_ref[walker] = totals[walker].astype(jnp.bfloat16)
 
     return pl.pallas_call(
         body,
         out_shape=jax.ShapeDtypeStruct(own.shape, jnp.bfloat16),
-        in_specs=[VMEM, VMEM, VMEM, VMEM, VMEM, VMEM, SMEM, SMEM],
+        in_specs=[VMEM, VMEM, VMEM, VMEM, VMEM, SMEM, SMEM],
         out_specs=VMEM,
         scratch_shapes=[
-            pltpu.VMEM((orbitals, occupied), jnp.bfloat16),
-            pltpu.VMEM((count, rows, orbitals), jnp.bfloat16),
+            pltpu.VMEM(own.shape, jnp.bfloat16),
+            pltpu.VMEM((w_local, orbitals, orbitals), jnp.bfloat16),
         ],
         compiler_params=params(16),
         name="propagate",
-    )(early, late, one_body, low, own, high, src_shift, src_slot)
+    )(blocks, one_body, low, own, high, src_shift, src_slot)
 
 
 def plain(chol, walkers, trial, one_body, fields, src_shift, src_slot):
@@ -333,18 +295,15 @@
 def held(chol, walkers, trial, one_body, fields, src_shift, src_slot):
     count = lax.axis_size("pair")
     w_local, orbitals, _ = walkers.shape
-    rows = chol.shape[1] // orbitals
-    cut = rows // 2
 
     low, high = neighbours(walkers)
-    moved = exchange(pack(walkers, count))
-    partials = exchange(bias_partial(moved, trial, chol, w_local))
+    sent = pack(walkers, count)
+    moved = exchange(sent)
+    partial = bias_partial(moved, trial, chol, w_local)
+    partials = exchange(partial)
     blocks = exchange(shift_blocks(partials, fields, src_shift, src_slot))
-    early, shift = potential_held(blocks, chol, w_local, orbitals, cut)
-    early = exchange(early)
-    late = potential_streamed(shift, chol, w_local, orbitals, cut, rows - cut)
-    late = exchange(late)
-    return propagate(early, late, one_body, low, walkers, high, src_shift, src_slot)
+    received = exchange(potential(blocks, chol, w_local, orbitals))
+    return propagate(received, one_body, low, walkers, high, src_shift, src_slot)
 
 
 def shards(chol, walkers, *rest):

time: 105 us -> 91.7 us (0.87)
  blocking collectives: 54.1 us -> 36.5 us
  waiting for transfers between devices: 15.1 us -> 24.3 us
  Pallas kernels: 27.9 us -> 22.2 us
    all_to_all x4 -> x3, blocking collectives: 54.1 us -> 36.5 us  [exchange(): lax.all_to_all(blocks, 'pair', split_axis=0, concat_axis=0, tiled=True)]
    all_to_all x1, waiting for transfers between devices: 7.32 us -> 13.1 us  [exchange(): lax.all_to_all(blocks, 'pair', split_axis=0, concat_axis=0, tiled=True)]
    pallas_call x2 -> x1, Pallas kernels: 12.5 us -> 8.36 us  [potential(): pl.pallas_call(body, out_shape=jax.ShapeDtypeStruct((count, w_local * row...]
    ppermute x1, waiting for transfers between devices: 1.66 us -> 3.66 us  [neighbours(): lax.ppermute(block, 'pair', backward)]
    pallas_call x1, Pallas kernels: 4.72 us -> 3.15 us  [propagate(): pl.pallas_call(body, out_shape=jax.ShapeDtypeStruct(own.shape, jnp.bfloat...]
    ppermute x1, waiting for transfers between devices: 6.14 us -> 7.6 us  [neighbours(): lax.ppermute(block, 'pair', forward)]
where the time goes in v3:
time: 91.7 us; the launch traced here: 90.5 us
  blocking collectives  36.5 us (40%)
  waiting for transfers between devices  24.3 us (26%)
  Pallas kernels  22.2 us (24%)
  starting transfers between devices  6.22 us (7%)
  local copies, waits for them, and re-layouts  1.14 us (1%)
    all_to_all x3, blocking collectives, exchange(): lax.all_to_all(blocks, 'pair', split_axis=0, concat_axis=0, tiled=True)  36.5 us
    all_to_all x1, waiting for transfers between devices, exchange(): lax.all_to_all(blocks, 'pair', split_axis=0, concat_axis=0, tiled=True)  13.1 us
    pallas_call x1, Pallas kernels, bias_partial(): pl.pallas_call(body, out_shape=jax.ShapeDtypeStruct((count, w_local * str...  10.1 us
    pallas_call x1, Pallas kernels, potential(): pl.pallas_call(body, out_shape=jax.ShapeDtypeStruct((count, w_local * row...  8.36 us
    ppermute x1, waiting for transfers between devices, neighbours(): lax.ppermute(block, 'pair', forward)  7.6 us
    all_to_all x1, starting transfers between devices, exchange(): lax.all_to_all(blocks, 'pair', split_axis=0, concat_axis=0, tiled=True)  4.53 us
    ppermute x1, waiting for transfers between devices, neighbours(): lax.ppermute(block, 'pair', backward)  3.66 us
    pallas_call x1, Pallas kernels, propagate(): pl.pallas_call(body, out_shape=jax.ShapeDtypeStruct(own.shape, jnp.bfloat...  3.15 us
  transfers between devices with their start and end apart: 3, of which 3 were waited for; matrix products, arithmetic and copies ran while one was open for 0% of the time, Pallas kernels for 0%

profile of v3, /device:TPU:1, one launch (start us, length us, event | category | flops | bytes accessed | tf_op | source)
XLA Modules:
  0.0 90.5 jit_solution(16518989096138509700)
XLA Ops:
  0.0 0.0 copy-start
  0.0 0.0 copy-start.3
  0.0 1.1 %copy-done.3 = bf16[2,512,128]{2,1,0:T(8,128)(2,1)S(1)} copy-done((bf16[2,512,128]{2,1,0:T(8,128)(2,1)S(1)}, bf16[2,512,128]{2,1,0:T(8,128)(2,1)}, u32[]{:S(2)}) %copy-start.3) | copy-done | bytes 262168
  1.1 0.0 copy-start.5
  1.1 0.0 copy-start.6
  1.1 0.0 copy-start.7
  1.2 0.0 copy-start.8
  1.2 16.9 %all_to_all.20.moved_ref = bf16[16,64,128]{2,1,0:T(8,128)(2,1)S(1)} all-to-all(bf16[16,64,128]{2,1,0:T(8,128)(2,1)S(1)} %pack.1), channel_id=1, replica_groups=mesh['groups'=2,'pair'=16] {'pair'}, dimensions={0} | all-to-all | bytes 524288 | tf_op jit(solution)/shard_map/all_to_all | solution.py:28
  18.1 0.0 copy-done
  18.1 0.0 copy-done.5
  18.1 10.1 %bias_partial.1 = bf16[16,16,128]{2,1,0:T(8,128)(2,1)S(1)} custom-call(bf16[16,64,128]{2,1,0:T(8,128)(2,1)S(1)} %all_to_all.20.moved_ref, bf16[512,128]{1,0:T(8,128)(2,1)S(1)} %copy-done.5, bf16[1024,16384]{1,0:T(8,128)(2,1)S(1)} %copy-done), custom_call_target="tpu_custom_call" | custom-call | tf_op jit(solution)/shard_map/bias_partial/pallas_call | solution.py:93
  28.2 9.2 %all_to_all.21.partials_ref = bf16[16,16,128]{2,1,0:T(8,128)(2,1)S(1)} all-to-all(bf16[16,16,128]{2,1,0:T(8,128)(2,1)S(1)} %bias_partial.1), channel_id=1, replica_groups=mesh['groups'=2,'pair'=16] {'pair'}, dimensions={0} | all-to-all | bytes 131072 | tf_op jit(solution)/shard_map/all_to_all | solution.py:28
  37.4 0.0 copy-done.6
  37.4 0.0 copy-done.7
  37.4 0.0 copy-done.8
  37.4 0.0 copy-start.1
  37.4 0.6 shift_blocks.1
  38.0 0.0 copy-start.4
  38.0 0.0 copy-start.2
  38.0 10.4 %all_to_all.22.blocks_ref = bf16[16,24,128]{2,1,0:T(8,128)(2,1)S(1)} all-to-all(bf16[16,24,128]{2,1,0:T(8,128)(2,1)S(1)} %shift_blocks.1), channel_id=1, replica_groups=mesh['groups'=2,'pair'=16] {'pair'}, dimensions={0} | all-to-all | bytes 196608 | tf_op jit(solution)/shard_map/all_to_all | solution.py:28
  48.4 0.0 copy-done.1
  48.4 8.4 %potential.1 = bf16[16,64,512]{2,1,0:T(8,128)(2,1)} custom-call(bf16[16,24,128]{2,1,0:T(8,128)(2,1)S(1)} %all_to_all.22.blocks_ref, bf16[1024,16384]{1,0:T(8,128)(2,1)S(1)} %copy-done.1), custom_call_target="tpu_custom_call" | custom-call | tf_op jit(solution)/shard_map/potential/pallas_call | solution.py:203
  56.7 4.5 %all-to-all-start.3 = ((bf16[16,64,512]{2,1,0:T(8,128)(2,1)}), bf16[16,64,512]{2,1,0:T(8,128)(2,1)S(1)}, u32[]{:S(2)}, u32[]{:S(2)}) async-start(bf16[16,64,512]{2,1,0:T(8,128)(2,1)} %potential.1), calls=%async_computation.3 | async-start | bytes 2097152 | tf_op jit(solution)/shard_map/all_to_all | solution.py:28
  61.3 0.0 copy-done.4
  61.3 1.7 %collective-permute-start = (bf16[2,512,128]{2,1,0:T(8,128)(2,1)S(1)}, bf16[2,512,128]{2,1,0:T(8,128)(2,1)S(1)}, u32[]{:S(2)}, u32[]{:S(2)}) collective-permute-start(bf16[2,512,128]{2,1,0:T(8,128)(2,1)S(1)} %copy-done.4), channel_id=1, source_target_pairs={{0,1},{1,2},{2,3},{3,4},{4,5},{5,6},{6,7},{7,8},{8,9},{9,10},{10,1... | collective-permute-start | bytes 786440 | tf_op jit(solution)/shard_map/ppermute | solution.py:35
  63.0 0.0 collective-permute-start.1
  63.0 7.6 %collective-permute-done.low_ref = bf16[2,512,128]{2,1,0:T(8,128)(2,1)S(1)} collective-permute-done((bf16[2,512,128]{2,1,0:T(8,128)(2,1)S(1)}, bf16[2,512,128]{2,1,0:T(8,128)(2,1)S(1)}, u32[]{:S(2)}, u32[]{:S(2)}) %collective-permute-start) | collective-permute-done | bytes 262176 | tf_op jit(solution)/shard_map/ppermute | solution.py:35
  70.6 3.7 %collective-permute-done.1.high_ref = bf16[2,512,128]{2,1,0:T(8,128)(2,1)S(1)} collective-permute-done((bf16[2,512,128]{2,1,0:T(8,128)(2,1)S(1)}, bf16[2,512,128]{2,1,0:T(8,128)(2,1)S(1)}, u32[]{:S(2)}, u32[]{:S(2)}) %collective-permute-start.1) | collective-permute-done | bytes 262176 | tf_op jit(solution)/shard_map/ppermute | solution.py:35
  74.2 13.1 %all-to-all-done.3.blocks_ref = bf16[16,64,512]{2,1,0:T(8,128)(2,1)S(1)} async-done(((bf16[16,64,512]{2,1,0:T(8,128)(2,1)}), bf16[16,64,512]{2,1,0:T(8,128)(2,1)S(1)}, u32[]{:S(2)}, u32[]{:S(2)}) %all-to-all-start.3) | async-done | bytes 1048608 | tf_op jit(solution)/shard_map/all_to_all | solution.py:28
  87.3 0.0 copy-done.2
  87.3 3.1 %propagate.1 = bf16[2,512,128]{2,1,0:T(8,128)(2,1)} custom-call(bf16[16,64,512]{2,1,0:T(8,128)(2,1)S(1)} %all-to-all-done.3.blocks_ref, bf16[512,512]{1,0:T(8,128)(2,1)S(1)} %copy-done.2, bf16[2,512,128]{2,1,0:T(8,128)(2,1)S(1)} %collective-permute-done.low_ref, bf16[2,512,128]{2,1,0:T(8,128)(2,1)S(1)} %copy-done.4, ...), custom_call_target="tpu_custom_call" | custom-call | tf_op jit(solution)/shard_map/propagate/pallas_call | solution.py:247
  (1 shorter events, 0.0 us)
Async XLA Ops:
  0.0 18.1 %copy-start = (bf16[1024,16384]{1,0:T(8,128)(2,1)S(1)}, bf16[1024,16384]{1,0:T(8,128)(2,1)}, u32[]{:S(2)}) copy-start(bf16[1024,16384]{1,0:T(8,128)(2,1)} %chol_ref.3) | copy-start | bytes 100663296
  0.0 1.1 %copy-start.3 = (bf16[2,512,128]{2,1,0:T(8,128)(2,1)S(1)}, bf16[2,512,128]{2,1,0:T(8,128)(2,1)}, u32[]{:S(2)}) copy-start(bf16[2,512,128]{2,1,0:T(8,128)(2,1)} %own_ref.1) | copy-start | bytes 786436
  1.1 17.0 %copy-start.5 = (bf16[512,128]{1,0:T(8,128)(2,1)S(1)}, bf16[512,128]{1,0:T(8,128)(2,1)}, u32[]{:S(2)}) copy-start(bf16[512,128]{1,0:T(8,128)(2,1)} %trial_ref.1) | copy-start | bytes 393220
  1.1 36.3 %copy-start.6 = (s32[2]{0:T(128)S(1)}, s32[2]{0:T(128)}, u32[]{:S(2)}) copy-start(s32[2]{0:T(128)} %from_ref.3) | copy-start | bytes 28
  1.1 36.3 %copy-start.7 = (s32[2]{0:T(128)S(1)}, s32[2]{0:T(128)}, u32[]{:S(2)}) copy-start(s32[2]{0:T(128)} %slot_ref.3) | copy-start | bytes 28
  1.2 36.2 %copy-start.8 = (f32[2,1024]{1,0:T(2,128)S(1)}, f32[2,1024]{1,0:T(2,128)}, u32[]{:S(2)}) copy-start(f32[2,1024]{1,0:T(2,128)} %fields_ref.1) | copy-start | bytes 24580
  37.4 11.0 %copy-start.1 = (bf16[1024,16384]{1,0:T(8,128)(2,1)S(1)}, bf16[1024,16384]{1,0:T(8,128)(2,1)}, u32[]{:S(2)}) copy-start(bf16[1024,16384]{1,0:T(8,128)(2,1)} %chol_ref.3) | copy-start | bytes 100663296
  38.0 23.3 %copy-start.4 = (bf16[2,512,128]{2,1,0:T(8,128)(2,1)S(1)}, bf16[2,512,128]{2,1,0:T(8,128)(2,1)}, u32[]{:S(2)}) copy-start(bf16[2,512,128]{2,1,0:T(8,128)(2,1)} %own_ref.1) | copy-start | bytes 786436
  38.0 49.3 %copy-start.2 = (bf16[512,512]{1,0:T(8,128)(2,1)S(1)}, bf16[512,512]{1,0:T(8,128)(2,1)}, u32[]{:S(2)}) copy-start(bf16[512,512]{1,0:T(8,128)(2,1)} %one_ref.1) | copy-start | bytes 1572868
  56.7 30.6 %all-to-all-start.3 = ((bf16[16,64,512]{2,1,0:T(8,128)(2,1)}), bf16[16,64,512]{2,1,0:T(8,128)(2,1)S(1)}, u32[]{:S(2)}, u32[]{:S(2)}) async-start(bf16[16,64,512]{2,1,0:T(8,128)(2,1)} %potential.1), calls=%async_computation.3 | async-start | bytes 2097152 | tf_op jit(solution)/shard_map/all_to_all | solution.py:28
  61.3 9.3 %collective-permute-start = (bf16[2,512,128]{2,1,0:T(8,128)(2,1)S(1)}, bf16[2,512,128]{2,1,0:T(8,128)(2,1)S(1)}, u32[]{:S(2)}, u32[]{:S(2)}) collective-permute-start(bf16[2,512,128]{2,1,0:T(8,128)(2,1)S(1)} %copy-done.4), channel_id=1, source_target_pairs={{0,1},{1,2},{2,3},{3,4},{4,5},{5,6},{6,7},{7,8},{8,9},{9,10},{10,1... | collective-permute-start | bytes 786440 | tf_op jit(solution)/shard_map/ppermute | solution.py:35
  63.0 11.3 %collective-permute-start.1 = (bf16[2,512,128]{2,1,0:T(8,128)(2,1)S(1)}, bf16[2,512,128]{2,1,0:T(8,128)(2,1)S(1)}, u32[]{:S(2)}, u32[]{:S(2)}) collective-permute-start(bf16[2,512,128]{2,1,0:T(8,128)(2,1)S(1)} %copy-done.4), channel_id=1, source_target_pairs={{1,0},{2,1},{3,2},{4,3},{5,4},{6,5},{7,6},{8,7},{9,8},{10,9},{11,1... | collective-permute-start | bytes 786440 | tf_op jit(solution)/shard_map/ppermute | solution.py:35

commit v4 on v3

--- a/solution.py
+++ b/solution.py
@@ -61,7 +61,7 @@
     rows = pairs // orbitals
     walkers = count * w_local
     strips = vectors // LANES
-    steps = 4
+    steps = 2
     width = pairs // steps
 
     def body(moved_ref, trial_ref, chol_ref, out_ref, wide_ref, lhs_ref, green_ref, acc_ref, flat_ref):
@@ -169,50 +169,46 @@
             ]
 
 
-def settle(acc_ref, out_ref, start, count, w_local, group, rows):
-    for lane in range(acc_ref.shape[0]):
-        done = acc_ref[lane].reshape(count, w_local, group, LANES).astype(jnp.bfloat16)
-        for slot in range(w_local):
-            out_ref[:, pl.ds(pl.multiple_of(slot * rows + start, group), group), pl.ds(lane * LANES, LANES)] = done[
-                :, slot
-            ]
-
-
 def potential(blocks, chol, w_local, orbitals):
     count, height, _ = blocks.shape
     vectors, pairs = chol.shape
     rows = pairs // orbitals
     walkers = count * w_local
     each = vectors // LANES
-
-    def body(blocks_ref, chol_ref, out_ref, wide_ref, shift_ref, acc_ref):
-        shift = parents_shift(blocks_ref, wide_ref, shift_ref, w_local, each)
-
-        @pl.loop(0, rows // GROUP)
-        def _(step):
-            for pair in range(0, GROUP, 4):
-                start = (step * GROUP + pair) * orbitals
-                cols = pl.ds(pl.multiple_of(start, 4 * orbitals), 4 * orbitals)
-                part = sqrt_tau * jnp.dot(shift, chol_ref[:, cols], preferred_element_type=jnp.float32)
-                for inner in range(4):
-                    spread(
-                        part[:, inner * orbitals : (inner + 1) * orbitals], acc_ref, pair + inner, count, w_local, GROUP
-                    )
-            settle(acc_ref, out_ref, step * GROUP, count, w_local, GROUP, rows)
-
-    return pl.pallas_call(
-        body,
-        out_shape=jax.ShapeDtypeStruct((count, w_local * rows, orbitals), jnp.bfloat16),
+    width = GROUP * orbitals
+
+    def body(blocks_ref, chol_ref, out_ref, wide_ref, shift_ref, picked_ref, acc_ref):
+        step = pl.program_id(0)
+
+        @pl.when(step == 0)
+        def _():
+            picked_ref[...] = parents_shift(blocks_ref, wide_ref, shift_ref, w_local, each)
+
+        cols = pl.ds(pl.multiple_of(step * width, width), width)
+        part = sqrt_tau * jnp.dot(picked_ref[...], chol_ref[:, cols], preferred_element_type=jnp.float32)
+        for row in range(GROUP):
+            spread(part[:, row * orbitals : (row + 1) * orbitals], acc_ref, row, count, w_local, GROUP)
+        for lane in range(orbitals // LANES):
+            out_ref[:, :, :, lane * LANES : (lane + 1) * LANES] = (
+                acc_ref[lane].reshape(count, w_local, GROUP, LANES).astype(jnp.bfloat16)
+            )
+
+    out = pl.pallas_call(
+        body,
+        out_shape=jax.ShapeDtypeStruct((count, w_local, rows, orbitals), jnp.bfloat16),
+        grid=(rows // GROUP,),
         in_specs=[VMEM, VMEM],
-        out_specs=VMEM,
+        out_specs=pl.BlockSpec((count, w_local, GROUP, orbitals), lambda i: (0, 0, i, 0)),
         scratch_shapes=[
             pltpu.VMEM((count * height, LANES), jnp.float32),
+            pltpu.VMEM((walkers, vectors), jnp.bfloat16),
             pltpu.VMEM((walkers, vectors), jnp.bfloat16),
             pltpu.VMEM((orbitals // LANES, walkers * GROUP, LANES), jnp.float32),
         ],
         compiler_params=params(12),
         name="potential",
     )(blocks, chol)
+    return out.reshape(count, w_local * rows, orbitals)
 
 
 def propagate(blocks, one_body, low, own, high, src_shift, src_slot):
@@ -220,18 +216,23 @@
     count = blocks.shape[0]
     rows = orbitals // count
 
-    def body(blocks_ref, one_ref, low_ref, own_ref, high_ref, from_ref, slot_ref, out_ref, term_ref, mat_ref):
+    def body(blocks_ref, one_ref, low_ref, own_ref, high_ref, from_ref, slot_ref, out_ref, term_ref, mat_ref, sems):
+        def fetch(source, walker):
+            return pltpu.make_async_copy(source.at[slot_ref[walker]], term_ref.at[walker], sems.at[walker])
+
         for walker in range(w_local):
             for offset, source in ((-1, low_ref), (0, own_ref), (1, high_ref)):
 
                 @pl.when(from_ref[walker] == offset)
                 def _():
-                    term_ref[walker] = source[slot_ref[walker]]
+                    fetch(source, walker).start()
 
         one = one_ref[...].astype(jnp.float32).reshape(count, rows, orbitals)
         for walker in range(w_local):
             mine = blocks_ref[:, walker * rows : (walker + 1) * rows, :].astype(jnp.float32)
             mat_ref[walker] = (mine + one).reshape(orbitals, orbitals).astype(jnp.bfloat16)
+        for walker in range(w_local):
+            fetch(own_ref, walker).wait()
         terms = [term_ref[walker] for walker in range(w_local)]
         totals = [term.astype(jnp.float32) for term in terms]
         for order in range(1, TERMS):
@@ -247,11 +248,12 @@
     return pl.pallas_call(
         body,
         out_shape=jax.ShapeDtypeStruct(own.shape, jnp.bfloat16),
-        in_specs=[VMEM, VMEM, VMEM, VMEM, VMEM, SMEM, SMEM],
+        in_specs=[VMEM, VMEM, ANY, ANY, ANY, SMEM, SMEM],
         out_specs=VMEM,
         scratch_shapes=[
             pltpu.VMEM(own.shape, jnp.bfloat16),
             pltpu.VMEM((w_local, orbitals, orbitals), jnp.bfloat16),
+            pltpu.SemaphoreType.DMA((w_local,)),
         ],
         compiler_params=params(16),
         name="propagate",

time: 91.7 us -> 91.8 us (level)
  no operation moved by 1% of the time
where the time goes in v4:
time: 91.8 us; the launch traced here: 90.6 us
  blocking collectives  36.5 us (40%)
  waiting for transfers between devices  24.3 us (26%)
  Pallas kernels  22.3 us (24%)
  starting transfers between devices  6.22 us (7%)
  local copies, waits for them, and re-layouts  1.14 us (1%)
    all_to_all x3, blocking collectives, exchange(): lax.all_to_all(blocks, 'pair', split_axis=0, concat_axis=0, tiled=True)  36.5 us
    all_to_all x1, waiting for transfers between devices, exchange(): lax.all_to_all(blocks, 'pair', split_axis=0, concat_axis=0, tiled=True)  13.1 us
    pallas_call x1, Pallas kernels, bias_partial(): pl.pallas_call(body, out_shape=jax.ShapeDtypeStruct((count, w_local * str...  9.78 us
    pallas_call x1, Pallas kernels, potential(): pl.pallas_call(body, out_shape=jax.ShapeDtypeStruct((count, w_local, rows...  8.07 us
    ppermute x1, waiting for transfers between devices, neighbours(): lax.ppermute(block, 'pair', forward)  7.6 us
    all_to_all x1, starting transfers between devices, exchange(): lax.all_to_all(blocks, 'pair', split_axis=0, concat_axis=0, tiled=True)  4.53 us
    pallas_call x1, Pallas kernels, propagate(): pl.pallas_call(body, out_shape=jax.ShapeDtypeStruct(own.shape, jnp.bfloat...  3.83 us
    ppermute x1, waiting for transfers between devices, neighbours(): lax.ppermute(block, 'pair', backward)  3.66 us
  transfers between devices with their start and end apart: 3, of which 3 were waited for; matrix products, arithmetic and copies ran while one was open for 0% of the time, Pallas kernels for 0%

profile of v4, /device:TPU:1, one launch (start us, length us, event | category | flops | bytes accessed | tf_op | source)
XLA Modules:
  0.0 90.6 jit_solution(15335387763397455677)
XLA Ops:
  0.0 0.0 copy-start
  0.0 0.0 copy-start.3
  0.0 1.1 %copy-done.3 = bf16[2,512,128]{2,1,0:T(8,128)(2,1)S(1)} copy-done((bf16[2,512,128]{2,1,0:T(8,128)(2,1)S(1)}, bf16[2,512,128]{2,1,0:T(8,128)(2,1)}, u32[]{:S(2)}) %copy-start.3) | copy-done | bytes 262168
  1.1 0.0 copy-start.5
  1.1 0.0 copy-start.6
  1.1 0.0 copy-start.7
  1.2 0.0 copy-start.8
  1.2 16.9 %all_to_all.20.moved_ref = bf16[16,64,128]{2,1,0:T(8,128)(2,1)S(1)} all-to-all(bf16[16,64,128]{2,1,0:T(8,128)(2,1)S(1)} %pack.1), channel_id=1, replica_groups=mesh['groups'=2,'pair'=16] {'pair'}, dimensions={0} | all-to-all | bytes 524288 | tf_op jit(solution)/shard_map/all_to_all | solution.py:28
  18.1 0.0 copy-done
  18.1 0.0 copy-done.5
  18.1 9.8 %bias_partial.1 = bf16[16,16,128]{2,1,0:T(8,128)(2,1)S(1)} custom-call(bf16[16,64,128]{2,1,0:T(8,128)(2,1)S(1)} %all_to_all.20.moved_ref, bf16[512,128]{1,0:T(8,128)(2,1)S(1)} %copy-done.5, bf16[1024,16384]{1,0:T(8,128)(2,1)S(1)} %copy-done), custom_call_target="tpu_custom_call" | custom-call | tf_op jit(solution)/shard_map/bias_partial/pallas_call | solution.py:93
  27.9 9.2 %all_to_all.21.partials_ref = bf16[16,16,128]{2,1,0:T(8,128)(2,1)S(1)} all-to-all(bf16[16,16,128]{2,1,0:T(8,128)(2,1)S(1)} %bias_partial.1), channel_id=1, replica_groups=mesh['groups'=2,'pair'=16] {'pair'}, dimensions={0} | all-to-all | bytes 131072 | tf_op jit(solution)/shard_map/all_to_all | solution.py:28
  37.1 0.0 copy-done.6
  37.1 0.0 copy-done.7
  37.1 0.0 copy-done.8
  37.1 0.0 copy-start.1
  37.1 0.6 shift_blocks.1
  37.7 0.0 copy-start.4
  37.7 0.0 copy-start.2
  37.7 10.4 %all_to_all.22.blocks_ref = bf16[16,24,128]{2,1,0:T(8,128)(2,1)S(1)} all-to-all(bf16[16,24,128]{2,1,0:T(8,128)(2,1)S(1)} %shift_blocks.1), channel_id=1, replica_groups=mesh['groups'=2,'pair'=16] {'pair'}, dimensions={0} | all-to-all | bytes 196608 | tf_op jit(solution)/shard_map/all_to_all | solution.py:28
  48.1 0.0 copy-done.1
  48.1 8.1 %potential.1 = bf16[16,2,32,512]{3,2,1,0:T(8,128)(2,1)} custom-call(bf16[16,24,128]{2,1,0:T(8,128)(2,1)S(1)} %all_to_all.22.blocks_ref, bf16[1024,16384]{1,0:T(8,128)(2,1)S(1)} %copy-done.1), custom_call_target="tpu_custom_call" | custom-call | tf_op jit(solution)/shard_map/potential/pallas_call | solution.py:196
  56.2 4.5 %all-to-all-start.3 = ((bf16[16,64,512]{2,1,0:T(8,128)(2,1)}), bf16[16,64,512]{2,1,0:T(8,128)(2,1)S(1)}, u32[]{:S(2)}, u32[]{:S(2)}) async-start(bf16[16,64,512]{2,1,0:T(8,128)(2,1)} %bitcast), calls=%async_computation.3 | async-start | bytes 2097152 | tf_op jit(solution)/shard_map/all_to_all | solution.py:28
  60.7 0.0 copy-done.4
  60.7 1.7 %collective-permute-start = (bf16[2,512,128]{2,1,0:T(8,128)(2,1)S(1)}, bf16[2,512,128]{2,1,0:T(8,128)(2,1)S(1)}, u32[]{:S(2)}, u32[]{:S(2)}) collective-permute-start(bf16[2,512,128]{2,1,0:T(8,128)(2,1)S(1)} %copy-done.4), channel_id=1, source_target_pairs={{0,1},{1,2},{2,3},{3,4},{4,5},{5,6},{6,7},{7,8},{8,9},{9,10},{10,1... | collective-permute-start | bytes 786440 | tf_op jit(solution)/shard_map/ppermute | solution.py:35
  62.4 0.0 collective-permute-start.1
  62.4 7.6 %collective-permute-done.low_ref = bf16[2,512,128]{2,1,0:T(8,128)(2,1)S(1)} collective-permute-done((bf16[2,512,128]{2,1,0:T(8,128)(2,1)S(1)}, bf16[2,512,128]{2,1,0:T(8,128)(2,1)S(1)}, u32[]{:S(2)}, u32[]{:S(2)}) %collective-permute-start) | collective-permute-done | bytes 262176 | tf_op jit(solution)/shard_map/ppermute | solution.py:35
  70.0 3.7 %collective-permute-done.1.high_ref = bf16[2,512,128]{2,1,0:T(8,128)(2,1)S(1)} collective-permute-done((bf16[2,512,128]{2,1,0:T(8,128)(2,1)S(1)}, bf16[2,512,128]{2,1,0:T(8,128)(2,1)S(1)}, u32[]{:S(2)}, u32[]{:S(2)}) %collective-permute-start.1) | collective-permute-done | bytes 262176 | tf_op jit(solution)/shard_map/ppermute | solution.py:35
  73.6 13.1 %all-to-all-done.3.blocks_ref = bf16[16,64,512]{2,1,0:T(8,128)(2,1)S(1)} async-done(((bf16[16,64,512]{2,1,0:T(8,128)(2,1)}), bf16[16,64,512]{2,1,0:T(8,128)(2,1)S(1)}, u32[]{:S(2)}, u32[]{:S(2)}) %all-to-all-start.3) | async-done | bytes 1048608 | tf_op jit(solution)/shard_map/all_to_all | solution.py:28
  86.7 0.0 copy-done.2
  86.7 3.8 %propagate.1 = bf16[2,512,128]{2,1,0:T(8,128)(2,1)} custom-call(bf16[16,64,512]{2,1,0:T(8,128)(2,1)S(1)} %all-to-all-done.3.blocks_ref, bf16[512,512]{1,0:T(8,128)(2,1)S(1)} %copy-done.2, bf16[2,512,128]{2,1,0:T(8,128)(2,1)S(1)} %collective-permute-done.low_ref, bf16[2,512,128]{2,1,0:T(8,128)(2,1)S(1)} %copy-done.4, ...), custom_call_target="tpu_custom_call" | custom-call | tf_op jit(solution)/shard_map/propagate/pallas_call | solution.py:248
  (1 shorter events, 0.0 us)
Async XLA Ops:
  0.0 18.1 %copy-start = (bf16[1024,16384]{1,0:T(8,128)(2,1)S(1)}, bf16[1024,16384]{1,0:T(8,128)(2,1)}, u32[]{:S(2)}) copy-start(bf16[1024,16384]{1,0:T(8,128)(2,1)} %chol_ref.3) | copy-start | bytes 100663296
  0.0 1.1 %copy-start.3 = (bf16[2,512,128]{2,1,0:T(8,128)(2,1)S(1)}, bf16[2,512,128]{2,1,0:T(8,128)(2,1)}, u32[]{:S(2)}) copy-start(bf16[2,512,128]{2,1,0:T(8,128)(2,1)} %own_ref.1) | copy-start | bytes 786436
  1.1 17.0 %copy-start.5 = (bf16[512,128]{1,0:T(8,128)(2,1)S(1)}, bf16[512,128]{1,0:T(8,128)(2,1)}, u32[]{:S(2)}) copy-start(bf16[512,128]{1,0:T(8,128)(2,1)} %trial_ref.1) | copy-start | bytes 393220
  1.1 36.0 %copy-start.6 = (s32[2]{0:T(128)S(1)}, s32[2]{0:T(128)}, u32[]{:S(2)}) copy-start(s32[2]{0:T(128)} %from_ref.3) | copy-start | bytes 28
  1.1 36.0 %copy-start.7 = (s32[2]{0:T(128)S(1)}, s32[2]{0:T(128)}, u32[]{:S(2)}) copy-start(s32[2]{0:T(128)} %slot_ref.3) | copy-start | bytes 28
  1.2 35.9 %copy-start.8 = (f32[2,1024]{1,0:T(2,128)S(1)}, f32[2,1024]{1,0:T(2,128)}, u32[]{:S(2)}) copy-start(f32[2,1024]{1,0:T(2,128)} %fields_ref.1) | copy-start | bytes 24580
  37.1 11.0 %copy-start.1 = (bf16[1024,16384]{1,0:T(8,128)(2,1)S(1)}, bf16[1024,16384]{1,0:T(8,128)(2,1)}, u32[]{:S(2)}) copy-start(bf16[1024,16384]{1,0:T(8,128)(2,1)} %chol_ref.3) | copy-start | bytes 100663296
  37.7 23.0 %copy-start.4 = (bf16[2,512,128]{2,1,0:T(8,128)(2,1)S(1)}, bf16[2,512,128]{2,1,0:T(8,128)(2,1)}, u32[]{:S(2)}) copy-start(bf16[2,512,128]{2,1,0:T(8,128)(2,1)} %own_ref.1) | copy-start | bytes 786436
  37.7 49.0 %copy-start.2 = (bf16[512,512]{1,0:T(8,128)(2,1)S(1)}, bf16[512,512]{1,0:T(8,128)(2,1)}, u32[]{:S(2)}) copy-start(bf16[512,512]{1,0:T(8,128)(2,1)} %one_ref.1) | copy-start | bytes 1572868
  56.2 30.6 %all-to-all-start.3 = ((bf16[16,64,512]{2,1,0:T(8,128)(2,1)}), bf16[16,64,512]{2,1,0:T(8,128)(2,1)S(1)}, u32[]{:S(2)}, u32[]{:S(2)}) async-start(bf16[16,64,512]{2,1,0:T(8,128)(2,1)} %bitcast), calls=%async_computation.3 | async-start | bytes 2097152 | tf_op jit(solution)/shard_map/all_to_all | solution.py:28
  60.7 9.3 %collective-permute-start = (bf16[2,512,128]{2,1,0:T(8,128)(2,1)S(1)}, bf16[2,512,128]{2,1,0:T(8,128)(2,1)S(1)}, u32[]{:S(2)}, u32[]{:S(2)}) collective-permute-start(bf16[2,512,128]{2,1,0:T(8,128)(2,1)S(1)} %copy-done.4), channel_id=1, source_target_pairs={{0,1},{1,2},{2,3},{3,4},{4,5},{5,6},{6,7},{7,8},{8,9},{9,10},{10,1... | collective-permute-start | bytes 786440 | tf_op jit(solution)/shard_map/ppermute | solution.py:35
  62.4 11.3 %collective-permute-start.1 = (bf16[2,512,128]{2,1,0:T(8,128)(2,1)S(1)}, bf16[2,512,128]{2,1,0:T(8,128)(2,1)S(1)}, u32[]{:S(2)}, u32[]{:S(2)}) collective-permute-start(bf16[2,512,128]{2,1,0:T(8,128)(2,1)S(1)} %copy-done.4), channel_id=1, source_target_pairs={{1,0},{2,1},{3,2},{4,3},{5,4},{6,5},{7,6},{8,7},{9,8},{10,9},{11,1... | collective-permute-start | bytes 786440 | tf_op jit(solution)/shard_map/ppermute | solution.py:35

commit v5 on v4

--- a/solution.py
+++ b/solution.py
@@ -26,6 +26,13 @@
 
 def exchange(blocks):
     return lax.all_to_all(blocks, "pair", split_axis=0, concat_axis=0, tiled=True)
+
+
+def both_sides(block):
+    count = lax.axis_size("pair")
+    inner = [(i, i + 1 if i % 2 == 0 else i - 1) for i in range(count)]
+    outer = [(i, (i - 1 if i % 2 == 0 else i + 1) % count) for i in range(count)]
+    return lax.ppermute(block, "pair", inner), lax.ppermute(block, "pair", outer)
 
 
 def neighbours(block):
@@ -211,21 +218,22 @@
     return out.reshape(count, w_local * rows, orbitals)
 
 
-def propagate(blocks, one_body, low, own, high, src_shift, src_slot):
+def propagate(blocks, one_body, inner, own, outer, src_shift, src_slot):
     w_local, orbitals, _ = own.shape
     count = blocks.shape[0]
     rows = orbitals // count
 
-    def body(blocks_ref, one_ref, low_ref, own_ref, high_ref, from_ref, slot_ref, out_ref, term_ref, mat_ref, sems):
+    def body(blocks_ref, one_ref, inner_ref, own_ref, outer_ref, from_ref, slot_ref, out_ref, term_ref, mat_ref, sems):
         def fetch(source, walker):
             return pltpu.make_async_copy(source.at[slot_ref[walker]], term_ref.at[walker], sems.at[walker])
 
-        for walker in range(w_local):
-            for offset, source in ((-1, low_ref), (0, own_ref), (1, high_ref)):
-
-                @pl.when(from_ref[walker] == offset)
+        side = 1 - 2 * lax.rem(lax.axis_index("pair"), 2)
+        for walker in range(w_local):
+            for offset, side_ref in ((-1, outer_ref), (0, own_ref), (1, inner_ref)):
+
+                @pl.when(from_ref[walker] * side == offset)
                 def _():
-                    fetch(source, walker).start()
+                    fetch(side_ref, walker).start()
 
         one = one_ref[...].astype(jnp.float32).reshape(count, rows, orbitals)
         for walker in range(w_local):
@@ -237,7 +245,7 @@
         totals = [term.astype(jnp.float32) for term in terms]
         for order in range(1, TERMS):
             products = [
-                jnp.dot(mat_ref[walker], terms[walker], preferred_element_type=jnp.float32) / order
+                jnp.dot(mat_ref[walker], terms[walker], preferred_element_type=jnp.float32) * (1.0 / order)
                 for walker in range(w_local)
             ]
             totals = [total + product for total, product in zip(totals, products)]
@@ -257,7 +265,7 @@
         ],
         compiler_params=params(16),
         name="propagate",
-    )(blocks, one_body, low, own, high, src_shift, src_slot)
+    )(blocks, one_body, inner, own, outer, src_shift, src_slot)
 
 
 def plain(chol, walkers, trial, one_body, fields, src_shift, src_slot):
@@ -298,19 +306,20 @@
     count = lax.axis_size("pair")
     w_local, orbitals, _ = walkers.shape
 
-    low, high = neighbours(walkers)
+    inner, outer = both_sides(walkers)
     sent = pack(walkers, count)
     moved = exchange(sent)
     partial = bias_partial(moved, trial, chol, w_local)
     partials = exchange(partial)
     blocks = exchange(shift_blocks(partials, fields, src_shift, src_slot))
     received = exchange(potential(blocks, chol, w_local, orbitals))
-    return propagate(received, one_body, low, walkers, high, src_shift, src_slot)
+    return propagate(received, one_body, inner, walkers, outer, src_shift, src_slot)
 
 
 def shards(chol, walkers, *rest):
     rows = chol.shape[1] // walkers.shape[1]
     fits = 2 * chol.size <= 32 * MIB and rows % 16 == 0 and chol.shape[0] % LANES == 0
+    fits = fits and lax.axis_size("pair") % 2 == 0
     return (held if fits else plain)(chol, walkers, *rest)
 
 

time: 91.8 us -> 91.8 us (level)
  transfers between devices with their start and end apart: 3 -> 3, of which waited for: 3 -> 2; matrix products, arithmetic and copies ran while one was open for 0% -> 0% of each run, Pallas kernels for 0% -> 0%
where the time goes in v5:
time: 91.8 us; the launch traced here: 90.6 us
  blocking collectives  36.5 us (40%)
  waiting for transfers between devices  24.2 us (26%)
  Pallas kernels  22.3 us (24%)
  starting transfers between devices  6.35 us (7%)
  local copies, waits for them, and re-layouts  1.14 us (1%)
    all_to_all x3, blocking collectives, exchange(): lax.all_to_all(blocks, 'pair', split_axis=0, concat_axis=0, tiled=True)  36.5 us
    all_to_all x1, waiting for transfers between devices, exchange(): lax.all_to_all(blocks, 'pair', split_axis=0, concat_axis=0, tiled=True)  13.1 us
    ppermute x1, waiting for transfers between devices, both_sides(): lax.ppermute(block, 'pair', outer)  11.1 us
    pallas_call x1, Pallas kernels, bias_partial(): pl.pallas_call(body, out_shape=jax.ShapeDtypeStruct((count, w_local * str...  9.78 us
    pallas_call x1, Pallas kernels, potential(): pl.pallas_call(body, out_shape=jax.ShapeDtypeStruct((count, w_local, rows...  8.07 us
    all_to_all x1, starting transfers between devices, exchange(): lax.all_to_all(blocks, 'pair', split_axis=0, concat_axis=0, tiled=True)  4.53 us
    pallas_call x1, Pallas kernels, propagate(): pl.pallas_call(body, out_shape=jax.ShapeDtypeStruct(own.shape, jnp.bfloat...  3.84 us
  transfers between devices with their start and end apart: 3, of which 2 were waited for; matrix products, arithmetic and copies ran while one was open for 0% of the time, Pallas kernels for 0%

profile of v5, /device:TPU:1, one launch (start us, length us, event | category | flops | bytes accessed | tf_op | source)
XLA Modules:
  0.0 90.6 jit_solution(6365857009138290585)
XLA Ops:
  0.0 0.0 copy-start
  0.0 0.0 copy-start.3
  0.0 1.1 %copy-done.3 = bf16[2,512,128]{2,1,0:T(8,128)(2,1)S(1)} copy-done((bf16[2,512,128]{2,1,0:T(8,128)(2,1)S(1)}, bf16[2,512,128]{2,1,0:T(8,128)(2,1)}, u32[]{:S(2)}) %copy-start.3) | copy-done | bytes 262168
  1.1 0.0 copy-start.5
  1.1 0.0 copy-start.6
  1.1 0.0 copy-start.7
  1.2 0.0 copy-start.8
  1.2 16.9 %all_to_all.20.moved_ref = bf16[16,64,128]{2,1,0:T(8,128)(2,1)S(1)} all-to-all(bf16[16,64,128]{2,1,0:T(8,128)(2,1)S(1)} %pack.1), channel_id=1, replica_groups=mesh['groups'=2,'pair'=16] {'pair'}, dimensions={0} | all-to-all | bytes 524288 | tf_op jit(solution)/shard_map/all_to_all | solution.py:28
  18.1 0.0 copy-done
  18.1 0.0 copy-done.5
  18.1 9.8 %bias_partial.1 = bf16[16,16,128]{2,1,0:T(8,128)(2,1)S(1)} custom-call(bf16[16,64,128]{2,1,0:T(8,128)(2,1)S(1)} %all_to_all.20.moved_ref, bf16[512,128]{1,0:T(8,128)(2,1)S(1)} %copy-done.5, bf16[1024,16384]{1,0:T(8,128)(2,1)S(1)} %copy-done), custom_call_target="tpu_custom_call" | custom-call | tf_op jit(solution)/shard_map/bias_partial/pallas_call | solution.py:100
  27.9 9.2 %all_to_all.21.partials_ref = bf16[16,16,128]{2,1,0:T(8,128)(2,1)S(1)} all-to-all(bf16[16,16,128]{2,1,0:T(8,128)(2,1)S(1)} %bias_partial.1), channel_id=1, replica_groups=mesh['groups'=2,'pair'=16] {'pair'}, dimensions={0} | all-to-all | bytes 131072 | tf_op jit(solution)/shard_map/all_to_all | solution.py:28
  37.1 0.0 copy-done.6
  37.1 0.0 copy-done.7
  37.1 0.0 copy-done.8
  37.1 0.0 copy-start.1
  37.1 0.6 shift_blocks.1
  37.7 0.0 copy-start.4
  37.7 0.0 copy-start.2
  37.7 10.4 %all_to_all.22.blocks_ref = bf16[16,24,128]{2,1,0:T(8,128)(2,1)S(1)} all-to-all(bf16[16,24,128]{2,1,0:T(8,128)(2,1)S(1)} %shift_blocks.1), channel_id=1, replica_groups=mesh['groups'=2,'pair'=16] {'pair'}, dimensions={0} | all-to-all | bytes 196608 | tf_op jit(solution)/shard_map/all_to_all | solution.py:28
  48.1 0.0 copy-done.1
  48.1 8.1 %potential.1 = bf16[16,2,32,512]{3,2,1,0:T(8,128)(2,1)} custom-call(bf16[16,24,128]{2,1,0:T(8,128)(2,1)S(1)} %all_to_all.22.blocks_ref, bf16[1024,16384]{1,0:T(8,128)(2,1)S(1)} %copy-done.1), custom_call_target="tpu_custom_call" | custom-call | tf_op jit(solution)/shard_map/potential/pallas_call | solution.py:203
  56.2 4.5 %all-to-all-start.3 = ((bf16[16,64,512]{2,1,0:T(8,128)(2,1)}), bf16[16,64,512]{2,1,0:T(8,128)(2,1)S(1)}, u32[]{:S(2)}, u32[]{:S(2)}) async-start(bf16[16,64,512]{2,1,0:T(8,128)(2,1)} %bitcast), calls=%async_computation.3 | async-start | bytes 2097152 | tf_op jit(solution)/shard_map/all_to_all | solution.py:28
  60.7 0.0 copy-done.4
  60.7 0.3 collective-permute-start
  61.0 1.5 %collective-permute-start.1 = (bf16[2,512,128]{2,1,0:T(8,128)(2,1)S(1)}, bf16[2,512,128]{2,1,0:T(8,128)(2,1)S(1)}, u32[]{:S(2)}, u32[]{:S(2)}) collective-permute-start(bf16[2,512,128]{2,1,0:T(8,128)(2,1)S(1)} %copy-done.4), channel_id=1, source_target_pairs={{0,15},{1,2},{2,1},{3,4},{4,3},{5,6},{6,5},{7,8},{8,7},{9,10},{10,... | collective-permute-start | bytes 786440 | tf_op jit(solution)/shard_map/ppermute | solution.py:35
  62.5 0.0 collective-permute-done.inner_ref
  62.5 11.1 %collective-permute-done.1.outer_ref = bf16[2,512,128]{2,1,0:T(8,128)(2,1)S(1)} collective-permute-done((bf16[2,512,128]{2,1,0:T(8,128)(2,1)S(1)}, bf16[2,512,128]{2,1,0:T(8,128)(2,1)S(1)}, u32[]{:S(2)}, u32[]{:S(2)}) %collective-permute-start.1) | collective-permute-done | bytes 262176 | tf_op jit(solution)/shard_map/ppermute | solution.py:35
  73.6 13.1 %all-to-all-done.3.blocks_ref = bf16[16,64,512]{2,1,0:T(8,128)(2,1)S(1)} async-done(((bf16[16,64,512]{2,1,0:T(8,128)(2,1)}), bf16[16,64,512]{2,1,0:T(8,128)(2,1)S(1)}, u32[]{:S(2)}, u32[]{:S(2)}) %all-to-all-start.3) | async-done | bytes 1048608 | tf_op jit(solution)/shard_map/all_to_all | solution.py:28
  86.7 0.0 copy-done.2
  86.7 3.8 %propagate.1 = bf16[2,512,128]{2,1,0:T(8,128)(2,1)} custom-call(bf16[16,64,512]{2,1,0:T(8,128)(2,1)S(1)} %all-to-all-done.3.blocks_ref, bf16[512,512]{1,0:T(8,128)(2,1)S(1)} %copy-done.2, bf16[2,512,128]{2,1,0:T(8,128)(2,1)S(1)} %collective-permute-done.inner_ref, bf16[2,512,128]{2,1,0:T(8,128)(2,1)S(1)} %copy-done.4, ...), custom_call_target="tpu_custom_call" | custom-call | tf_op jit(solution)/shard_map/propagate/pallas_call | solution.py:256
  (1 shorter events, 0.0 us)
Async XLA Ops:
  0.0 18.1 %copy-start = (bf16[1024,16384]{1,0:T(8,128)(2,1)S(1)}, bf16[1024,16384]{1,0:T(8,128)(2,1)}, u32[]{:S(2)}) copy-start(bf16[1024,16384]{1,0:T(8,128)(2,1)} %chol_ref.3) | copy-start | bytes 100663296
  0.0 1.1 %copy-start.3 = (bf16[2,512,128]{2,1,0:T(8,128)(2,1)S(1)}, bf16[2,512,128]{2,1,0:T(8,128)(2,1)}, u32[]{:S(2)}) copy-start(bf16[2,512,128]{2,1,0:T(8,128)(2,1)} %own_ref.1) | copy-start | bytes 786436
  1.1 17.0 %copy-start.5 = (bf16[512,128]{1,0:T(8,128)(2,1)S(1)}, bf16[512,128]{1,0:T(8,128)(2,1)}, u32[]{:S(2)}) copy-start(bf16[512,128]{1,0:T(8,128)(2,1)} %trial_ref.1) | copy-start | bytes 393220
  1.1 36.0 %copy-start.6 = (s32[2]{0:T(128)S(1)}, s32[2]{0:T(128)}, u32[]{:S(2)}) copy-start(s32[2]{0:T(128)} %from_ref.3) | copy-start | bytes 28
  1.1 36.0 %copy-start.7 = (s32[2]{0:T(128)S(1)}, s32[2]{0:T(128)}, u32[]{:S(2)}) copy-start(s32[2]{0:T(128)} %slot_ref.3) | copy-start | bytes 28
  1.2 35.9 %copy-start.8 = (f32[2,1024]{1,0:T(2,128)S(1)}, f32[2,1024]{1,0:T(2,128)}, u32[]{:S(2)}) copy-start(f32[2,1024]{1,0:T(2,128)} %fields_ref.1) | copy-start | bytes 24580
  37.1 11.0 %copy-start.1 = (bf16[1024,16384]{1,0:T(8,128)(2,1)S(1)}, bf16[1024,16384]{1,0:T(8,128)(2,1)}, u32[]{:S(2)}) copy-start(bf16[1024,16384]{1,0:T(8,128)(2,1)} %chol_ref.3) | copy-start | bytes 100663296
  37.7 23.0 %copy-start.4 = (bf16[2,512,128]{2,1,0:T(8,128)(2,1)S(1)}, bf16[2,512,128]{2,1,0:T(8,128)(2,1)}, u32[]{:S(2)}) copy-start(bf16[2,512,128]{2,1,0:T(8,128)(2,1)} %own_ref.1) | copy-start | bytes 786436
  37.7 49.0 %copy-start.2 = (bf16[512,512]{1,0:T(8,128)(2,1)S(1)}, bf16[512,512]{1,0:T(8,128)(2,1)}, u32[]{:S(2)}) copy-start(bf16[512,512]{1,0:T(8,128)(2,1)} %one_ref.1) | copy-start | bytes 1572868
  56.2 30.6 %all-to-all-start.3 = ((bf16[16,64,512]{2,1,0:T(8,128)(2,1)}), bf16[16,64,512]{2,1,0:T(8,128)(2,1)S(1)}, u32[]{:S(2)}, u32[]{:S(2)}) async-start(bf16[16,64,512]{2,1,0:T(8,128)(2,1)} %bitcast), calls=%async_computation.3 | async-start | bytes 2097152 | tf_op jit(solution)/shard_map/all_to_all | solution.py:28
  60.7 1.8 %collective-permute-start = (bf16[2,512,128]{2,1,0:T(8,128)(2,1)S(1)}, bf16[2,512,128]{2,1,0:T(8,128)(2,1)S(1)}, u32[]{:S(2)}, u32[]{:S(2)}) collective-permute-start(bf16[2,512,128]{2,1,0:T(8,128)(2,1)S(1)} %copy-done.4), channel_id=1, source_target_pairs={{0,1},{1,0},{2,3},{3,2},{4,5},{5,4},{6,7},{7,6},{8,9},{9,8},{10,11... | collective-permute-start | bytes 786440 | tf_op jit(solution)/shard_map/ppermute | solution.py:35
  61.0 12.7 %collective-permute-start.1 = (bf16[2,512,128]{2,1,0:T(8,128)(2,1)S(1)}, bf16[2,512,128]{2,1,0:T(8,128)(2,1)S(1)}, u32[]{:S(2)}, u32[]{:S(2)}) collective-permute-start(bf16[2,512,128]{2,1,0:T(8,128)(2,1)S(1)} %copy-done.4), channel_id=1, source_target_pairs={{0,15},{1,2},{2,1},{3,4},{4,3},{5,6},{6,5},{7,8},{8,7},{9,10},{10,... | collective-permute-start | bytes 786440 | tf_op jit(solution)/shard_map/ppermute | solution.py:35

commit v6 on v5

--- a/solution.py
+++ b/solution.py
@@ -10,7 +10,7 @@
 LANES = 128
 MIB = 1 << 20
 GROUP = 8
-COVER = pl.CostEstimate(flops=100_000_000_000, bytes_accessed=400_000_000, transcendentals=0)
+COVER = pl.CostEstimate(flops=200_000_000_000, bytes_accessed=200_000_000, transcendentals=0)
 
 sqrt_tau = 0.1
 bias_cap = 1.0
@@ -56,27 +56,78 @@
         in_specs=[VMEM],
         out_specs=VMEM,
         compiler_params=params(4),
-        cost_estimate=COVER,
         name="pack",
     )(walkers)
 
 
-def bias_partial(moved, trial, chol, w_local):
+def fold(chol, trial, vectors):
+    orbitals, occupied = trial.shape
+    rows = chol.shape[1] // orbitals
+    per = 4
+
+    def body(chol_ref, trial_ref, folded_ref):
+        for row in range(per):
+            folded_ref[:, row * occupied : (row + 1) * occupied] = jnp.dot(
+                chol_ref[:, row * orbitals : (row + 1) * orbitals],
+                trial_ref[...],
+                preferred_element_type=jnp.float32,
+            ).astype(jnp.bfloat16)
+
+    return pl.pallas_call(
+        body,
+        out_shape=pltpu.HBM((vectors, rows * occupied), jnp.bfloat16),
+        grid=(rows // per,),
+        in_specs=[
+            pl.BlockSpec((vectors, per * orbitals), lambda i: (0, i)),
+            pl.BlockSpec((orbitals, occupied), lambda i: (0, 0)),
+        ],
+        out_specs=pl.BlockSpec((vectors, per * occupied), lambda i: (0, i)),
+        compiler_params=params(16),
+        cost_estimate=pl.CostEstimate(
+            flops=2 * vectors * rows * orbitals * occupied,
+            bytes_accessed=2 * vectors * rows * orbitals,
+            transcendentals=0,
+        ),
+        name="fold",
+    )(pltpu.with_memory_space_constraint(chol, pltpu.HBM), trial)
+
+
+def bias_partial(moved, trial, folded, chol, w_local):
     count, height, occupied = moved.shape
     orbitals = trial.shape[0]
     vectors, pairs = chol.shape
+    ready = folded.shape[0]
     rows = pairs // orbitals
     walkers = count * w_local
     strips = vectors // LANES
-    steps = 2
+    steps = 4
     width = pairs // steps
 
-    def body(moved_ref, trial_ref, chol_ref, out_ref, wide_ref, lhs_ref, green_ref, acc_ref, flat_ref):
+    def body(moved_ref, trial_ref, folded_ref, chol_ref, out_ref, *scratch):
+        wide_ref, lhs_ref, flat_lhs_ref, green_ref, folded_held_ref, chol_held_ref, flat_ref, sems = scratch
+        fetch = pltpu.make_async_copy(folded_ref, folded_held_ref, sems.at[steps])
+        fetch.start()
+
+        def part_of(step):
+            cols = pl.ds(step * width, width)
+            return pltpu.make_async_copy(
+                chol_ref.at[pl.ds(ready, vectors - ready), cols], chol_held_ref.at[:, cols], sems.at[step]
+            )
+
+        for step in range(steps):
+            part_of(step).start()
+
+        def place(sums, first):
+            for strip in range(sums.shape[0] // LANES):
+                flat_ref[pl.ds(first + strip, walkers, stride=strips), :] = sums[
+                    strip * LANES : (strip + 1) * LANES, :
+                ].T
+
         wide_ref[...] = moved_ref[...].astype(jnp.float32).reshape(count * height, occupied)
         for row in range(rows):
-            lhs_ref[row * walkers : (row + 1) * walkers, :] = wide_ref[
-                pl.ds(row, walkers, stride=rows), :
-            ].astype(jnp.bfloat16)
+            mine = wide_ref[pl.ds(row, walkers, stride=rows), :].astype(jnp.bfloat16)
+            lhs_ref[row * walkers : (row + 1) * walkers, :] = mine
+            flat_lhs_ref[:, row * occupied : (row + 1) * occupied] = mine
         formed = lax.dot_general(
             lhs_ref[...], trial_ref[...], (((1,), (1,)), ((), ())), preferred_element_type=jnp.float32
         )
@@ -84,34 +135,46 @@
             green_ref[:, row * orbitals : (row + 1) * orbitals] = formed[
                 row * walkers : (row + 1) * walkers, :
             ].astype(jnp.bfloat16)
-        acc_ref[...] = jnp.zeros_like(acc_ref)
-
-        @pl.loop(0, steps)
-        def _(step):
-            cols = pl.ds(pl.multiple_of(step * width, width), width)
-            acc_ref[...] += lax.dot_general(
-                chol_ref[:, cols], green_ref[:, cols], (((1,), (1,)), ((), ())), preferred_element_type=jnp.float32
+        fetch.wait()
+        place(
+            lax.dot_general(
+                folded_held_ref[...], flat_lhs_ref[...], (((1,), (1,)), ((), ())), preferred_element_type=jnp.float32
+            ),
+            0,
+        )
+        sums = jnp.zeros((vectors - ready, walkers), jnp.float32)
+        for step in range(steps):
+            part_of(step).wait()
+            cols = slice(step * width, (step + 1) * width)
+            sums = sums + lax.dot_general(
+                chol_held_ref[:, cols], green_ref[:, cols], (((1,), (1,)), ((), ())), preferred_element_type=jnp.float32
             )
-
-        for strip in range(strips):
-            flat_ref[pl.ds(strip, walkers, stride=strips), :] = acc_ref[strip * LANES : (strip + 1) * LANES, :].T
+        place(sums, ready // LANES)
         out_ref[...] = flat_ref[...].astype(jnp.bfloat16).reshape(out_ref.shape)
 
     return pl.pallas_call(
         body,
         out_shape=jax.ShapeDtypeStruct((count, w_local * strips, LANES), jnp.bfloat16),
-        in_specs=[VMEM, VMEM, VMEM],
+        in_specs=[VMEM, VMEM, ANY, ANY],
         out_specs=VMEM,
         scratch_shapes=[
             pltpu.VMEM((count * height, occupied), jnp.float32),
             pltpu.VMEM((count * height, occupied), jnp.bfloat16),
+            pltpu.VMEM((walkers, rows * occupied), jnp.bfloat16),
             pltpu.VMEM((walkers, pairs), jnp.bfloat16),
-            pltpu.VMEM((vectors, walkers), jnp.float32),
+            pltpu.VMEM(folded.shape, jnp.bfloat16),
+            pltpu.VMEM((vectors - ready, pairs), jnp.bfloat16),
             pltpu.VMEM((walkers * strips, LANES), jnp.float32),
+            pltpu.SemaphoreType.DMA((steps + 1,)),
         ],
-        compiler_params=params(16),
+        compiler_params=params(26),
         name="bias_partial",
-    )(moved, trial, chol)
+    )(
+        moved,
+        trial,
+        pltpu.with_memory_space_constraint(folded, pltpu.HBM),
+        pltpu.with_memory_space_constraint(chol, pltpu.HBM),
+    )
 
 
 def shift_blocks(partials, fields, src_shift, src_slot):
@@ -309,7 +372,8 @@
     inner, outer = both_sides(walkers)
     sent = pack(walkers, count)
     moved = exchange(sent)
-    partial = bias_partial(moved, trial, chol, w_local)
+    folded = fold(chol, trial, chol.shape[0] * 5 // 8 // LANES * LANES)
+    partial = bias_partial(moved, trial, folded, chol, w_local)
     partials = exchange(partial)
     blocks = exchange(shift_blocks(partials, fields, src_shift, src_slot))
     received = exchange(potential(blocks, chol, w_local, orbitals))
@@ -318,7 +382,7 @@
 
 def shards(chol, walkers, *rest):
     rows = chol.shape[1] // walkers.shape[1]
-    fits = 2 * chol.size <= 32 * MIB and rows % 16 == 0 and chol.shape[0] % LANES == 0
+    fits = 2 * chol.size <= 32 * MIB and rows % 16 == 0 and chol.shape[0] % (8 * LANES) == 0
     fits = fits and lax.axis_size("pair") % 2 == 0
     return (held if fits else plain)(chol, walkers, *rest)
 

time: 91.8 us -> 101 us (1.10)
  Pallas kernels: 22.3 us -> 37.9 us
  blocking collectives: 36.5 us -> 22.2 us
  starting transfers between devices: 6.35 us -> 13.7 us
    all_to_all x3 -> x2, blocking collectives: 36.5 us -> 22.2 us  [exchange(): lax.all_to_all(blocks, 'pair', split_axis=0, concat_axis=0, tiled=True)]
    pallas_call x0 -> x1, Pallas kernels: none -> 13.6 us  [fold(): pl.pallas_call(body, out_shape=pltpu.HBM((vectors, rows * occupied), jnp....]
    all_to_all x1 -> x2, starting transfers between devices: 4.53 us -> 11.9 us  [exchange(): lax.all_to_all(blocks, 'pair', split_axis=0, concat_axis=0, tiled=True)]
    pallas_call x1, Pallas kernels: 9.78 us -> 11.1 us  [bias_partial(): pl.pallas_call(body, out_shape=jax.ShapeDtypeStruct((count, w_local * str...]
    all_to_all x1 -> x2, waiting for transfers between devices: 13.1 us -> 13.1 us  [exchange(): lax.all_to_all(blocks, 'pair', split_axis=0, concat_axis=0, tiled=True)]
  transfers between devices with their start and end apart: 3 -> 4, of which waited for: 2 -> 2; matrix products, arithmetic and copies ran while one was open for 0% -> 0% of each run, Pallas kernels for 0% -> 14%
where the time goes in v6:
time: 101 us; the launch traced here: 99.9 us
  Pallas kernels  37.9 us (38%)
  waiting for transfers between devices  24.2 us (24%)
  blocking collectives  22.2 us (22%)
  starting transfers between devices  13.7 us (14%)
  local copies, waits for them, and re-layouts  1.88 us (2%)
    all_to_all x2, blocking collectives, exchange(): lax.all_to_all(blocks, 'pair', split_axis=0, concat_axis=0, tiled=True)  22.2 us
    pallas_call x1, Pallas kernels, fold(): pl.pallas_call(body, out_shape=pltpu.HBM((vectors, rows * occupied), jnp....  13.6 us
    all_to_all x2, waiting for transfers between devices, exchange(): lax.all_to_all(blocks, 'pair', split_axis=0, concat_axis=0, tiled=True)  13.1 us
    all_to_all x2, starting transfers between devices, exchange(): lax.all_to_all(blocks, 'pair', split_axis=0, concat_axis=0, tiled=True)  11.9 us
    ppermute x1, waiting for transfers between devices, both_sides(): lax.ppermute(block, 'pair', outer)  11.1 us
    pallas_call x1, Pallas kernels, bias_partial(): pl.pallas_call(body, out_shape=jax.ShapeDtypeStruct((count, w_local * str...  11.1 us
    pallas_call x1, Pallas kernels, potential(): pl.pallas_call(body, out_shape=jax.ShapeDtypeStruct((count, w_local, rows...  8.04 us
    pallas_call x1, Pallas kernels, propagate(): pl.pallas_call(body, out_shape=jax.ShapeDtypeStruct(own.shape, jnp.bfloat...  3.84 us
  transfers between devices with their start and end apart: 4, of which 2 were waited for; matrix products, arithmetic and copies ran while one was open for 0% of the time, Pallas kernels for 14%

profile of v6, /device:TPU:1, one launch (start us, length us, event | category | flops | bytes accessed | tf_op | source)
XLA Modules:
  0.0 99.9 jit_solution(5273133626587781389)
XLA Ops:
  0.0 0.0 copy-start.1
  0.0 0.9 copy-done.1
  1.0 0.0 copy-start.4
  1.0 0.7 pack.1
  1.7 7.3 %all-to-all-start = ((bf16[16,64,128]{2,1,0:T(8,128)(2,1)}), bf16[16,64,128]{2,1,0:T(8,128)(2,1)S(1)}, u32[]{:S(2)}, u32[]{:S(2)}) async-start(bf16[16,64,128]{2,1,0:T(8,128)(2,1)} %pack.1), calls=%async_computation | async-start | bytes 524288 | tf_op jit(solution)/shard_map/all_to_all | solution.py:28
  9.0 0.0 copy-start.3
  9.0 0.9 copy-done.3
  9.9 0.0 copy-start.6
  9.9 0.0 copy-start.7
  9.9 0.0 copy-start.8
  9.9 13.6 %fold.1.folded_ref = bf16[640,4096]{1,0:T(8,128)(2,1)} custom-call(bf16[1024,16384]{1,0:T(8,128)(2,1)} %chol_ref.5, bf16[512,128]{1,0:T(8,128)(2,1)S(1)} %copy-done.3), custom_call_target="tpu_custom_call" | custom-call | flops 2684354560 | bytes 20971520 | tf_op jit(solution)/shard_map/fold/pallas_call | solution.py:76
  23.5 0.0 all-to-all-done.moved_ref
  23.5 0.0 copy-done.4
  23.5 11.1 %bias_partial.1 = bf16[16,16,128]{2,1,0:T(8,128)(2,1)S(1)} custom-call(bf16[16,64,128]{2,1,0:T(8,128)(2,1)S(1)} %all-to-all-done.moved_ref, bf16[512,128]{1,0:T(8,128)(2,1)S(1)} %copy-done.4, bf16[640,4096]{1,0:T(8,128)(2,1)} %fold.1.folded_ref, bf16[1024,16384]{1,0:T(8,128)(2,1)} %chol_ref.5), custom_call_target="tpu_custom_call" | custom-call | tf_op jit(solution)/shard_map/bias_partial/pallas_call | solution.py:155
  34.6 11.9 %all_to_all.20.partials_ref = bf16[16,16,128]{2,1,0:T(8,128)(2,1)S(1)} all-to-all(bf16[16,16,128]{2,1,0:T(8,128)(2,1)S(1)} %bias_partial.1), channel_id=1, replica_groups=mesh['groups'=2,'pair'=16] {'pair'}, dimensions={0} | all-to-all | bytes 131072 | tf_op jit(solution)/shard_map/all_to_all | solution.py:28
  46.5 0.0 copy-done.6
  46.5 0.0 copy-done.7
  46.5 0.0 copy-done.8
  46.5 0.0 copy-start
  46.5 0.6 shift_blocks.1
  47.1 0.0 copy-start.2
  47.1 0.0 copy-start.5
  47.1 10.4 %all_to_all.21.blocks_ref = bf16[16,24,128]{2,1,0:T(8,128)(2,1)S(1)} all-to-all(bf16[16,24,128]{2,1,0:T(8,128)(2,1)S(1)} %shift_blocks.1), channel_id=1, replica_groups=mesh['groups'=2,'pair'=16] {'pair'}, dimensions={0} | all-to-all | bytes 196608 | tf_op jit(solution)/shard_map/all_to_all | solution.py:28
  57.5 0.0 copy-done
  57.5 8.0 %potential.1 = bf16[16,2,32,512]{3,2,1,0:T(8,128)(2,1)} custom-call(bf16[16,24,128]{2,1,0:T(8,128)(2,1)S(1)} %all_to_all.21.blocks_ref, bf16[1024,16384]{1,0:T(8,128)(2,1)S(1)} %copy-done), custom_call_target="tpu_custom_call" | custom-call | tf_op jit(solution)/shard_map/potential/pallas_call | solution.py:266
  65.5 4.5 %all-to-all-start.3 = ((bf16[16,64,512]{2,1,0:T(8,128)(2,1)}), bf16[16,64,512]{2,1,0:T(8,128)(2,1)S(1)}, u32[]{:S(2)}, u32[]{:S(2)}) async-start(bf16[16,64,512]{2,1,0:T(8,128)(2,1)} %bitcast), calls=%async_computation.3 | async-start | bytes 2097152 | tf_op jit(solution)/shard_map/all_to_all | solution.py:28
  70.0 0.0 copy-done.2
  70.0 0.3 collective-permute-start
  70.3 1.5 %collective-permute-start.1 = (bf16[2,512,128]{2,1,0:T(8,128)(2,1)S(1)}, bf16[2,512,128]{2,1,0:T(8,128)(2,1)S(1)}, u32[]{:S(2)}, u32[]{:S(2)}) collective-permute-start(bf16[2,512,128]{2,1,0:T(8,128)(2,1)S(1)} %copy-done.2), channel_id=1, source_target_pairs={{0,15},{1,2},{2,1},{3,4},{4,3},{5,6},{6,5},{7,8},{8,7},{9,10},{10,... | collective-permute-start | bytes 786440 | tf_op jit(solution)/shard_map/ppermute | solution.py:35
  71.9 0.0 collective-permute-done.inner_ref
  71.9 11.1 %collective-permute-done.1.outer_ref = bf16[2,512,128]{2,1,0:T(8,128)(2,1)S(1)} collective-permute-done((bf16[2,512,128]{2,1,0:T(8,128)(2,1)S(1)}, bf16[2,512,128]{2,1,0:T(8,128)(2,1)S(1)}, u32[]{:S(2)}, u32[]{:S(2)}) %collective-permute-start.1) | collective-permute-done | bytes 262176 | tf_op jit(solution)/shard_map/ppermute | solution.py:35
  83.0 13.1 %all-to-all-done.3.blocks_ref = bf16[16,64,512]{2,1,0:T(8,128)(2,1)S(1)} async-done(((bf16[16,64,512]{2,1,0:T(8,128)(2,1)}), bf16[16,64,512]{2,1,0:T(8,128)(2,1)S(1)}, u32[]{:S(2)}, u32[]{:S(2)}) %all-to-all-start.3) | async-done | bytes 1048608 | tf_op jit(solution)/shard_map/all_to_all | solution.py:28
  96.1 0.0 copy-done.5
  96.1 3.8 %propagate.1 = bf16[2,512,128]{2,1,0:T(8,128)(2,1)} custom-call(bf16[16,64,512]{2,1,0:T(8,128)(2,1)S(1)} %all-to-all-done.3.blocks_ref, bf16[512,512]{1,0:T(8,128)(2,1)S(1)} %copy-done.5, bf16[2,512,128]{2,1,0:T(8,128)(2,1)S(1)} %collective-permute-done.inner_ref, bf16[2,512,128]{2,1,0:T(8,128)(2,1)S(1)} %copy-done.2, ...), custom_call_target="tpu_custom_call" | custom-call | tf_op jit(solution)/shard_map/propagate/pallas_call | solution.py:319
Async XLA Ops:
  0.0 0.9 copy-start.1
  1.0 22.6 %copy-start.4 = (bf16[512,128]{1,0:T(8,128)(2,1)S(1)}, bf16[512,128]{1,0:T(8,128)(2,1)}, u32[]{:S(2)}) copy-start(bf16[512,128]{1,0:T(8,128)(2,1)} %trial_ref.3) | copy-start | bytes 393220
  1.7 21.8 %all-to-all-start = ((bf16[16,64,128]{2,1,0:T(8,128)(2,1)}), bf16[16,64,128]{2,1,0:T(8,128)(2,1)S(1)}, u32[]{:S(2)}, u32[]{:S(2)}) async-start(bf16[16,64,128]{2,1,0:T(8,128)(2,1)} %pack.1), calls=%async_computation | async-start | bytes 524288 | tf_op jit(solution)/shard_map/all_to_all | solution.py:28
  9.0 0.9 copy-start.3
  9.9 36.6 %copy-start.6 = (s32[2]{0:T(128)S(1)}, s32[2]{0:T(128)}, u32[]{:S(2)}) copy-start(s32[2]{0:T(128)} %from_ref.3) | copy-start | bytes 28
  9.9 36.6 %copy-start.7 = (s32[2]{0:T(128)S(1)}, s32[2]{0:T(128)}, u32[]{:S(2)}) copy-start(s32[2]{0:T(128)} %slot_ref.3) | copy-start | bytes 28
  9.9 36.6 %copy-start.8 = (f32[2,1024]{1,0:T(2,128)S(1)}, f32[2,1024]{1,0:T(2,128)}, u32[]{:S(2)}) copy-start(f32[2,1024]{1,0:T(2,128)} %fields_ref.1) | copy-start | bytes 24580
  46.5 11.0 %copy-start = (bf16[1024,16384]{1,0:T(8,128)(2,1)S(1)}, bf16[1024,16384]{1,0:T(8,128)(2,1)}, u32[]{:S(2)}) copy-start(bf16[1024,16384]{1,0:T(8,128)(2,1)} %chol_ref.5) | copy-start | bytes 100663296
  47.1 23.0 %copy-start.2 = (bf16[2,512,128]{2,1,0:T(8,128)(2,1)S(1)}, bf16[2,512,128]{2,1,0:T(8,128)(2,1)}, u32[]{:S(2)}) copy-start(bf16[2,512,128]{2,1,0:T(8,128)(2,1)} %own_ref.1) | copy-start | bytes 786436
  47.1 49.0 %copy-start.5 = (bf16[512,512]{1,0:T(8,128)(2,1)S(1)}, bf16[512,512]{1,0:T(8,128)(2,1)}, u32[]{:S(2)}) copy-start(bf16[512,512]{1,0:T(8,128)(2,1)} %one_ref.1) | copy-start | bytes 1572868
  65.5 30.6 %all-to-all-start.3 = ((bf16[16,64,512]{2,1,0:T(8,128)(2,1)}), bf16[16,64,512]{2,1,0:T(8,128)(2,1)S(1)}, u32[]{:S(2)}, u32[]{:S(2)}) async-start(bf16[16,64,512]{2,1,0:T(8,128)(2,1)} %bitcast), calls=%async_computation.3 | async-start | bytes 2097152 | tf_op jit(solution)/shard_map/all_to_all | solution.py:28
  70.0 1.8 %collective-permute-start = (bf16[2,512,128]{2,1,0:T(8,128)(2,1)S(1)}, bf16[2,512,128]{2,1,0:T(8,128)(2,1)S(1)}, u32[]{:S(2)}, u32[]{:S(2)}) collective-permute-start(bf16[2,512,128]{2,1,0:T(8,128)(2,1)S(1)} %copy-done.2), channel_id=1, source_target_pairs={{0,1},{1,0},{2,3},{3,2},{4,5},{5,4},{6,7},{7,6},{8,9},{9,8},{10,11... | collective-permute-start | bytes 786440 | tf_op jit(solution)/shard_map/ppermute | solution.py:35
  70.3 12.7 %collective-permute-start.1 = (bf16[2,512,128]{2,1,0:T(8,128)(2,1)S(1)}, bf16[2,512,128]{2,1,0:T(8,128)(2,1)S(1)}, u32[]{:S(2)}, u32[]{:S(2)}) collective-permute-start(bf16[2,512,128]{2,1,0:T(8,128)(2,1)S(1)} %copy-done.2), channel_id=1, source_target_pairs={{0,15},{1,2},{2,1},{3,4},{4,3},{5,6},{6,5},{7,8},{8,7},{9,10},{10,... | collective-permute-start | bytes 786440 | tf_op jit(solution)/shard_map/ppermute | solution.py:35

commit v7 on v5

--- a/solution.py
+++ b/solution.py
@@ -10,6 +10,9 @@
 LANES = 128
 MIB = 1 << 20
 GROUP = 8
+TILE = 256
+UNITS = 2
+HELD_ROWS = 1024
 COVER = pl.CostEstimate(flops=100_000_000_000, bytes_accessed=400_000_000, transcendentals=0)
 
 sqrt_tau = 0.1
@@ -68,33 +71,93 @@
     rows = pairs // orbitals
     walkers = count * w_local
     strips = vectors // LANES
-    steps = 2
-    width = pairs // steps
-
-    def body(moved_ref, trial_ref, chol_ref, out_ref, wide_ref, lhs_ref, green_ref, acc_ref, flat_ref):
+    streamed = vectors - TILE
+    pieces = 2
+    piece = streamed // pieces
+    tiles = pairs // TILE
+    unroll = 32 if tiles % 32 == 0 else UNITS
+    tall = rows // 2 * walkers
+
+    def body(moved_ref, trial_ref, chol_ref, out_ref, wide_ref, lhs_ref, green_ref, flat_ref):
         wide_ref[...] = moved_ref[...].astype(jnp.float32).reshape(count * height, occupied)
+        lhs_ref[:, occupied:] = jnp.zeros((rows * walkers, TILE - occupied), jnp.bfloat16)
         for row in range(rows):
-            lhs_ref[row * walkers : (row + 1) * walkers, :] = wide_ref[
+            lhs_ref[row * walkers : (row + 1) * walkers, :occupied] = wide_ref[
                 pl.ds(row, walkers, stride=rows), :
             ].astype(jnp.bfloat16)
-        formed = lax.dot_general(
-            lhs_ref[...], trial_ref[...], (((1,), (1,)), ((), ())), preferred_element_type=jnp.float32
+
+        def form(*accs):
+            beside = jnp.zeros((TILE, TILE - occupied), jnp.bfloat16)
+            for unit in range(UNITS):
+                weights = jnp.concatenate([trial_ref[unit * TILE : (unit + 1) * TILE, :], beside], axis=1)
+                pltpu.matmul_push_rhs(weights, 0, unit, transpose=True)
+            for half in range(2):
+                for unit in range(UNITS):
+                    lhs = lhs_ref[half * tall : (half + 1) * tall, :]
+                    pltpu.matmul_acc_lhs(accs[half * UNITS + unit], lhs, load_staged_rhs=None if half else 0)
+            for half in range(2):
+                for unit in range(UNITS):
+                    formed = pltpu.matmul_pop(accs[half * UNITS + unit]).astype(jnp.bfloat16)
+                    for row in range(rows // 2):
+                        start = (half * rows // 2 + row) * orbitals + unit * TILE
+                        green_ref[:, start : start + TILE] = formed[row * walkers : (row + 1) * walkers, :]
+
+        pl.run_scoped(form, *[pltpu.ACC(unit)((tall, TILE), jnp.float32) for _ in range(2) for unit in range(UNITS)])
+        below = jnp.zeros((TILE - walkers, TILE), jnp.bfloat16)
+
+        def contract(*accs):
+            stream_accs, weight_accs = accs[: pieces * UNITS], accs[pieces * UNITS :]
+
+            @pl.loop(0, tiles // unroll)
+            def _(step):
+                def cols(tile):
+                    return pl.ds(pl.multiple_of((step * unroll + tile) * TILE, TILE), TILE)
+
+                def push_green(tile):
+                    for unit in range(UNITS):
+                        weights = jnp.concatenate([green_ref[:, cols(tile + unit)], below], axis=0)
+                        pltpu.matmul_push_rhs(weights, 0, unit, transpose=True)
+
+                push_green(0)
+                for tile in range(0, unroll, UNITS):
+                    for part in range(pieces):
+                        for unit in range(UNITS):
+                            pltpu.matmul_acc_lhs(
+                                stream_accs[part * UNITS + unit],
+                                chol_ref[part * piece : (part + 1) * piece, cols(tile + unit)],
+                                load_staged_rhs=0 if part == 0 else None,
+                            )
+                        if part == 0:
+                            for unit in range(UNITS):
+                                pltpu.matmul_push_rhs(chol_ref[streamed:, cols(tile + unit)], 1, unit, transpose=True)
+                    for unit in range(UNITS):
+                        pltpu.matmul_acc_lhs(weight_accs[unit], green_ref[:, cols(tile + unit)], load_staged_rhs=1)
+                    if tile + UNITS < unroll:
+                        push_green(tile + UNITS)
+
+            def total(refs):
+                first, *others = [pltpu.matmul_pop(ref) for ref in refs]
+                for other in others:
+                    first = first + other
+                return first
+
+            for part in range(pieces):
+                sums = total(stream_accs[part * UNITS : (part + 1) * UNITS])[:, :walkers]
+                for strip in range(piece // LANES):
+                    flat_ref[pl.ds(part * (piece // LANES) + strip, walkers, stride=strips), :] = sums[
+                        strip * LANES : (strip + 1) * LANES, :
+                    ].T
+            sums = total(weight_accs)
+            for strip in range(TILE // LANES):
+                flat_ref[pl.ds(streamed // LANES + strip, walkers, stride=strips), :] = sums[
+                    :, strip * LANES : (strip + 1) * LANES
+                ]
+
+        pl.run_scoped(
+            contract,
+            *[pltpu.ACC(unit)((piece, TILE), jnp.float32) for _ in range(pieces) for unit in range(UNITS)],
+            *[pltpu.ACC(unit)((walkers, TILE), jnp.float32) for unit in range(UNITS)],
         )
-        for row in range(rows):
-            green_ref[:, row * orbitals : (row + 1) * orbitals] = formed[
-                row * walkers : (row + 1) * walkers, :
-            ].astype(jnp.bfloat16)
-        acc_ref[...] = jnp.zeros_like(acc_ref)
-
-        @pl.loop(0, steps)
-        def _(step):
-            cols = pl.ds(pl.multiple_of(step * width, width), width)
-            acc_ref[...] += lax.dot_general(
-                chol_ref[:, cols], green_ref[:, cols], (((1,), (1,)), ((), ())), preferred_element_type=jnp.float32
-            )
-
-        for strip in range(strips):
-            flat_ref[pl.ds(strip, walkers, stride=strips), :] = acc_ref[strip * LANES : (strip + 1) * LANES, :].T
         out_ref[...] = flat_ref[...].astype(jnp.bfloat16).reshape(out_ref.shape)
 
     return pl.pallas_call(
@@ -104,9 +167,8 @@
         out_specs=VMEM,
         scratch_shapes=[
             pltpu.VMEM((count * height, occupied), jnp.float32),
-            pltpu.VMEM((count * height, occupied), jnp.bfloat16),
+            pltpu.VMEM((rows * walkers, TILE), jnp.bfloat16),
             pltpu.VMEM((walkers, pairs), jnp.bfloat16),
-            pltpu.VMEM((vectors, walkers), jnp.float32),
             pltpu.VMEM((walkers * strips, LANES), jnp.float32),
         ],
         compiler_params=params(16),
@@ -319,7 +381,12 @@
 def shards(chol, walkers, *rest):
     rows = chol.shape[1] // walkers.shape[1]
     fits = 2 * chol.size <= 32 * MIB and rows % 16 == 0 and chol.shape[0] % LANES == 0
-    fits = fits and lax.axis_size("pair") % 2 == 0
+    walkers_all = walkers.shape[0] * lax.axis_size("pair")
+    fits = fits and lax.axis_size("pair") % 2 == 0 and walkers_all % 16 == 0 and walkers_all < TILE
+    fits = fits and chol.shape[1] % (UNITS * TILE) == 0 and chol.shape[0] % TILE == 0
+    fits = fits and walkers.shape[1] == UNITS * TILE and walkers.shape[2] < TILE
+    fits = fits and rows * walkers_all <= HELD_ROWS
+    fits = fits and TILE < chol.shape[0] and chol.shape[0] - TILE + walkers_all <= HELD_ROWS
     return (held if fits else plain)(chol, walkers, *rest)
 
 

time: 91.8 us -> 89.7 us (0.977)
  Pallas kernels: 22.3 us -> 20.2 us
    pallas_call x1, Pallas kernels: 9.78 us -> 7.72 us  [bias_partial(): pl.pallas_call(body, out_shape=jax.ShapeDtypeStruct((count, w_local * str...]
where the time goes in v7:
time: 89.7 us; the launch traced here: 88.5 us
  blocking collectives  36.5 us (41%)
  waiting for transfers between devices  24.2 us (27%)
  Pallas kernels  20.2 us (23%)
  starting transfers between devices  6.34 us (7%)
  local copies, waits for them, and re-layouts  1.14 us (1%)
    all_to_all x3, blocking collectives, exchange(): lax.all_to_all(blocks, 'pair', split_axis=0, concat_axis=0, tiled=True)  36.5 us
    all_to_all x1, waiting for transfers between devices, exchange(): lax.all_to_all(blocks, 'pair', split_axis=0, concat_axis=0, tiled=True)  13.1 us
    ppermute x1, waiting for transfers between devices, both_sides(): lax.ppermute(block, 'pair', outer)  11.1 us
    pallas_call x1, Pallas kernels, potential(): pl.pallas_call(body, out_shape=jax.ShapeDtypeStruct((count, w_local, rows...  8.08 us
    pallas_call x1, Pallas kernels, bias_partial(): pl.pallas_call(body, out_shape=jax.ShapeDtypeStruct((count, w_local * str...  7.72 us
    all_to_all x1, starting transfers between devices, exchange(): lax.all_to_all(blocks, 'pair', split_axis=0, concat_axis=0, tiled=True)  4.52 us
    pallas_call x1, Pallas kernels, propagate(): pl.pallas_call(body, out_shape=jax.ShapeDtypeStruct(own.shape, jnp.bfloat...  3.84 us
  transfers between devices with their start and end apart: 3, of which 2 were waited for; matrix products, arithmetic and copies ran while one was open for 0% of the time, Pallas kernels for 0%

profile of v7, /device:TPU:1, one launch (start us, length us, event | category | flops | bytes accessed | tf_op | source)
XLA Modules:
  0.0 88.5 jit_solution(4983970440231910004)
XLA Ops:
  0.0 0.0 copy-start
  0.0 0.0 copy-start.3
  0.0 1.1 %copy-done.3 = bf16[2,512,128]{2,1,0:T(8,128)(2,1)S(1)} copy-done((bf16[2,512,128]{2,1,0:T(8,128)(2,1)S(1)}, bf16[2,512,128]{2,1,0:T(8,128)(2,1)}, u32[]{:S(2)}) %copy-start.3) | copy-done | bytes 262168
  1.1 0.0 copy-start.5
  1.1 0.0 copy-start.6
  1.1 0.0 copy-start.7
  1.2 0.0 copy-start.8
  1.2 16.9 %all_to_all.20.moved_ref = bf16[16,64,128]{2,1,0:T(8,128)(2,1)S(1)} all-to-all(bf16[16,64,128]{2,1,0:T(8,128)(2,1)S(1)} %pack.1), channel_id=1, replica_groups=mesh['groups'=2,'pair'=16] {'pair'}, dimensions={0} | all-to-all | bytes 524288 | tf_op jit(solution)/shard_map/all_to_all | solution.py:31
  18.1 0.0 copy-done
  18.1 0.0 copy-done.5
  18.1 7.7 %bias_partial.1 = bf16[16,16,128]{2,1,0:T(8,128)(2,1)S(1)} custom-call(bf16[16,64,128]{2,1,0:T(8,128)(2,1)S(1)} %all_to_all.20.moved_ref, bf16[512,128]{1,0:T(8,128)(2,1)S(1)} %copy-done.5, bf16[1024,16384]{1,0:T(8,128)(2,1)S(1)} %copy-done), custom_call_target="tpu_custom_call" | custom-call | tf_op jit(solution)/shard_map/bias_partial/pallas_call | solution.py:163
  25.8 9.2 %all_to_all.21.partials_ref = bf16[16,16,128]{2,1,0:T(8,128)(2,1)S(1)} all-to-all(bf16[16,16,128]{2,1,0:T(8,128)(2,1)S(1)} %bias_partial.1), channel_id=1, replica_groups=mesh['groups'=2,'pair'=16] {'pair'}, dimensions={0} | all-to-all | bytes 131072 | tf_op jit(solution)/shard_map/all_to_all | solution.py:31
  35.0 0.0 copy-done.6
  35.0 0.0 copy-done.7
  35.0 0.0 copy-done.8
  35.0 0.0 copy-start.1
  35.0 0.6 shift_blocks.1
  35.6 0.0 copy-start.4
  35.6 0.0 copy-start.2
  35.7 10.4 %all_to_all.22.blocks_ref = bf16[16,24,128]{2,1,0:T(8,128)(2,1)S(1)} all-to-all(bf16[16,24,128]{2,1,0:T(8,128)(2,1)S(1)} %shift_blocks.1), channel_id=1, replica_groups=mesh['groups'=2,'pair'=16] {'pair'}, dimensions={0} | all-to-all | bytes 196608 | tf_op jit(solution)/shard_map/all_to_all | solution.py:31
  46.0 0.0 copy-done.1
  46.0 8.1 %potential.1 = bf16[16,2,32,512]{3,2,1,0:T(8,128)(2,1)} custom-call(bf16[16,24,128]{2,1,0:T(8,128)(2,1)S(1)} %all_to_all.22.blocks_ref, bf16[1024,16384]{1,0:T(8,128)(2,1)S(1)} %copy-done.1), custom_call_target="tpu_custom_call" | custom-call | tf_op jit(solution)/shard_map/potential/pallas_call | solution.py:265
  54.1 4.5 %all-to-all-start.3 = ((bf16[16,64,512]{2,1,0:T(8,128)(2,1)}), bf16[16,64,512]{2,1,0:T(8,128)(2,1)S(1)}, u32[]{:S(2)}, u32[]{:S(2)}) async-start(bf16[16,64,512]{2,1,0:T(8,128)(2,1)} %bitcast), calls=%async_computation.3 | async-start | bytes 2097152 | tf_op jit(solution)/shard_map/all_to_all | solution.py:31
  58.6 0.0 copy-done.4
  58.6 0.3 collective-permute-start
  58.9 1.5 %collective-permute-start.1 = (bf16[2,512,128]{2,1,0:T(8,128)(2,1)S(1)}, bf16[2,512,128]{2,1,0:T(8,128)(2,1)S(1)}, u32[]{:S(2)}, u32[]{:S(2)}) collective-permute-start(bf16[2,512,128]{2,1,0:T(8,128)(2,1)S(1)} %copy-done.4), channel_id=1, source_target_pairs={{0,15},{1,2},{2,1},{3,4},{4,3},{5,6},{6,5},{7,8},{8,7},{9,10},{10,... | collective-permute-start | bytes 786440 | tf_op jit(solution)/shard_map/ppermute | solution.py:38
  60.4 0.0 collective-permute-done.inner_ref
  60.4 11.1 %collective-permute-done.1.outer_ref = bf16[2,512,128]{2,1,0:T(8,128)(2,1)S(1)} collective-permute-done((bf16[2,512,128]{2,1,0:T(8,128)(2,1)S(1)}, bf16[2,512,128]{2,1,0:T(8,128)(2,1)S(1)}, u32[]{:S(2)}, u32[]{:S(2)}) %collective-permute-start.1) | collective-permute-done | bytes 262176 | tf_op jit(solution)/shard_map/ppermute | solution.py:38
  71.6 13.1 %all-to-all-done.3.blocks_ref = bf16[16,64,512]{2,1,0:T(8,128)(2,1)S(1)} async-done(((bf16[16,64,512]{2,1,0:T(8,128)(2,1)}), bf16[16,64,512]{2,1,0:T(8,128)(2,1)S(1)}, u32[]{:S(2)}, u32[]{:S(2)}) %all-to-all-start.3) | async-done | bytes 1048608 | tf_op jit(solution)/shard_map/all_to_all | solution.py:31
  84.7 0.0 copy-done.2
  84.7 3.8 %propagate.1 = bf16[2,512,128]{2,1,0:T(8,128)(2,1)} custom-call(bf16[16,64,512]{2,1,0:T(8,128)(2,1)S(1)} %all-to-all-done.3.blocks_ref, bf16[512,512]{1,0:T(8,128)(2,1)S(1)} %copy-done.2, bf16[2,512,128]{2,1,0:T(8,128)(2,1)S(1)} %collective-permute-done.inner_ref, bf16[2,512,128]{2,1,0:T(8,128)(2,1)S(1)} %copy-done.4, ...), custom_call_target="tpu_custom_call" | custom-call | tf_op jit(solution)/shard_map/propagate/pallas_call | solution.py:318
  (1 shorter events, 0.0 us)
Async XLA Ops:
  0.0 18.1 %copy-start = (bf16[1024,16384]{1,0:T(8,128)(2,1)S(1)}, bf16[1024,16384]{1,0:T(8,128)(2,1)}, u32[]{:S(2)}) copy-start(bf16[1024,16384]{1,0:T(8,128)(2,1)} %chol_ref.3) | copy-start | bytes 100663296
  0.0 1.1 %copy-start.3 = (bf16[2,512,128]{2,1,0:T(8,128)(2,1)S(1)}, bf16[2,512,128]{2,1,0:T(8,128)(2,1)}, u32[]{:S(2)}) copy-start(bf16[2,512,128]{2,1,0:T(8,128)(2,1)} %own_ref.1) | copy-start | bytes 786436
  1.1 17.0 %copy-start.5 = (bf16[512,128]{1,0:T(8,128)(2,1)S(1)}, bf16[512,128]{1,0:T(8,128)(2,1)}, u32[]{:S(2)}) copy-start(bf16[512,128]{1,0:T(8,128)(2,1)} %trial_ref.1) | copy-start | bytes 393220
  1.1 33.9 %copy-start.6 = (s32[2]{0:T(128)S(1)}, s32[2]{0:T(128)}, u32[]{:S(2)}) copy-start(s32[2]{0:T(128)} %from_ref.3) | copy-start | bytes 28
  1.1 33.9 %copy-start.7 = (s32[2]{0:T(128)S(1)}, s32[2]{0:T(128)}, u32[]{:S(2)}) copy-start(s32[2]{0:T(128)} %slot_ref.3) | copy-start | bytes 28
  1.2 33.9 %copy-start.8 = (f32[2,1024]{1,0:T(2,128)S(1)}, f32[2,1024]{1,0:T(2,128)}, u32[]{:S(2)}) copy-start(f32[2,1024]{1,0:T(2,128)} %fields_ref.1) | copy-start | bytes 24580
  35.0 11.0 %copy-start.1 = (bf16[1024,16384]{1,0:T(8,128)(2,1)S(1)}, bf16[1024,16384]{1,0:T(8,128)(2,1)}, u32[]{:S(2)}) copy-start(bf16[1024,16384]{1,0:T(8,128)(2,1)} %chol_ref.3) | copy-start | bytes 100663296
  35.6 23.0 %copy-start.4 = (bf16[2,512,128]{2,1,0:T(8,128)(2,1)S(1)}, bf16[2,512,128]{2,1,0:T(8,128)(2,1)}, u32[]{:S(2)}) copy-start(bf16[2,512,128]{2,1,0:T(8,128)(2,1)} %own_ref.1) | copy-start | bytes 786436
  35.6 49.0 %copy-start.2 = (bf16[512,512]{1,0:T(8,128)(2,1)S(1)}, bf16[512,512]{1,0:T(8,128)(2,1)}, u32[]{:S(2)}) copy-start(bf16[512,512]{1,0:T(8,128)(2,1)} %one_ref.1) | copy-start | bytes 1572868
  54.1 30.6 %all-to-all-start.3 = ((bf16[16,64,512]{2,1,0:T(8,128)(2,1)}), bf16[16,64,512]{2,1,0:T(8,128)(2,1)S(1)}, u32[]{:S(2)}, u32[]{:S(2)}) async-start(bf16[16,64,512]{2,1,0:T(8,128)(2,1)} %bitcast), calls=%async_computation.3 | async-start | bytes 2097152 | tf_op jit(solution)/shard_map/all_to_all | solution.py:31
  58.6 1.8 %collective-permute-start = (bf16[2,512,128]{2,1,0:T(8,128)(2,1)S(1)}, bf16[2,512,128]{2,1,0:T(8,128)(2,1)S(1)}, u32[]{:S(2)}, u32[]{:S(2)}) collective-permute-start(bf16[2,512,128]{2,1,0:T(8,128)(2,1)S(1)} %copy-done.4), channel_id=1, source_target_pairs={{0,1},{1,0},{2,3},{3,2},{4,5},{5,4},{6,7},{7,6},{8,9},{9,8},{10,11... | collective-permute-start | bytes 786440 | tf_op jit(solution)/shard_map/ppermute | solution.py:38
  58.9 12.7 %collective-permute-start.1 = (bf16[2,512,128]{2,1,0:T(8,128)(2,1)S(1)}, bf16[2,512,128]{2,1,0:T(8,128)(2,1)S(1)}, u32[]{:S(2)}, u32[]{:S(2)}) collective-permute-start(bf16[2,512,128]{2,1,0:T(8,128)(2,1)S(1)} %copy-done.4), channel_id=1, source_target_pairs={{0,15},{1,2},{2,1},{3,4},{4,3},{5,6},{6,5},{7,8},{8,7},{9,10},{10,... | collective-permute-start | bytes 786440 | tf_op jit(solution)/shard_map/ppermute | solution.py:38

commit v8 on v7

--- a/solution.py
+++ b/solution.py
@@ -9,7 +9,7 @@
 TERMS = 6
 LANES = 128
 MIB = 1 << 20
-GROUP = 8
+GROUP = 16
 TILE = 256
 UNITS = 2
 HELD_ROWS = 1024
@@ -31,11 +31,10 @@
     return lax.all_to_all(blocks, "pair", split_axis=0, concat_axis=0, tiled=True)
 
 
-def both_sides(block):
-    count = lax.axis_size("pair")
+def partners(count):
     inner = [(i, i + 1 if i % 2 == 0 else i - 1) for i in range(count)]
     outer = [(i, (i - 1 if i % 2 == 0 else i + 1) % count) for i in range(count)]
-    return lax.ppermute(block, "pair", inner), lax.ppermute(block, "pair", outer)
+    return inner, outer
 
 
 def neighbours(block):
@@ -280,30 +279,37 @@
     return out.reshape(count, w_local * rows, orbitals)
 
 
-def propagate(blocks, one_body, inner, own, outer, src_shift, src_slot):
-    w_local, orbitals, _ = own.shape
+def choose_parents(inner, own, outer, src_shift, src_slot):
+    def body(inner_ref, own_ref, outer_ref, from_ref, slot_ref, out_ref):
+        side = 1 - 2 * lax.rem(lax.axis_index("pair"), 2)
+        for walker in range(own.shape[0]):
+            for offset, side_ref in ((-1, outer_ref), (0, own_ref), (1, inner_ref)):
+
+                @pl.when(from_ref[walker] * side == offset)
+                def _():
+                    out_ref[walker] = side_ref[slot_ref[walker]]
+
+    return pl.pallas_call(
+        body,
+        out_shape=jax.ShapeDtypeStruct(own.shape, jnp.bfloat16),
+        in_specs=[VMEM, VMEM, VMEM, SMEM, SMEM],
+        out_specs=VMEM,
+        compiler_params=params(4),
+        name="choose_parents",
+    )(inner, own, outer, src_shift, src_slot)
+
+
+def propagate(blocks, one_body, parents):
+    w_local, orbitals, _ = parents.shape
     count = blocks.shape[0]
     rows = orbitals // count
 
-    def body(blocks_ref, one_ref, inner_ref, own_ref, outer_ref, from_ref, slot_ref, out_ref, term_ref, mat_ref, sems):
-        def fetch(source, walker):
-            return pltpu.make_async_copy(source.at[slot_ref[walker]], term_ref.at[walker], sems.at[walker])
-
-        side = 1 - 2 * lax.rem(lax.axis_index("pair"), 2)
-        for walker in range(w_local):
-            for offset, side_ref in ((-1, outer_ref), (0, own_ref), (1, inner_ref)):
-
-                @pl.when(from_ref[walker] * side == offset)
-                def _():
-                    fetch(side_ref, walker).start()
-
+    def body(blocks_ref, one_ref, parents_ref, out_ref, mat_ref):
         one = one_ref[...].astype(jnp.float32).reshape(count, rows, orbitals)
         for walker in range(w_local):
             mine = blocks_ref[:, walker * rows : (walker + 1) * rows, :].astype(jnp.float32)
             mat_ref[walker] = (mine + one).reshape(orbitals, orbitals).astype(jnp.bfloat16)
-        for walker in range(w_local):
-            fetch(own_ref, walker).wait()
-        terms = [term_ref[walker] for walker in range(w_local)]
+        terms = [parents_ref[walker] for walker in range(w_local)]
         totals = [term.astype(jnp.float32) for term in terms]
         for order in range(1, TERMS):
             products = [
@@ -317,17 +323,13 @@
 
     return pl.pallas_call(
         body,
-        out_shape=jax.ShapeDtypeStruct(own.shape, jnp.bfloat16),
-        in_specs=[VMEM, VMEM, ANY, ANY, ANY, SMEM, SMEM],
+        out_shape=jax.ShapeDtypeStruct(parents.shape, jnp.bfloat16),
+        in_specs=[VMEM, VMEM, VMEM],
         out_specs=VMEM,
-        scratch_shapes=[
-            pltpu.VMEM(own.shape, jnp.bfloat16),
-            pltpu.VMEM((w_local, orbitals, orbitals), jnp.bfloat16),
-            pltpu.SemaphoreType.DMA((w_local,)),
-        ],
+        scratch_shapes=[pltpu.VMEM((w_local, orbitals, orbitals), jnp.bfloat16)],
         compiler_params=params(16),
         name="propagate",
-    )(blocks, one_body, inner, own, outer, src_shift, src_slot)
+    )(blocks, one_body, parents)
 
 
 def plain(chol, walkers, trial, one_body, fields, src_shift, src_slot):
@@ -368,14 +370,18 @@
     count = lax.axis_size("pair")
     w_local, orbitals, _ = walkers.shape
 
-    inner, outer = both_sides(walkers)
+    inner_pairs, outer_pairs = partners(count)
+    outer = lax.ppermute(walkers, "pair", outer_pairs)
+    inner = lax.ppermute(walkers, "pair", inner_pairs)
     sent = pack(walkers, count)
     moved = exchange(sent)
     partial = bias_partial(moved, trial, chol, w_local)
     partials = exchange(partial)
     blocks = exchange(shift_blocks(partials, fields, src_shift, src_slot))
-    received = exchange(potential(blocks, chol, w_local, orbitals))
-    return propagate(received, one_body, inner, walkers, outer, src_shift, src_slot)
+    sent = potential(blocks, chol, w_local, orbitals)
+    received = exchange(sent)
+    chosen = choose_parents(inner, walkers, outer, src_shift, src_slot)
+    return propagate(received, one_body, chosen)
 
 
 def shards(chol, walkers, *rest):

time: 89.7 us -> 89.8 us (level)
    pallas_call x1 -> x2, Pallas kernels: 3.84 us -> 3.15 us  [the longest x1 2.52 us: propagate(): pl.pallas_call(body, out_shape=jax.ShapeDtypeStruct(parents.shape, jnp.bf...]
  transfers between devices with their start and end apart: 3 -> 3, of which waited for: 2 -> 2; matrix products, arithmetic and copies ran while one was open for 0% -> 0% of each run, Pallas kernels for 0% -> 1%
where the time goes in v8:
time: 89.8 us; the launch traced here: 88 us
  blocking collectives  36.5 us (41%)
  waiting for transfers between devices  23.6 us (26%)
  Pallas kernels  20.4 us (23%)
  starting transfers between devices  6.34 us (7%)
  local copies, waits for them, and re-layouts  1.14 us (1%)
    all_to_all x3, blocking collectives, exchange(): lax.all_to_all(blocks, 'pair', split_axis=0, concat_axis=0, tiled=True)  36.5 us
    all_to_all x1, waiting for transfers between devices, exchange(): lax.all_to_all(blocks, 'pair', split_axis=0, concat_axis=0, tiled=True)  12.4 us
    ppermute x1, waiting for transfers between devices, held(): outer = lax.ppermute(walkers, 'pair', outer_pairs)  11.1 us
    pallas_call x1, Pallas kernels, potential(): pl.pallas_call(body, out_shape=jax.ShapeDtypeStruct((count, w_local, rows...  8.94 us
    pallas_call x1, Pallas kernels, bias_partial(): pl.pallas_call(body, out_shape=jax.ShapeDtypeStruct((count, w_local * str...  7.72 us
    all_to_all x1, starting transfers between devices, exchange(): lax.all_to_all(blocks, 'pair', split_axis=0, concat_axis=0, tiled=True)  4.52 us
    pallas_call x1, Pallas kernels, propagate(): pl.pallas_call(body, out_shape=jax.ShapeDtypeStruct(parents.shape, jnp.bf...  2.52 us
  transfers between devices with their start and end apart: 3, of which 2 were waited for; matrix products, arithmetic and copies ran while one was open for 0% of the time, Pallas kernels for 1%

profile of v8, /device:TPU:1, one launch (start us, length us, event | category | flops | bytes accessed | tf_op | source)
XLA Modules:
  0.0 88.0 jit_solution(12683148558477756300)
XLA Ops:
  0.0 0.0 copy-start
  0.0 0.0 copy-start.3
  0.0 1.1 %copy-done.3 = bf16[2,512,128]{2,1,0:T(8,128)(2,1)S(1)} copy-done((bf16[2,512,128]{2,1,0:T(8,128)(2,1)S(1)}, bf16[2,512,128]{2,1,0:T(8,128)(2,1)}, u32[]{:S(2)}) %copy-start.3) | copy-done | bytes 262168
  1.1 0.0 copy-start.5
  1.1 0.0 copy-start.6
  1.1 0.0 copy-start.7
  1.2 0.0 copy-start.8
  1.2 16.9 %all_to_all.20.moved_ref = bf16[16,64,128]{2,1,0:T(8,128)(2,1)S(1)} all-to-all(bf16[16,64,128]{2,1,0:T(8,128)(2,1)S(1)} %pack.1), channel_id=1, replica_groups=mesh['groups'=2,'pair'=16] {'pair'}, dimensions={0} | all-to-all | bytes 524288 | tf_op jit(solution)/shard_map/all_to_all | solution.py:31
  18.1 0.0 copy-done
  18.1 0.0 copy-done.5
  18.1 7.7 %bias_partial.1 = bf16[16,16,128]{2,1,0:T(8,128)(2,1)S(1)} custom-call(bf16[16,64,128]{2,1,0:T(8,128)(2,1)S(1)} %all_to_all.20.moved_ref, bf16[512,128]{1,0:T(8,128)(2,1)S(1)} %copy-done.5, bf16[1024,16384]{1,0:T(8,128)(2,1)S(1)} %copy-done), custom_call_target="tpu_custom_call" | custom-call | tf_op jit(solution)/shard_map/bias_partial/pallas_call | solution.py:162
  25.8 9.2 %all_to_all.21.partials_ref = bf16[16,16,128]{2,1,0:T(8,128)(2,1)S(1)} all-to-all(bf16[16,16,128]{2,1,0:T(8,128)(2,1)S(1)} %bias_partial.1), channel_id=1, replica_groups=mesh['groups'=2,'pair'=16] {'pair'}, dimensions={0} | all-to-all | bytes 131072 | tf_op jit(solution)/shard_map/all_to_all | solution.py:31
  35.0 0.0 copy-done.6
  35.0 0.0 copy-done.7
  35.0 0.0 copy-done.8
  35.0 0.0 copy-start.1
  35.0 0.6 shift_blocks.1
  35.6 0.0 copy-start.4
  35.6 0.0 copy-start.2
  35.7 10.4 %all_to_all.22.blocks_ref = bf16[16,24,128]{2,1,0:T(8,128)(2,1)S(1)} all-to-all(bf16[16,24,128]{2,1,0:T(8,128)(2,1)S(1)} %shift_blocks.1), channel_id=1, replica_groups=mesh['groups'=2,'pair'=16] {'pair'}, dimensions={0} | all-to-all | bytes 196608 | tf_op jit(solution)/shard_map/all_to_all | solution.py:31
  46.0 0.0 copy-done.1
  46.0 8.9 %potential.1 = bf16[16,2,32,512]{3,2,1,0:T(8,128)(2,1)} custom-call(bf16[16,24,128]{2,1,0:T(8,128)(2,1)S(1)} %all_to_all.22.blocks_ref, bf16[1024,16384]{1,0:T(8,128)(2,1)S(1)} %copy-done.1), custom_call_target="tpu_custom_call" | custom-call | tf_op jit(solution)/shard_map/potential/pallas_call | solution.py:264
  55.0 4.5 %all-to-all-start.3 = ((bf16[16,64,512]{2,1,0:T(8,128)(2,1)}), bf16[16,64,512]{2,1,0:T(8,128)(2,1)S(1)}, u32[]{:S(2)}, u32[]{:S(2)}) async-start(bf16[16,64,512]{2,1,0:T(8,128)(2,1)} %bitcast), calls=%async_computation.3 | async-start | bytes 2097152 | tf_op jit(solution)/shard_map/all_to_all | solution.py:31
  59.5 0.0 copy-done.4
  59.5 0.3 collective-permute-start
  59.8 1.5 %collective-permute-start.1 = (bf16[2,512,128]{2,1,0:T(8,128)(2,1)S(1)}, bf16[2,512,128]{2,1,0:T(8,128)(2,1)S(1)}, u32[]{:S(2)}, u32[]{:S(2)}) collective-permute-start(bf16[2,512,128]{2,1,0:T(8,128)(2,1)S(1)} %copy-done.4), channel_id=1, source_target_pairs={{0,15},{1,2},{2,1},{3,4},{4,3},{5,6},{6,5},{7,8},{8,7},{9,10},{10,... | collective-permute-start | bytes 786440 | tf_op jit(solution)/shard_map/ppermute | solution.py:374
  61.3 0.0 collective-permute-done.inner_ref
  61.3 11.1 %collective-permute-done.1.outer_ref = bf16[2,512,128]{2,1,0:T(8,128)(2,1)S(1)} collective-permute-done((bf16[2,512,128]{2,1,0:T(8,128)(2,1)S(1)}, bf16[2,512,128]{2,1,0:T(8,128)(2,1)S(1)}, u32[]{:S(2)}, u32[]{:S(2)}) %collective-permute-start.1) | collective-permute-done | bytes 262176 | tf_op jit(solution)/shard_map/ppermute | solution.py:374
  72.4 0.6 choose_parents.1.parents_ref
  73.1 12.4 %all-to-all-done.3.blocks_ref = bf16[16,64,512]{2,1,0:T(8,128)(2,1)S(1)} async-done(((bf16[16,64,512]{2,1,0:T(8,128)(2,1)}), bf16[16,64,512]{2,1,0:T(8,128)(2,1)S(1)}, u32[]{:S(2)}, u32[]{:S(2)}) %all-to-all-start.3) | async-done | bytes 1048608 | tf_op jit(solution)/shard_map/all_to_all | solution.py:31
  85.5 0.0 copy-done.2
  85.5 2.5 %propagate.1 = bf16[2,512,128]{2,1,0:T(8,128)(2,1)} custom-call(bf16[16,64,512]{2,1,0:T(8,128)(2,1)S(1)} %all-to-all-done.3.blocks_ref, bf16[512,512]{1,0:T(8,128)(2,1)S(1)} %copy-done.2, bf16[2,512,128]{2,1,0:T(8,128)(2,1)S(1)} %choose_parents.1.parents_ref), custom_call_target="tpu_custom_call" | custom-call | tf_op jit(solution)/shard_map/propagate/pallas_call | solution.py:324
  (1 shorter events, 0.0 us)
Async XLA Ops:
  0.0 18.1 %copy-start = (bf16[1024,16384]{1,0:T(8,128)(2,1)S(1)}, bf16[1024,16384]{1,0:T(8,128)(2,1)}, u32[]{:S(2)}) copy-start(bf16[1024,16384]{1,0:T(8,128)(2,1)} %chol_ref.3) | copy-start | bytes 100663296
  0.0 1.1 %copy-start.3 = (bf16[2,512,128]{2,1,0:T(8,128)(2,1)S(1)}, bf16[2,512,128]{2,1,0:T(8,128)(2,1)}, u32[]{:S(2)}) copy-start(bf16[2,512,128]{2,1,0:T(8,128)(2,1)} %own_ref.1) | copy-start | bytes 786436
  1.1 17.0 %copy-start.5 = (bf16[512,128]{1,0:T(8,128)(2,1)S(1)}, bf16[512,128]{1,0:T(8,128)(2,1)}, u32[]{:S(2)}) copy-start(bf16[512,128]{1,0:T(8,128)(2,1)} %trial_ref.1) | copy-start | bytes 393220
  1.1 33.9 %copy-start.6 = (s32[2]{0:T(128)S(1)}, s32[2]{0:T(128)}, u32[]{:S(2)}) copy-start(s32[2]{0:T(128)} %from_ref.3) | copy-start | bytes 28
  1.1 33.9 %copy-start.7 = (s32[2]{0:T(128)S(1)}, s32[2]{0:T(128)}, u32[]{:S(2)}) copy-start(s32[2]{0:T(128)} %slot_ref.3) | copy-start | bytes 28
  1.2 33.9 %copy-start.8 = (f32[2,1024]{1,0:T(2,128)S(1)}, f32[2,1024]{1,0:T(2,128)}, u32[]{:S(2)}) copy-start(f32[2,1024]{1,0:T(2,128)} %fields_ref.1) | copy-start | bytes 24580
  35.0 11.0 %copy-start.1 = (bf16[1024,16384]{1,0:T(8,128)(2,1)S(1)}, bf16[1024,16384]{1,0:T(8,128)(2,1)}, u32[]{:S(2)}) copy-start(bf16[1024,16384]{1,0:T(8,128)(2,1)} %chol_ref.3) | copy-start | bytes 100663296
  35.6 23.9 %copy-start.4 = (bf16[2,512,128]{2,1,0:T(8,128)(2,1)S(1)}, bf16[2,512,128]{2,1,0:T(8,128)(2,1)}, u32[]{:S(2)}) copy-start(bf16[2,512,128]{2,1,0:T(8,128)(2,1)} %own_ref.1) | copy-start | bytes 786436
  35.6 49.9 %copy-start.2 = (bf16[512,512]{1,0:T(8,128)(2,1)S(1)}, bf16[512,512]{1,0:T(8,128)(2,1)}, u32[]{:S(2)}) copy-start(bf16[512,512]{1,0:T(8,128)(2,1)} %one_ref.1) | copy-start | bytes 1572868
  55.0 30.6 %all-to-all-start.3 = ((bf16[16,64,512]{2,1,0:T(8,128)(2,1)}), bf16[16,64,512]{2,1,0:T(8,128)(2,1)S(1)}, u32[]{:S(2)}, u32[]{:S(2)}) async-start(bf16[16,64,512]{2,1,0:T(8,128)(2,1)} %bitcast), calls=%async_computation.3 | async-start | bytes 2097152 | tf_op jit(solution)/shard_map/all_to_all | solution.py:31
  59.5 1.8 %collective-permute-start = (bf16[2,512,128]{2,1,0:T(8,128)(2,1)S(1)}, bf16[2,512,128]{2,1,0:T(8,128)(2,1)S(1)}, u32[]{:S(2)}, u32[]{:S(2)}) collective-permute-start(bf16[2,512,128]{2,1,0:T(8,128)(2,1)S(1)} %copy-done.4), channel_id=1, source_target_pairs={{0,1},{1,0},{2,3},{3,2},{4,5},{5,4},{6,7},{7,6},{8,9},{9,8},{10,11... | collective-permute-start | bytes 786440 | tf_op jit(solution)/shard_map/ppermute | solution.py:375
  59.8 12.7 %collective-permute-start.1 = (bf16[2,512,128]{2,1,0:T(8,128)(2,1)S(1)}, bf16[2,512,128]{2,1,0:T(8,128)(2,1)S(1)}, u32[]{:S(2)}, u32[]{:S(2)}) collective-permute-start(bf16[2,512,128]{2,1,0:T(8,128)(2,1)S(1)} %copy-done.4), channel_id=1, source_target_pairs={{0,15},{1,2},{2,1},{3,4},{4,3},{5,6},{6,5},{7,8},{8,7},{9,10},{10,... | collective-permute-start | bytes 786440 | tf_op jit(solution)/shard_map/ppermute | solution.py:374

commit v9 on v8

--- a/solution.py
+++ b/solution.py
@@ -9,7 +9,7 @@
 TERMS = 6
 LANES = 128
 MIB = 1 << 20
-GROUP = 16
+GROUP = 8
 TILE = 256
 UNITS = 2
 HELD_ROWS = 1024
@@ -189,21 +189,21 @@
         lane = lax.broadcasted_iota(jnp.int32, (8, LANES), 1)
         table = jnp.zeros((8, LANES), jnp.int32)
         for walker in range(w_local):
-            table = jnp.where(lane == walker, from_ref[walker], table)
-            table = jnp.where(lane == w_local + walker, slot_ref[walker], table)
+            table = jnp.where(lane == walker, from_ref[:, walker : walker + 1], table)
+            table = jnp.where(lane == w_local + walker, slot_ref[:, walker : walker + 1], table)
         block = jnp.concatenate([shift, table.astype(jnp.float32)], axis=0).astype(jnp.bfloat16)
         out_ref[...] = jnp.broadcast_to(block[None], out_ref.shape)
 
     return pl.pallas_call(
         body,
         out_shape=jax.ShapeDtypeStruct((count, strips + 8, LANES), jnp.bfloat16),
-        in_specs=[VMEM, VMEM, SMEM, SMEM],
+        in_specs=[VMEM, VMEM, VMEM, VMEM],
         out_specs=VMEM,
         scratch_shapes=[pltpu.VMEM((strips, LANES), jnp.float32)],
         compiler_params=params(4),
         cost_estimate=COVER,
         name="shift_blocks",
-    )(partials, fields, src_shift, src_slot)
+    )(partials, fields, src_shift[None], src_slot[None])
 
 
 def parents_shift(blocks_ref, wide_ref, shift_ref, w_local, each):

time: 89.8 us -> 88.4 us (0.984)
  Pallas kernels: 20.4 us -> 19 us
where the time goes in v9:
time: 88.4 us; the launch traced here: 86.7 us
  blocking collectives  36.5 us (41%)
  waiting for transfers between devices  23.6 us (27%)
  Pallas kernels  19 us (21%)
  starting transfers between devices  6.27 us (7%)
  local copies, waits for them, and re-layouts  1.22 us (1%)
    all_to_all x3, blocking collectives, exchange(): lax.all_to_all(blocks, 'pair', split_axis=0, concat_axis=0, tiled=True)  36.5 us
    all_to_all x1, waiting for transfers between devices, exchange(): lax.all_to_all(blocks, 'pair', split_axis=0, concat_axis=0, tiled=True)  12.4 us
    ppermute x1, waiting for transfers between devices, held(): outer = lax.ppermute(walkers, 'pair', outer_pairs)  11.1 us
    pallas_call x1, Pallas kernels, potential(): pl.pallas_call(body, out_shape=jax.ShapeDtypeStruct((count, w_local, rows...  8.08 us
    pallas_call x1, Pallas kernels, bias_partial(): pl.pallas_call(body, out_shape=jax.ShapeDtypeStruct((count, w_local * str...  7.72 us
    all_to_all x1, starting transfers between devices, exchange(): lax.all_to_all(blocks, 'pair', split_axis=0, concat_axis=0, tiled=True)  4.44 us
    pallas_call x1, Pallas kernels, propagate(): pl.pallas_call(body, out_shape=jax.ShapeDtypeStruct(parents.shape, jnp.bf...  2.53 us
  transfers between devices with their start and end apart: 3, of which 2 were waited for; matrix products, arithmetic and copies ran while one was open for 0% of the time, Pallas kernels for 1%

profile of v9, /device:TPU:1, one launch (start us, length us, event | category | flops | bytes accessed | tf_op | source)
XLA Modules:
  0.0 86.7 jit_solution(7320949790872205864)
XLA Ops:
  0.0 0.0 copy-start
  0.0 0.0 copy-start.3
  0.0 1.1 %copy-done.3 = bf16[2,512,128]{2,1,0:T(8,128)(2,1)S(1)} copy-done((bf16[2,512,128]{2,1,0:T(8,128)(2,1)S(1)}, bf16[2,512,128]{2,1,0:T(8,128)(2,1)}, u32[]{:S(2)}) %copy-start.3) | copy-done | bytes 262168
  1.1 0.0 copy-start.5
  1.1 0.0 copy-start.6
  1.1 0.0 copy-start.7
  1.2 0.0 copy-start.8
  1.2 16.9 %all_to_all.20.moved_ref = bf16[16,64,128]{2,1,0:T(8,128)(2,1)S(1)} all-to-all(bf16[16,64,128]{2,1,0:T(8,128)(2,1)S(1)} %pack.1), channel_id=1, replica_groups=mesh['groups'=2,'pair'=16] {'pair'}, dimensions={0} | all-to-all | bytes 524288 | tf_op jit(solution)/shard_map/all_to_all | solution.py:31
  18.1 0.0 copy-done
  18.1 0.0 copy-done.5
  18.1 7.7 %bias_partial.1 = bf16[16,16,128]{2,1,0:T(8,128)(2,1)S(1)} custom-call(bf16[16,64,128]{2,1,0:T(8,128)(2,1)S(1)} %all_to_all.20.moved_ref, bf16[512,128]{1,0:T(8,128)(2,1)S(1)} %copy-done.5, bf16[1024,16384]{1,0:T(8,128)(2,1)S(1)} %copy-done), custom_call_target="tpu_custom_call" | custom-call | tf_op jit(solution)/shard_map/bias_partial/pallas_call | solution.py:162
  25.8 9.2 %all_to_all.21.partials_ref = bf16[16,16,128]{2,1,0:T(8,128)(2,1)S(1)} all-to-all(bf16[16,16,128]{2,1,0:T(8,128)(2,1)S(1)} %bias_partial.1), channel_id=1, replica_groups=mesh['groups'=2,'pair'=16] {'pair'}, dimensions={0} | all-to-all | bytes 131072 | tf_op jit(solution)/shard_map/all_to_all | solution.py:31
  35.0 0.0 copy-done.6
  35.0 0.0 copy-done.7
  35.0 0.0 copy-done.8
  35.0 0.0 copy-start.1
  35.0 0.1 shift_blocks.1
  35.1 0.0 copy-start.4
  35.1 0.0 copy-start.2
  35.1 10.4 %all_to_all.22.blocks_ref = bf16[16,24,128]{2,1,0:T(8,128)(2,1)S(1)} all-to-all(bf16[16,24,128]{2,1,0:T(8,128)(2,1)S(1)} %shift_blocks.1), channel_id=1, replica_groups=mesh['groups'=2,'pair'=16] {'pair'}, dimensions={0} | all-to-all | bytes 196608 | tf_op jit(solution)/shard_map/all_to_all | solution.py:31
  45.5 0.1 copy-done.1
  45.6 8.1 %potential.1 = bf16[16,2,32,512]{3,2,1,0:T(8,128)(2,1)} custom-call(bf16[16,24,128]{2,1,0:T(8,128)(2,1)S(1)} %all_to_all.22.blocks_ref, bf16[1024,16384]{1,0:T(8,128)(2,1)S(1)} %copy-done.1), custom_call_target="tpu_custom_call" | custom-call | tf_op jit(solution)/shard_map/potential/pallas_call | solution.py:264
  53.7 4.4 %all-to-all-start.3 = ((bf16[16,64,512]{2,1,0:T(8,128)(2,1)}), bf16[16,64,512]{2,1,0:T(8,128)(2,1)S(1)}, u32[]{:S(2)}, u32[]{:S(2)}) async-start(bf16[16,64,512]{2,1,0:T(8,128)(2,1)} %bitcast.2), calls=%async_computation.3 | async-start | bytes 2097152 | tf_op jit(solution)/shard_map/all_to_all | solution.py:31
  58.1 0.0 copy-done.4
  58.1 0.3 collective-permute-start
  58.4 1.5 %collective-permute-start.1 = (bf16[2,512,128]{2,1,0:T(8,128)(2,1)S(1)}, bf16[2,512,128]{2,1,0:T(8,128)(2,1)S(1)}, u32[]{:S(2)}, u32[]{:S(2)}) collective-permute-start(bf16[2,512,128]{2,1,0:T(8,128)(2,1)S(1)} %copy-done.4), channel_id=1, source_target_pairs={{0,15},{1,2},{2,1},{3,4},{4,3},{5,6},{6,5},{7,8},{8,7},{9,10},{10,... | collective-permute-start | bytes 786440 | tf_op jit(solution)/shard_map/ppermute | solution.py:374
  59.9 0.0 collective-permute-done.inner_ref
  59.9 11.1 %collective-permute-done.1.outer_ref = bf16[2,512,128]{2,1,0:T(8,128)(2,1)S(1)} collective-permute-done((bf16[2,512,128]{2,1,0:T(8,128)(2,1)S(1)}, bf16[2,512,128]{2,1,0:T(8,128)(2,1)S(1)}, u32[]{:S(2)}, u32[]{:S(2)}) %collective-permute-start.1) | collective-permute-done | bytes 262176 | tf_op jit(solution)/shard_map/ppermute | solution.py:374
  71.1 0.6 choose_parents.1.parents_ref
  71.7 12.4 %all-to-all-done.3.blocks_ref = bf16[16,64,512]{2,1,0:T(8,128)(2,1)S(1)} async-done(((bf16[16,64,512]{2,1,0:T(8,128)(2,1)}), bf16[16,64,512]{2,1,0:T(8,128)(2,1)S(1)}, u32[]{:S(2)}, u32[]{:S(2)}) %all-to-all-start.3) | async-done | bytes 1048608 | tf_op jit(solution)/shard_map/all_to_all | solution.py:31
  84.2 0.0 copy-done.2
  84.2 2.5 %propagate.1 = bf16[2,512,128]{2,1,0:T(8,128)(2,1)} custom-call(bf16[16,64,512]{2,1,0:T(8,128)(2,1)S(1)} %all-to-all-done.3.blocks_ref, bf16[512,512]{1,0:T(8,128)(2,1)S(1)} %copy-done.2, bf16[2,512,128]{2,1,0:T(8,128)(2,1)S(1)} %choose_parents.1.parents_ref), custom_call_target="tpu_custom_call" | custom-call | tf_op jit(solution)/shard_map/propagate/pallas_call | solution.py:324
  (1 shorter events, 0.0 us)
Async XLA Ops:
  0.0 18.1 %copy-start = (bf16[1024,16384]{1,0:T(8,128)(2,1)S(1)}, bf16[1024,16384]{1,0:T(8,128)(2,1)}, u32[]{:S(2)}) copy-start(bf16[1024,16384]{1,0:T(8,128)(2,1)} %chol_ref.3) | copy-start | bytes 100663296
  0.0 1.1 %copy-start.3 = (bf16[2,512,128]{2,1,0:T(8,128)(2,1)S(1)}, bf16[2,512,128]{2,1,0:T(8,128)(2,1)}, u32[]{:S(2)}) copy-start(bf16[2,512,128]{2,1,0:T(8,128)(2,1)} %own_ref.1) | copy-start | bytes 786436
  1.1 17.0 %copy-start.5 = (bf16[512,128]{1,0:T(8,128)(2,1)S(1)}, bf16[512,128]{1,0:T(8,128)(2,1)}, u32[]{:S(2)}) copy-start(bf16[512,128]{1,0:T(8,128)(2,1)} %trial_ref.1) | copy-start | bytes 393220
  1.1 33.9 %copy-start.6 = (s32[2]{0:T(128)S(1)}, s32[2]{0:T(128)}, u32[]{:S(2)}) copy-start(s32[2]{0:T(128)} %from_ref.1) | copy-start | bytes 28
  1.1 33.9 %copy-start.7 = (s32[2]{0:T(128)S(1)}, s32[2]{0:T(128)}, u32[]{:S(2)}) copy-start(s32[2]{0:T(128)} %slot_ref.1) | copy-start | bytes 28
  1.2 33.9 %copy-start.8 = (f32[2,1024]{1,0:T(2,128)S(1)}, f32[2,1024]{1,0:T(2,128)}, u32[]{:S(2)}) copy-start(f32[2,1024]{1,0:T(2,128)} %fields_ref.1) | copy-start | bytes 24580
  35.0 10.5 %copy-start.1 = (bf16[1024,16384]{1,0:T(8,128)(2,1)S(1)}, bf16[1024,16384]{1,0:T(8,128)(2,1)}, u32[]{:S(2)}) copy-start(bf16[1024,16384]{1,0:T(8,128)(2,1)} %chol_ref.3) | copy-start | bytes 100663296
  35.1 23.0 %copy-start.4 = (bf16[2,512,128]{2,1,0:T(8,128)(2,1)S(1)}, bf16[2,512,128]{2,1,0:T(8,128)(2,1)}, u32[]{:S(2)}) copy-start(bf16[2,512,128]{2,1,0:T(8,128)(2,1)} %own_ref.1) | copy-start | bytes 786436
  35.1 49.0 %copy-start.2 = (bf16[512,512]{1,0:T(8,128)(2,1)S(1)}, bf16[512,512]{1,0:T(8,128)(2,1)}, u32[]{:S(2)}) copy-start(bf16[512,512]{1,0:T(8,128)(2,1)} %one_ref.1) | copy-start | bytes 1572868
  53.7 30.5 %all-to-all-start.3 = ((bf16[16,64,512]{2,1,0:T(8,128)(2,1)}), bf16[16,64,512]{2,1,0:T(8,128)(2,1)S(1)}, u32[]{:S(2)}, u32[]{:S(2)}) async-start(bf16[16,64,512]{2,1,0:T(8,128)(2,1)} %bitcast.2), calls=%async_computation.3 | async-start | bytes 2097152 | tf_op jit(solution)/shard_map/all_to_all | solution.py:31
  58.1 1.8 %collective-permute-start = (bf16[2,512,128]{2,1,0:T(8,128)(2,1)S(1)}, bf16[2,512,128]{2,1,0:T(8,128)(2,1)S(1)}, u32[]{:S(2)}, u32[]{:S(2)}) collective-permute-start(bf16[2,512,128]{2,1,0:T(8,128)(2,1)S(1)} %copy-done.4), channel_id=1, source_target_pairs={{0,1},{1,0},{2,3},{3,2},{4,5},{5,4},{6,7},{7,6},{8,9},{9,8},{10,11... | collective-permute-start | bytes 786440 | tf_op jit(solution)/shard_map/ppermute | solution.py:375
  58.4 12.7 %collective-permute-start.1 = (bf16[2,512,128]{2,1,0:T(8,128)(2,1)S(1)}, bf16[2,512,128]{2,1,0:T(8,128)(2,1)S(1)}, u32[]{:S(2)}, u32[]{:S(2)}) collective-permute-start(bf16[2,512,128]{2,1,0:T(8,128)(2,1)S(1)} %copy-done.4), channel_id=1, source_target_pairs={{0,15},{1,2},{2,1},{3,4},{4,3},{5,6},{6,5},{7,8},{8,7},{9,10},{10,... | collective-permute-start | bytes 786440 | tf_op jit(solution)/shard_map/ppermute | solution.py:374
